TPU v7x, 32 devices: a whole 2x2x4 slice. The times are simulated.
32 devices in a mesh: groups: 1, dev: 8 (over z, y), side: 4 (over x, core).
Axes of the slice: x: 2, y: 2, z: 4, core: 2. Of those that a mesh axis runs over, the one named last changes fastest.
Arguments:
- queries: bfloat16 [256, 4096], P(('groups', 'dev', 'side')), may hold values from -160 to 160
- kv_cache: bfloat16 [256, 192, 1024], P(('groups', 'dev', 'side')), may hold values from -4 to 4
- new_kv: bfloat16 [256, 1024], P(('groups', 'dev', 'side')), may hold values from -4 to 4
- lengths: int32 [256], P(('groups', 'dev', 'side')), may hold values from 24 to 192, as said below
- residual: bfloat16 [256, 2048], P(('groups', 'dev', 'side')), may hold values from -36 to 36
- w_out: bfloat16 [4096, 2048], P('side'), may hold values from -0.59765625 to 0.59765625
- norm_gain: float32 [2048], replicated, may hold values from 0.5 to 1.5
- expert_ids: int32 [256, 8], P(('groups', 'dev', 'side')), may hold values from 0 to 15, all different within a row; in each aligned block of 8 rows (0 to 7, 8 to 15, ...) at most 8 rows name the same one
- route_level: int32 [256, 8], P(('groups', 'dev', 'side')), may hold values from 1 to 255
- w_in: bfloat16 [32, 2048, 768], P(('dev', 'side')), may hold values from -0.125 to 0.125
- w_down: bfloat16 [32, 384, 2048], P(('dev', 'side')), may hold values from -0.4375 to 0.4375
Outputs:
- stream: bfloat16 [256, 2048], P(('groups', 'dev', 'side'))
- expert_sum: bfloat16 [256, 2048], P(('groups', 'dev', 'side'))
Inputs may be any that keep to these rules, and one draw needn't show every extreme that they name: `lengths`: in each aligned block of 8 requests some request has 192 cached tokens. `expert_ids`: A row names 8 different experts. In each aligned block of 8 rows no expert is named by more than 8 rows, and in some block some expert is named by exactly 8 rows.
All inputs are finite; a program needn't handle non-finite values.
Results may differ from a plain program's by a relative error of at most 0.013.
Values may be sent and summed in bfloat16 or wider, within the bound.
No kernel may reach another device: no remote copies, remote signals or barrier semaphores. Data moves between devices by JAX's collectives and lax.ppermute only.
A program may use at most 64 MiB of HBM per device.

v0:
```python
import functools
import math

import jax
import jax.numpy as jnp
from jax import lax
from jax.experimental import pallas as pl
from jax.experimental.pallas import tpu as pltpu
from jax.sharding import PartitionSpec as P

HD = 128
GRANT = 16 << 20
VMEM = pl.BlockSpec(memory_space=pltpu.VMEM)
HBM = pl.BlockSpec(memory_space=pltpu.HBM)


def kernel_call(body, operands, outs, in_specs=None, scratch=(), cost=None):
    return pl.pallas_call(
        body,
        out_shape=outs,
        in_specs=in_specs or [VMEM] * len(operands),
        out_specs=jax.tree.map(lambda _: VMEM, outs, is_leaf=lambda x: hasattr(x, "shape")),
        scratch_shapes=list(scratch),
        compiler_params=pltpu.CompilerParams(vmem_limit_bytes=GRANT),
        cost_estimate=cost,
    )(*operands)


def in_hbm(*arrays):
    return [pltpu.with_memory_space_constraint(x, pltpu.HBM) for x in arrays]


def partner(block, axis, mask):
    count = lax.axis_size(axis)
    return lax.ppermute(block, axis, [(i, i ^ mask) for i in range(count)])


def start_all(copies):
    for copy in copies:
        copy.start()


def wait_all(copies):
    for copy in copies:
        copy.wait()


def half_copies(which, q_hbm, kv_hbm, new_hbm, q_ref, kv, new_ref, sems, kv_sems):
    rows, _, span = kv.shape
    share = span // 2
    whole = kv_hbm.shape[2] // 2
    keys = pl.ds(pl.multiple_of(which * share, share), share)
    values = pl.ds(pl.multiple_of(whole + which * share, share), share)
    span_q = q_ref.shape[1]
    small = [
        pltpu.make_async_copy(
            q_hbm.at[:, pl.ds(pl.multiple_of(which * span_q, span_q), span_q)],
            q_ref,
            sems.at[0],
        ),
        pltpu.make_async_copy(new_hbm.at[:, keys], new_ref.at[:, :share], sems.at[1]),
        pltpu.make_async_copy(new_hbm.at[:, values], new_ref.at[:, share:], sems.at[2]),
    ]
    large = [
        (
            pltpu.make_async_copy(kv_hbm.at[r, :, keys], kv.at[r, :, :share], kv_sems.at[0, r]),
            pltpu.make_async_copy(kv_hbm.at[r, :, values], kv.at[r, :, share:], kv_sems.at[1, r]),
        )
        for r in range(rows)
    ]
    return small, large


def attend_heads(q_ref, kv, new_ref, lengths, flat, mixed_flat, key_wait, value_wait, length_wait):
    rows, cache, span = kv.shape
    share = span // 2
    kv_heads = share // HD
    heads = q_ref.shape[1] // HD
    group = heads // kv_heads
    for h in range(heads):
        flat[h * rows : (h + 1) * rows, :] = q_ref[:, h * HD : (h + 1) * HD].astype(jnp.float32)
    scaling = 1.0 / math.sqrt(HD)
    asked = [flat[pl.ds(r, heads, stride=rows), :] for r in range(rows)]
    place = lax.broadcasted_iota(jnp.int32, (heads, cache), 1)
    fresh = new_ref[...].astype(jnp.float32)

    def spread(r, start):
        pieces = [
            jnp.broadcast_to(
                fresh[r : r + 1, start + g * HD : start + (g + 1) * HD], (group, HD)
            )
            for g in range(kv_heads)
        ]
        return jnp.concatenate(pieces, axis=0)

    all_scores = []
    for r in range(rows):
        q = asked[r].astype(jnp.bfloat16)
        key_wait(r)
        all_scores.append(
            jnp.concatenate(
                [
                    lax.dot_general(
                        q[g * group : (g + 1) * group],
                        kv[r, :, g * HD : (g + 1) * HD],
                        (((1,), (1,)), ((), ())),
                        preferred_element_type=jnp.float32,
                    )
                    for g in range(kv_heads)
                ],
                axis=0,
            )
        )
    length_wait()
    probs, own_probs = [], []
    for r in range(rows):
        own = jnp.sum(asked[r] * spread(r, 0), axis=1, keepdims=True) * scaling
        scores = jnp.where(place < lengths[r], all_scores[r] * scaling, -jnp.inf)
        peak = jnp.maximum(jnp.max(scores, axis=1, keepdims=True), own)
        weights = jnp.exp(scores - peak)
        own_weight = jnp.exp(own - peak)
        denominator = jnp.sum(weights, axis=1, keepdims=True) + own_weight
        scale = 1.0 / denominator
        probs.append((weights * scale).astype(jnp.bfloat16))
        own_probs.append((own_weight * scale).astype(jnp.bfloat16).astype(jnp.float32))
    for r in range(rows):
        value_wait(r)
        mixed = jnp.concatenate(
            [
                jnp.dot(
                    probs[r][g * group : (g + 1) * group],
                    kv[r, :, share + g * HD : share + (g + 1) * HD],
                    preferred_element_type=jnp.float32,
                )
                for g in range(kv_heads)
            ],
            axis=0,
        )
        mixed_flat[pl.ds(r, heads, stride=rows), :] = mixed + own_probs[r] * spread(r, share)


def put_pieces(out_ref, mixed_flat):
    pieces, rows, columns = out_ref.shape
    heads = columns // HD // 2
    mine = lax.axis_index("side")
    core = lax.rem(mine, 2)
    low = lax.rem(lax.div(mine, 2), pieces)
    for d in range(pieces):
        chip = jnp.bitwise_xor(low, d)
        for other in range(2):
            first = (2 * chip + jnp.bitwise_xor(core, other)) * heads
            for h in range(heads):
                at = pl.multiple_of((first + h) * rows, rows)
                to = (other * heads + h) * HD
                out_ref[d, :, to : to + HD] = mixed_flat[pl.ds(at, rows), :].astype(jnp.bfloat16)


def far_kernel(
    q_hbm, kv_hbm, new_hbm, length_hbm, out_ref, q_near, kv_near, new_near, q_ref, kv, new_ref,
    lengths, flat, mixed_flat, sems, kv_sems, near_sems, near_kv_sems, length_sem,
):
    here = lax.div(lax.axis_index("side"), lax.axis_size("side") // 2)
    length_copy = pltpu.make_async_copy(length_hbm, lengths, length_sem)
    small, large = half_copies(
        1 - here, q_hbm, kv_hbm, new_hbm, q_ref, kv, new_ref, sems, kv_sems
    )
    near_small, near_large = half_copies(
        here, q_hbm, kv_hbm, new_hbm, q_near, kv_near, new_near, near_sems, near_kv_sems
    )
    start_all(small)
    start_all([length_copy] + [pair[0] for pair in large])
    start_all([pair[1] for pair in large])
    start_all(near_small)
    for pair in near_large:
        start_all(pair)
    wait_all(small)
    attend_heads(
        q_ref, kv, new_ref, lengths, flat, mixed_flat,
        lambda r: large[r][0].wait(), lambda r: large[r][1].wait(), length_copy.wait,
    )
    put_pieces(out_ref, mixed_flat)
    wait_all(near_small)
    for pair in near_large:
        wait_all(pair)


def near_kernel(
    q_ref, kv, new_ref, length_hbm, w_hbm, out_ref, w_ref, lengths, flat, mixed_flat, length_sem,
    w_sem,
):
    length_copy = pltpu.make_async_copy(length_hbm, lengths, length_sem)
    w_copy = pltpu.make_async_copy(w_hbm, w_ref, w_sem)
    start_all([length_copy, w_copy])
    nothing = lambda r: None
    attend_heads(
        q_ref, kv, new_ref, lengths, flat, mixed_flat, nothing, nothing, length_copy.wait
    )
    put_pieces(out_ref, mixed_flat)
    w_copy.wait()


def attend(queries, kv_cache, new_kv, lengths, w_out):
    rows, features = queries.shape
    chips = lax.axis_size("side") // 2
    q_half = pltpu.VMEM((rows, features // 2), queries.dtype)
    kv_half = pltpu.VMEM((*kv_cache.shape[:2], kv_cache.shape[2] // 2), kv_cache.dtype)
    new_half = pltpu.VMEM((rows, new_kv.shape[1] // 2), new_kv.dtype)
    pieces = pltpu.VMEM((chips // 2, rows, features // chips), jnp.bfloat16)
    flat = pltpu.VMEM((rows * features // 2 // HD, HD), jnp.float32)
    smem = pltpu.SMEM(lengths.shape, lengths.dtype)
    dma = pltpu.SemaphoreType.DMA
    queries, kv_cache, new_kv, lengths, w_out = in_hbm(queries, kv_cache, new_kv, lengths, w_out)
    sent, q_near, kv_near, new_near = kernel_call(
        far_kernel,
        (queries, kv_cache, new_kv, lengths),
        (pieces, q_half, kv_half, new_half),
        in_specs=[HBM] * 4,
        scratch=[
            q_half, kv_half, new_half, smem, flat, flat,
            dma((3,)), dma((2, rows)), dma((3,)), dma((2, rows)), dma,
        ],
    )
    received = partner(sent, "side", chips)
    kept, w_near = kernel_call(
        near_kernel,
        (q_near, kv_near, new_near, lengths, w_out),
        (pieces, pltpu.VMEM(w_out.shape, w_out.dtype)),
        in_specs=[VMEM] * 3 + [HBM] * 2,
        scratch=[smem, flat, flat, dma, dma],
        cost=pl.CostEstimate(flops=8 << 20, bytes_accessed=8 << 20, transcendentals=0),
    )
    blocks = {0: kept, chips // 2: received}
    bit = chips // 4
    while bit:
        blocks.update({d ^ bit: partner(block, "side", 2 * bit) for d, block in blocks.items()})
        bit //= 2
    return [blocks[d] for d in range(chips)], w_near


def project_kernel(*refs):
    kept_ref, sent_ref = refs[-2:]
    w_near, w_other, residual_ref, ids_ref, level_ref = refs[-7:-2]
    blocks = refs[:-7]
    rows, width = residual_ref.shape
    depth = w_near.shape[0]
    experts = lax.axis_size("dev") * lax.axis_size("side") // 2
    lhs = jnp.concatenate([ref[d % ref.shape[0]] for d, ref in enumerate(blocks)], axis=0)
    product = jnp.dot(lhs[:, :depth], w_near[...], preferred_element_type=jnp.float32) + jnp.dot(
        lhs[:, depth:], w_other[...], preferred_element_type=jnp.float32
    )
    level = level_ref[...].astype(jnp.float32)
    share = level / jnp.sum(level, axis=1, keepdims=True)
    spare = kept_ref.shape[1] - width
    lane = lax.broadcasted_iota(jnp.int32, (rows, spare), 1)
    ids = ids_ref[...]
    high, low = jnp.zeros((2, rows, spare), jnp.float32)
    for k in range(ids.shape[1]):
        chosen, part = ids[:, k : k + 1], share[:, k : k + 1]
        top = part.astype(jnp.bfloat16).astype(jnp.float32)
        high = high + jnp.where(lane == chosen, top, 0.0)
        low = low + jnp.where(lane == chosen + experts, part - top, 0.0)
    count = len(blocks)
    for d in range(count):
        here = product[d * rows : (d + 1) * rows]
        aside = jnp.zeros((rows, spare), jnp.float32)
        if d == 0:
            here = here + residual_ref[...].astype(jnp.float32)
            aside = high + low
        at = slice(d * rows, (d + 1) * rows)
        kept_ref[at, :width] = here
        kept_ref[at, width:] = aside
        at = slice((d ^ 1) * rows, ((d ^ 1) + 1) * rows)
        sent_ref[at, :width] = here.astype(jnp.bfloat16)
        sent_ref[at, width:] = aside.astype(jnp.bfloat16)


def project(blocks, w_near, w_other, residual, expert_ids, route_level):
    rows, width = residual.shape
    chips = len(blocks)
    experts = lax.axis_size("dev") * chips
    shape = (chips * rows, width + pl.cdiv(2 * experts, 128) * 128)
    kept, sent = kernel_call(
        project_kernel,
        (
            *blocks,
            w_near,
            pltpu.with_memory_space_constraint(w_other, pltpu.VMEM),
            residual,
            expert_ids,
            route_level,
        ),
        (jax.ShapeDtypeStruct(shape, jnp.float32), jax.ShapeDtypeStruct(shape, jnp.bfloat16)),
    )
    bit = 1
    more = partner(sent, "side", 2 * bit)
    while 2 * bit < chips:
        kept = kept + more.astype(jnp.float32)
        bit *= 2
        swapped = [kept[(d ^ bit) * rows : ((d ^ bit) + 1) * rows] for d in range(chips)]
        more = partner(jnp.concatenate(swapped).astype(jnp.bfloat16), "side", 2 * bit)
    return kept, sent, more


def fetch_kernel(after_ref, in_hbm_ref, down_hbm_ref, in_ref, down_ref, sems):
    copies = [
        pltpu.make_async_copy(in_hbm_ref.at[0], in_ref, sems.at[0]),
        pltpu.make_async_copy(down_hbm_ref.at[0], down_ref, sems.at[1]),
    ]
    start_all(copies)
    wait_all(copies)


def fetch(after, w_in, w_down):
    return kernel_call(
        fetch_kernel,
        (after, *in_hbm(w_in, w_down)),
        (pltpu.VMEM(w_in.shape[1:], w_in.dtype), pltpu.VMEM(w_down.shape[1:], w_down.dtype)),
        in_specs=[VMEM, HBM, HBM],
        scratch=[pltpu.SemaphoreType.DMA((2,))],
        cost=pl.CostEstimate(flops=0, bytes_accessed=8 << 20, transcendentals=0),
    )


def norm_kernel(total_ref, more_ref, gain_ref, normed_ref, stream_ref):
    rows, width = stream_ref.shape
    stream = total_ref[:, :width] + more_ref[:, :width].astype(jnp.float32)
    mean_square = jnp.mean(stream * stream, axis=1, keepdims=True)
    normed = stream * lax.rsqrt(mean_square + 1e-06) * gain_ref[...]
    normed_ref[:, :width] = normed.astype(jnp.bfloat16)
    aside = total_ref[:, width:] + more_ref[:, width:].astype(jnp.float32)
    normed_ref[:, width:] = aside.astype(jnp.bfloat16)
    stream_ref[...] = stream[:rows].astype(jnp.bfloat16)


def expert_kernel(rows, *refs):
    kept_ref, sent_ref = refs[-2:]
    in_own, in_other, down_own, down_other = refs[-6:-2]
    blocks = refs[:-6]
    width = kept_ref.shape[1]
    units = down_own.shape[0]
    chips = lax.axis_size("side") // 2
    experts = lax.axis_size("dev") * chips
    mine = lax.axis_index("dev") * chips + lax.div(lax.axis_index("side"), 2)
    tokens = jnp.concatenate([ref[:, :width] for ref in blocks], axis=0)
    aside = jnp.concatenate([ref[:, width:] for ref in blocks], axis=0).astype(jnp.float32)
    lane = lax.broadcasted_iota(jnp.int32, aside.shape, 1)
    picked = jnp.where((lane == mine) | (lane == mine + experts), aside, 0.0)
    share = jnp.sum(picked, axis=1, keepdims=True)
    hidden = []
    for w_ref in (in_own, in_other):
        gate_up = jnp.dot(tokens, w_ref[...], preferred_element_type=jnp.float32)
        gate = gate_up[:, :units]
        hidden.append((gate / (1.0 + jnp.exp(-gate)) * gate_up[:, units:]).astype(jnp.bfloat16))
    result = jnp.dot(hidden[0], down_own[...], preferred_element_type=jnp.float32) + jnp.dot(
        hidden[1], down_other[...], preferred_element_type=jnp.float32
    )
    result = result * share
    count = tokens.shape[0] // (chips * rows)
    for d in range(chips):
        for i in range(count):
            start = (i * chips + d) * rows
            piece = result[start : start + rows]
            to = ((d % (chips // 2)) * count + i) * rows
            if d < chips // 2:
                kept_ref[to : to + rows, :] = piece
            else:
                sent_ref[to : to + rows, :] = piece.astype(jnp.bfloat16)


def run_experts(blocks, weights, rows, width):
    shape = (sum(block.shape[0] for block in blocks) // 2, width)
    return kernel_call(
        functools.partial(expert_kernel, rows),
        (*blocks, *weights),
        (jax.ShapeDtypeStruct(shape, jnp.float32), jax.ShapeDtypeStruct(shape, jnp.bfloat16)),
        cost=pl.CostEstimate(flops=1 << 30, bytes_accessed=4 << 20, transcendentals=0),
    )


def merge_kernel(kept_ref, more_ref, *out_refs):
    total = kept_ref[...] + more_ref[...].astype(jnp.float32)
    start = 0
    for ref in out_refs:
        ref[...] = total[start : start + ref.shape[0]].astype(ref.dtype)
        start += ref.shape[0]


def merge(kept, more, pieces):
    outs = tuple(jax.ShapeDtypeStruct((rows, kept.shape[1]), dtype) for rows, dtype in pieces)
    return kernel_call(merge_kernel, (kept, more), outs)


def homeward(kept, sent, aways, rows):
    bit = lax.axis_size("side") // 4
    while bit:
        more = partner(sent, "side", 2 * bit)
        half = kept.shape[0] // 2
        pieces = ((half, jnp.float32), (half, jnp.bfloat16))
        kept, sent = merge(kept, more, pieces)
        bit //= 2
    more = partner(sent, "dev", 1)
    pieces = tuple((rows, jnp.bfloat16 if away else jnp.float32) for away in aways)
    return merge(kept, more, pieces)


def dev_groups(devs):
    upper = list(range(0, devs, 2))
    return upper[: len(upper) // 2], upper[len(upper) // 2 :]


def body(
    queries,
    kv_cache,
    new_kv,
    lengths,
    residual,
    w_out,
    norm_gain,
    expert_ids,
    route_level,
    w_in,
    w_down,
):
    rows, width = residual.shape
    devs = lax.axis_size("dev")

    w_other = partner(w_out, "side", 1)
    blocks, w_near = attend(queries, kv_cache, new_kv, lengths, w_out)
    total, sent, more = project(blocks, w_near, w_other, residual, expert_ids, route_level)
    w_in, w_down = fetch(sent, w_in, w_down)
    w_in, w_down, more = lax.optimization_barrier((w_in, w_down, more))
    weights = (w_in, partner(w_in, "side", 1), w_down, partner(w_down, "side", 1))
    normed, stream = kernel_call(
        norm_kernel,
        (total, more, norm_gain.reshape(1, width)),
        (
            jax.ShapeDtypeStruct(total.shape, jnp.bfloat16),
            jax.ShapeDtypeStruct((rows, width), jnp.bfloat16),
        ),
    )

    early, late = dev_groups(devs)
    near = {0: normed}
    for away in late + early[1:]:
        near[away] = partner(normed, "dev", away)
    near_early = [near[away] for away in early]
    far_early = [partner(jnp.concatenate(near_early), "dev", 1)]
    near_late = [near[away] for away in late]
    far_late = [partner(near[away], "dev", 1) for away in late]
    home = []
    for aways, blocks in ((early, near_early + far_early), (late, near_late + far_late)):
        kept, sent = run_experts(blocks, weights, rows, width)
        for away, block in zip(aways, homeward(kept, sent, aways, rows)):
            if away:
                block = partner(block, "dev", away).astype(jnp.float32)
            home.append(block)
    expert_sum = functools.reduce(jnp.add, home)
    return (stream, expert_sum.astype(jnp.bfloat16))


def solution(mesh):
    by_request = ("groups", "dev", "side")
    return jax.shard_map(
        body,
        mesh=mesh,
        in_specs=(
            P(by_request, None),
            P(by_request, None, None),
            P(by_request, None),
            P(by_request),
            P(by_request, None),
            P("side", None),
            P(),
            P(by_request, None),
            P(by_request, None),
            P(("dev", "side"), None, None),
            P(("dev", "side"), None, None),
        ),
        out_specs=(P(by_request, None), P(by_request, None)),
        check_vma=False,
    )
```

profile of v0, /device:TPU:0, one launch (start us, length us, event | category | flops | bytes accessed | tf_op | source)
XLA Modules:
  0.0 53.8 jit_solution(7761835191963800751)
XLA Ops:
  0.6 0.6 %collective-permute-start.1 = (bf16[1024,2048]{1,0:T(8,128)(2,1)}, bf16[1024,2048]{1,0:T(8,128)(2,1)S(1)}, u32[]{:S(2)}, u32[]{:S(2)}) collective-permute-start(bf16[1024,2048]{1,0:T(8,128)(2,1)} %w_hbm.1), channel_id=1, source_target_pairs={{0,1},{1,0},{2,3},{3,2},{4,5},{5,4},{6,7},{7,6},{8,9},{9,8},{10,11... | collective-permute-start | bytes 12582920 | tf_op jit(solution)/shard_map/ppermute | solution.py:35
  1.2 4.8 %shard_map.122 = (bf16[1,8,2048]{2,1,0:T(8,128)(2,1)S(1)}, bf16[8,2048]{1,0:T(8,128)(2,1)S(1)}, bf16[8,192,512]{2,1,0:T(8,128)(2,1)S(1)}, bf16[8,512]{1,0:T(8,128)(2,1)S(1)}) custom-call(bf16[8,4096]{1,0:T(8,128)(2,1)} %q_hbm.1, bf16[8,192,1024]{2,1,0:T(8,128)(2,1)} %kv_hbm.1, bf16[8,1024]{1,0:T(8,128)(2,1)} %new_hbm.1, s32[8]{0:T(128)} %length_hbm.3), custom_call_target="tpu_custom_call" | custom-call | tf_op jit(solution)/shard_map/pallas_call | solution.py:18
  6.0 0.0 copy-start
  6.0 0.0 copy-start.2
  6.1 0.0 copy-start.3
  6.1 2.6 %collective-permute-start = (bf16[1,8,2048]{2,1,0:T(8,128)(2,1)S(1)}, bf16[1,8,2048]{2,1,0:T(8,128)(2,1)S(1)}, u32[]{:S(2)}, u32[]{:S(2)}) collective-permute-start(bf16[1,8,2048]{2,1,0:T(8,128)(2,1)S(1)} %get-tuple-element.33), channel_id=1, source_target_pairs={{0,2},{1,3},{2,0},{3,1},{4,6},{5,7},{6,4},{7,5},{8,10},{9,11},{10,... | collective-permute-start | bytes 98312 | tf_op jit(solution)/shard_map/ppermute | solution.py:35
  8.6 2.2 %shard_map.123 = (bf16[1,8,2048]{2,1,0:T(8,128)(2,1)S(1)}, bf16[1024,2048]{1,0:T(8,128)(2,1)S(1)}) custom-call(bf16[8,2048]{1,0:T(8,128)(2,1)S(1)} %get-tuple-element.29.q_ref, bf16[8,192,512]{2,1,0:T(8,128)(2,1)S(1)} %get-tuple-element.30.kv, bf16[8,512]{1,0:T(8,128)(2,1)S(1)} %get-tuple-element.31.new_ref, s32[8]{0:T(128)} %length_hbm.3, ...), custom_call_target="tpu_custom_call" | custom-call | flops 8388608 | bytes 8388608 | tf_op jit(solution)/shard_map/pallas_call | solution.py:18
  10.9 0.0 collective-permute-done.refs_1_
  10.9 0.0 collective-permute-done.1.refs_3_
  10.9 0.0 copy-done
  10.9 0.0 copy-done.2
  10.9 0.0 copy-done.3
  10.9 1.2 %shard_map.124 = (f32[16,2176]{1,0:T(8,128)S(1)}, bf16[16,2176]{1,0:T(8,128)(2,1)S(1)}) custom-call(bf16[1,8,2048]{2,1,0:T(8,128)(2,1)S(1)} %get-tuple-element.32.refs_0_, bf16[1,8,2048]{2,1,0:T(8,128)(2,1)S(1)} %collective-permute-done.refs_1_, bf16[1024,2048]{1,0:T(8,128)(2,1)S(1)} %get-tuple-element.34.refs_2_, ...), custom_call_target="tpu_custom_call" | custom-call | tf_op jit(solution)/shard_map/pallas_call | solution.py:18
  12.1 0.0 copy-start.1
  12.1 1.7 %collective-permute-start.2 = (bf16[16,2176]{1,0:T(8,128)(2,1)S(1)}, bf16[16,2176]{1,0:T(8,128)(2,1)S(1)}, u32[]{:S(2)}, u32[]{:S(2)}) collective-permute-start(bf16[16,2176]{1,0:T(8,128)(2,1)S(1)} %get-tuple-element.36.after_ref), channel_id=1, source_target_pairs={{0,2},{1,3},{2,0},{3,1},{4,6},{5,7},{6,4},{7,5},{8,10},{9,11},{10,... | collective-permute-start | bytes 208904 | tf_op jit(solution)/shard_map/ppermute | solution.py:35
  13.8 2.4 %shard_map.125 = (bf16[2048,768]{1,0:T(8,128)(2,1)S(1)}, bf16[384,2048]{1,0:T(8,128)(2,1)S(1)}) custom-call(bf16[16,2176]{1,0:T(8,128)(2,1)S(1)} %get-tuple-element.36.after_ref, bf16[1,2048,768]{2,1,0:T(8,128)(2,1)} %in_hbm_ref.1, bf16[1,384,2048]{2,1,0:T(8,128)(2,1)} %down_hbm_ref.1), custom_call_target="tpu_custom_call" | custom-call | bytes 8388608 | tf_op jit(solution)/shard_map/pallas_call | solution.py:18
  16.2 0.3 collective-permute-done.2.more_ref
  16.4 0.0 collective-permute-start.5
  16.4 0.5 collective-permute-start.6
  16.9 0.0 copy-done.1
  16.9 0.6 %shard_map.126 = (bf16[16,2176]{1,0:T(8,128)(2,1)S(1)}, bf16[8,2048]{1,0:T(8,128)(2,1)}) custom-call(f32[16,2176]{1,0:T(8,128)S(1)} %get-tuple-element.35.total_ref, bf16[16,2176]{1,0:T(8,128)(2,1)S(1)} %collective-permute-done.2.more_ref, f32[1,2048]{1,0:T(1,128)S(1)} %bitcast.1), custom_call_target="tpu_custom_call" | custom-call | tf_op jit(solution)/shard_map/pallas_call | solution.py:18
  17.6 2.8 %collective-permute-start.10 = (bf16[16,2176]{1,0:T(8,128)(2,1)S(1)}, bf16[16,2176]{1,0:T(8,128)(2,1)S(1)}, u32[]{:S(2)}, u32[]{:S(2)}) collective-permute-start(bf16[16,2176]{1,0:T(8,128)(2,1)S(1)} %get-tuple-element.41.refs_0_), channel_id=1, source_target_pairs={{0,16},{4,20},{8,24},{12,28},{16,0},{20,4},{24,8},{28,12},{1,17},{... | collective-permute-start | bytes 208904 | tf_op jit(solution)/shard_map/ppermute | solution.py:35
  20.4 1.3 %collective-permute-start.11 = (bf16[16,2176]{1,0:T(8,128)(2,1)S(1)}, bf16[16,2176]{1,0:T(8,128)(2,1)S(1)}, u32[]{:S(2)}, u32[]{:S(2)}) collective-permute-start(bf16[16,2176]{1,0:T(8,128)(2,1)S(1)} %get-tuple-element.41.refs_0_), channel_id=1, source_target_pairs={{0,24},{4,28},{8,16},{12,20},{16,8},{20,12},{24,0},{28,4},{1,25},{... | collective-permute-start | bytes 208904 | tf_op jit(solution)/shard_map/ppermute | solution.py:35
  21.7 0.2 collective-permute-start.3
  21.9 3.4 %collective-permute-done.10.refs_0_ = bf16[16,2176]{1,0:T(8,128)(2,1)S(1)} collective-permute-done((bf16[16,2176]{1,0:T(8,128)(2,1)S(1)}, bf16[16,2176]{1,0:T(8,128)(2,1)S(1)}, u32[]{:S(2)}, u32[]{:S(2)}) %collective-permute-start.10) | collective-permute-done | bytes 69664 | tf_op jit(solution)/shard_map/ppermute | solution.py:35
  25.4 1.8 %collective-permute-start.12 = (bf16[16,2176]{1,0:T(8,128)(2,1)S(1)}, bf16[16,2176]{1,0:T(8,128)(2,1)S(1)}, u32[]{:S(2)}, u32[]{:S(2)}) collective-permute-start(bf16[16,2176]{1,0:T(8,128)(2,1)S(1)} %collective-permute-done.10.refs_0_), channel_id=1, source_target_pairs={{0,4},{4,0},{8,12},{12,8},{16,20},{20,16},{24,28},{28,24},{1,5},{5... | collective-permute-start | bytes 208904 | tf_op jit(solution)/shard_map/ppermute | solution.py:35
  27.2 0.0 collective-permute-done.11.refs_1_
  27.2 1.0 %collective-permute-start.13 = (bf16[16,2176]{1,0:T(8,128)(2,1)S(1)}, bf16[16,2176]{1,0:T(8,128)(2,1)S(1)}, u32[]{:S(2)}, u32[]{:S(2)}) collective-permute-start(bf16[16,2176]{1,0:T(8,128)(2,1)S(1)} %collective-permute-done.11.refs_1_), channel_id=1, source_target_pairs={{0,4},{4,0},{8,12},{12,8},{16,20},{20,16},{24,28},{28,24},{1,5},{5... | collective-permute-start | bytes 208904 | tf_op jit(solution)/shard_map/ppermute | solution.py:35
  28.2 0.0 collective-permute-done.3.refs_1_
  28.3 1.1 %collective-permute-start.4 = (bf16[32,2176]{1,0:T(8,128)(2,1)S(1)}, bf16[32,2176]{1,0:T(8,128)(2,1)S(1)}, u32[]{:S(2)}, u32[]{:S(2)}) collective-permute-start(bf16[32,2176]{1,0:T(8,128)(2,1)S(1)} %pad_maximum_fusion), channel_id=1, source_target_pairs={{0,4},{4,0},{8,12},{12,8},{16,20},{20,16},{24,28},{28,24},{1,5},{5... | collective-permute-start | bytes 417800 | tf_op jit(solution)/shard_map/ppermute | solution.py:35
  29.3 0.9 %collective-permute-done.12.refs_2_ = bf16[16,2176]{1,0:T(8,128)(2,1)S(1)} collective-permute-done((bf16[16,2176]{1,0:T(8,128)(2,1)S(1)}, bf16[16,2176]{1,0:T(8,128)(2,1)S(1)}, u32[]{:S(2)}, u32[]{:S(2)}) %collective-permute-start.12) | collective-permute-done | bytes 69664 | tf_op jit(solution)/shard_map/ppermute | solution.py:35
  30.3 1.7 %collective-permute-done.13.refs_3_ = bf16[16,2176]{1,0:T(8,128)(2,1)S(1)} collective-permute-done((bf16[16,2176]{1,0:T(8,128)(2,1)S(1)}, bf16[16,2176]{1,0:T(8,128)(2,1)S(1)}, u32[]{:S(2)}, u32[]{:S(2)}) %collective-permute-start.13) | collective-permute-done | bytes 69664 | tf_op jit(solution)/shard_map/ppermute | solution.py:35
  31.9 0.0 collective-permute-done.6.refs_6_.refs_7_
  31.9 0.0 collective-permute-done.5.refs_4_.refs_5_
  31.9 1.9 %shard_map.130 = (f32[32,2048]{1,0:T(8,128)S(1)}, bf16[32,2048]{1,0:T(8,128)(2,1)S(1)}) custom-call(bf16[16,2176]{1,0:T(8,128)(2,1)S(1)} %collective-permute-done.10.refs_0_, bf16[16,2176]{1,0:T(8,128)(2,1)S(1)} %collective-permute-done.11.refs_1_, bf16[16,2176]{1,0:T(8,128)(2,1)S(1)} %collective-permute-done.12.refs_2_, ...), custom_call_target="tpu_custom_call" | custom-call | flops 1073741824 | bytes 4194304 | tf_op jit(solution)/shard_map/pallas_call | solution.py:18
  33.8 1.7 %collective-permute-start.14 = (bf16[32,2048]{1,0:T(8,128)(2,1)S(1)}, bf16[32,2048]{1,0:T(8,128)(2,1)S(1)}, u32[]{:S(2)}, u32[]{:S(2)}) collective-permute-start(bf16[32,2048]{1,0:T(8,128)(2,1)S(1)} %get-tuple-element.51), channel_id=1, source_target_pairs={{0,2},{1,3},{2,0},{3,1},{4,6},{5,7},{6,4},{7,5},{8,10},{9,11},{10,... | collective-permute-start | bytes 393224 | tf_op jit(solution)/shard_map/ppermute | solution.py:35
  35.5 0.0 collective-permute-done.4.refs_2_
  35.5 1.8 %shard_map.127 = (f32[32,2048]{1,0:T(8,128)S(1)}, bf16[32,2048]{1,0:T(8,128)(2,1)S(1)}) custom-call(bf16[16,2176]{1,0:T(8,128)(2,1)S(1)} %get-tuple-element.41.refs_0_, bf16[16,2176]{1,0:T(8,128)(2,1)S(1)} %collective-permute-done.3.refs_1_, bf16[32,2176]{1,0:T(8,128)(2,1)S(1)} %collective-permute-done.4.refs_2_, ...), custom_call_target="tpu_custom_call" | custom-call | flops 1073741824 | bytes 4194304 | tf_op jit(solution)/shard_map/pallas_call | solution.py:18
  37.4 0.4 collective-permute-start.7
  37.8 1.3 %collective-permute-done.14.more_ref = bf16[32,2048]{1,0:T(8,128)(2,1)S(1)} collective-permute-done((bf16[32,2048]{1,0:T(8,128)(2,1)S(1)}, bf16[32,2048]{1,0:T(8,128)(2,1)S(1)}, u32[]{:S(2)}, u32[]{:S(2)}) %collective-permute-start.14) | collective-permute-done | bytes 131104 | tf_op jit(solution)/shard_map/ppermute | solution.py:35
  39.1 1.3 %collective-permute-start.15 = (bf16[16,2048]{1,0:T(8,128)(2,1)S(1)}, bf16[16,2048]{1,0:T(8,128)(2,1)S(1)}, u32[]{:S(2)}, u32[]{:S(2)}) collective-permute-start(bf16[16,2048]{1,0:T(8,128)(2,1)S(1)} %get-tuple-element.53), channel_id=1, source_target_pairs={{0,4},{4,0},{8,12},{12,8},{16,20},{20,16},{24,28},{28,24},{1,5},{5... | collective-permute-start | bytes 196616 | tf_op jit(solution)/shard_map/ppermute | solution.py:35
  40.4 2.0 %collective-permute-done.7.more_ref = bf16[32,2048]{1,0:T(8,128)(2,1)S(1)} collective-permute-done((bf16[32,2048]{1,0:T(8,128)(2,1)S(1)}, bf16[32,2048]{1,0:T(8,128)(2,1)S(1)}, u32[]{:S(2)}, u32[]{:S(2)}) %collective-permute-start.7) | collective-permute-done | bytes 131104 | tf_op jit(solution)/shard_map/ppermute | solution.py:35
  42.4 1.3 %collective-permute-start.8 = (bf16[16,2048]{1,0:T(8,128)(2,1)S(1)}, bf16[16,2048]{1,0:T(8,128)(2,1)S(1)}, u32[]{:S(2)}, u32[]{:S(2)}) collective-permute-start(bf16[16,2048]{1,0:T(8,128)(2,1)S(1)} %get-tuple-element.47), channel_id=1, source_target_pairs={{0,4},{4,0},{8,12},{12,8},{16,20},{20,16},{24,28},{28,24},{1,5},{5... | collective-permute-start | bytes 196616 | tf_op jit(solution)/shard_map/ppermute | solution.py:35
  43.7 0.0 collective-permute-done.15.more_ref
  43.7 4.6 %collective-permute-start.17 = (bf16[8,2048]{1,0:T(8,128)(2,1)S(1)}, bf16[8,2048]{1,0:T(8,128)(2,1)S(1)}, u32[]{:S(2)}, u32[]{:S(2)}) collective-permute-start(bf16[8,2048]{1,0:T(8,128)(2,1)S(1)} %get-tuple-element.55), channel_id=1, source_target_pairs={{0,24},{4,28},{8,16},{12,20},{16,8},{20,12},{24,0},{28,4},{1,25},{... | collective-permute-start | bytes 98312 | tf_op jit(solution)/shard_map/ppermute | solution.py:35
  48.4 0.0 collective-permute-start.16
  48.4 0.0 collective-permute-done.8.more_ref
  48.4 0.7 %collective-permute-start.9 = (bf16[8,2048]{1,0:T(8,128)(2,1)S(1)}, bf16[8,2048]{1,0:T(8,128)(2,1)S(1)}, u32[]{:S(2)}, u32[]{:S(2)}) collective-permute-start(bf16[8,2048]{1,0:T(8,128)(2,1)S(1)} %get-tuple-element.49), channel_id=1, source_target_pairs={{0,8},{4,12},{8,0},{12,4},{16,24},{20,28},{24,16},{28,20},{1,9},{5... | collective-permute-start | bytes 98312 | tf_op jit(solution)/shard_map/ppermute | solution.py:35
  49.1 1.4 %collective-permute-done.17 = bf16[8,2048]{1,0:T(8,128)(2,1)S(1)} collective-permute-done((bf16[8,2048]{1,0:T(8,128)(2,1)S(1)}, bf16[8,2048]{1,0:T(8,128)(2,1)S(1)}, u32[]{:S(2)}, u32[]{:S(2)}) %collective-permute-start.17) | collective-permute-done | bytes 32800 | tf_op jit(solution)/shard_map/ppermute | solution.py:35
  50.5 2.7 %collective-permute-done.16 = bf16[8,2048]{1,0:T(8,128)(2,1)S(1)} collective-permute-done((bf16[8,2048]{1,0:T(8,128)(2,1)S(1)}, bf16[8,2048]{1,0:T(8,128)(2,1)S(1)}, u32[]{:S(2)}, u32[]{:S(2)}) %collective-permute-start.16) | collective-permute-done | bytes 32800 | tf_op jit(solution)/shard_map/ppermute | solution.py:35
  53.2 0.0 collective-permute-done.9
  53.2 0.6 %add_convert_fusion = bf16[8,2048]{1,0:T(8,128)(2,1)} fusion(bf16[8,2048]{1,0:T(8,128)(2,1)S(1)} %collective-permute-done.17, bf16[8,2048]{1,0:T(8,128)(2,1)S(1)} %collective-permute-done.16, f32[8,2048]{1,0:T(8,128)S(1)} %get-tuple-element.48, bf16[8,2048]{1,0:T(8,128)(2,1)S(1)} %collective-permute-done.9), kind=kLoop, calls=%fused_computation.1 | loop fusion | flops 114688 | bytes 196608 | tf_op jit(solution)/shard_map/convert_element_type | solution.py:458
  (5 shorter events, 0.1 us)
Async XLA Ops:
  0.6 10.2 %collective-permute-start.1 = (bf16[1024,2048]{1,0:T(8,128)(2,1)}, bf16[1024,2048]{1,0:T(8,128)(2,1)S(1)}, u32[]{:S(2)}, u32[]{:S(2)}) collective-permute-start(bf16[1024,2048]{1,0:T(8,128)(2,1)} %w_hbm.1), channel_id=1, source_target_pairs={{0,1},{1,0},{2,3},{3,2},{4,5},{5,4},{6,7},{7,6},{8,9},{9,8},{10,11... | collective-permute-start | bytes 12582920 | tf_op jit(solution)/shard_map/ppermute | solution.py:35
  6.0 4.8 %copy-start = (bf16[8,2048]{1,0:T(8,128)(2,1)S(1)}, bf16[8,2048]{1,0:T(8,128)(2,1)}, u32[]{:S(2)}) copy-start(bf16[8,2048]{1,0:T(8,128)(2,1)} %refs_4_.1) | copy-start | bytes 98308
  6.0 4.8 %copy-start.2 = (s32[8,8]{1,0:T(8,128)S(1)}, s32[8,8]{1,0:T(8,128)}, u32[]{:S(2)}) copy-start(s32[8,8]{1,0:T(8,128)} %refs_5_.1) | copy-start | bytes 772
  6.1 4.8 %copy-start.3 = (s32[8,8]{1,0:T(8,128)S(1)}, s32[8,8]{1,0:T(8,128)}, u32[]{:S(2)}) copy-start(s32[8,8]{1,0:T(8,128)} %refs_6_.1) | copy-start | bytes 772
  6.1 4.8 %collective-permute-start = (bf16[1,8,2048]{2,1,0:T(8,128)(2,1)S(1)}, bf16[1,8,2048]{2,1,0:T(8,128)(2,1)S(1)}, u32[]{:S(2)}, u32[]{:S(2)}) collective-permute-start(bf16[1,8,2048]{2,1,0:T(8,128)(2,1)S(1)} %get-tuple-element.33), channel_id=1, source_target_pairs={{0,2},{1,3},{2,0},{3,1},{4,6},{5,7},{6,4},{7,5},{8,10},{9,11},{10,... | collective-permute-start | bytes 98312 | tf_op jit(solution)/shard_map/ppermute | solution.py:35
  12.1 4.8 %copy-start.1 = (f32[2048]{0:T(1024)S(1)}, f32[2048]{0:T(1024)}, u32[]{:S(2)}) copy-start(f32[2048]{0:T(1024)} %param.17) | copy-start | bytes 24580
  12.1 4.3 %collective-permute-start.2 = (bf16[16,2176]{1,0:T(8,128)(2,1)S(1)}, bf16[16,2176]{1,0:T(8,128)(2,1)S(1)}, u32[]{:S(2)}, u32[]{:S(2)}) collective-permute-start(bf16[16,2176]{1,0:T(8,128)(2,1)S(1)} %get-tuple-element.36.after_ref), channel_id=1, source_target_pairs={{0,2},{1,3},{2,0},{3,1},{4,6},{5,7},{6,4},{7,5},{8,10},{9,11},{10,... | collective-permute-start | bytes 208904 | tf_op jit(solution)/shard_map/ppermute | solution.py:35
  16.4 15.5 %collective-permute-start.5 = (bf16[2048,768]{1,0:T(8,128)(2,1)S(1)}, bf16[2048,768]{1,0:T(8,128)(2,1)S(1)}, u32[]{:S(2)}, u32[]{:S(2)}) collective-permute-start(bf16[2048,768]{1,0:T(8,128)(2,1)S(1)} %get-tuple-element.42.refs_3_.refs_4_), channel_id=1, source_target_pairs={{0,1},{1,0},{2,3},{3,2},{4,5},{5,4},{6,7},{7,6},{8,9},{9,8},{10,11... | collective-permute-start | bytes 9437192 | tf_op jit(solution)/shard_map/ppermute | solution.py:35
  16.4 15.5 %collective-permute-start.6 = (bf16[384,2048]{1,0:T(8,128)(2,1)S(1)}, bf16[384,2048]{1,0:T(8,128)(2,1)S(1)}, u32[]{:S(2)}, u32[]{:S(2)}) collective-permute-start(bf16[384,2048]{1,0:T(8,128)(2,1)S(1)} %get-tuple-element.43.refs_5_.refs_6_), channel_id=1, source_target_pairs={{0,1},{1,0},{2,3},{3,2},{4,5},{5,4},{6,7},{7,6},{8,9},{9,8},{10,11... | collective-permute-start | bytes 4718600 | tf_op jit(solution)/shard_map/ppermute | solution.py:35
  17.6 7.8 %collective-permute-start.10 = (bf16[16,2176]{1,0:T(8,128)(2,1)S(1)}, bf16[16,2176]{1,0:T(8,128)(2,1)S(1)}, u32[]{:S(2)}, u32[]{:S(2)}) collective-permute-start(bf16[16,2176]{1,0:T(8,128)(2,1)S(1)} %get-tuple-element.41.refs_0_), channel_id=1, source_target_pairs={{0,16},{4,20},{8,24},{12,28},{16,0},{20,4},{24,8},{28,12},{1,17},{... | collective-permute-start | bytes 208904 | tf_op jit(solution)/shard_map/ppermute | solution.py:35
  20.4 6.9 %collective-permute-start.11 = (bf16[16,2176]{1,0:T(8,128)(2,1)S(1)}, bf16[16,2176]{1,0:T(8,128)(2,1)S(1)}, u32[]{:S(2)}, u32[]{:S(2)}) collective-permute-start(bf16[16,2176]{1,0:T(8,128)(2,1)S(1)} %get-tuple-element.41.refs_0_), channel_id=1, source_target_pairs={{0,24},{4,28},{8,16},{12,20},{16,8},{20,12},{24,0},{28,4},{1,25},{... | collective-permute-start | bytes 208904 | tf_op jit(solution)/shard_map/ppermute | solution.py:35
  21.7 6.5 %collective-permute-start.3 = (bf16[16,2176]{1,0:T(8,128)(2,1)S(1)}, bf16[16,2176]{1,0:T(8,128)(2,1)S(1)}, u32[]{:S(2)}, u32[]{:S(2)}) collective-permute-start(bf16[16,2176]{1,0:T(8,128)(2,1)S(1)} %get-tuple-element.41.refs_0_), channel_id=1, source_target_pairs={{0,8},{4,12},{8,0},{12,4},{16,24},{20,28},{24,16},{28,20},{1,9},{5... | collective-permute-start | bytes 208904 | tf_op jit(solution)/shard_map/ppermute | solution.py:35
  25.4 4.9 %collective-permute-start.12 = (bf16[16,2176]{1,0:T(8,128)(2,1)S(1)}, bf16[16,2176]{1,0:T(8,128)(2,1)S(1)}, u32[]{:S(2)}, u32[]{:S(2)}) collective-permute-start(bf16[16,2176]{1,0:T(8,128)(2,1)S(1)} %collective-permute-done.10.refs_0_), channel_id=1, source_target_pairs={{0,4},{4,0},{8,12},{12,8},{16,20},{20,16},{24,28},{28,24},{1,5},{5... | collective-permute-start | bytes 208904 | tf_op jit(solution)/shard_map/ppermute | solution.py:35
  27.2 4.7 %collective-permute-start.13 = (bf16[16,2176]{1,0:T(8,128)(2,1)S(1)}, bf16[16,2176]{1,0:T(8,128)(2,1)S(1)}, u32[]{:S(2)}, u32[]{:S(2)}) collective-permute-start(bf16[16,2176]{1,0:T(8,128)(2,1)S(1)} %collective-permute-done.11.refs_1_), channel_id=1, source_target_pairs={{0,4},{4,0},{8,12},{12,8},{16,20},{20,16},{24,28},{28,24},{1,5},{5... | collective-permute-start | bytes 208904 | tf_op jit(solution)/shard_map/ppermute | solution.py:35
  28.3 7.3 %collective-permute-start.4 = (bf16[32,2176]{1,0:T(8,128)(2,1)S(1)}, bf16[32,2176]{1,0:T(8,128)(2,1)S(1)}, u32[]{:S(2)}, u32[]{:S(2)}) collective-permute-start(bf16[32,2176]{1,0:T(8,128)(2,1)S(1)} %pad_maximum_fusion), channel_id=1, source_target_pairs={{0,4},{4,0},{8,12},{12,8},{16,20},{20,16},{24,28},{28,24},{1,5},{5... | collective-permute-start | bytes 417800 | tf_op jit(solution)/shard_map/ppermute | solution.py:35
  33.8 5.3 %collective-permute-start.14 = (bf16[32,2048]{1,0:T(8,128)(2,1)S(1)}, bf16[32,2048]{1,0:T(8,128)(2,1)S(1)}, u32[]{:S(2)}, u32[]{:S(2)}) collective-permute-start(bf16[32,2048]{1,0:T(8,128)(2,1)S(1)} %get-tuple-element.51), channel_id=1, source_target_pairs={{0,2},{1,3},{2,0},{3,1},{4,6},{5,7},{6,4},{7,5},{8,10},{9,11},{10,... | collective-permute-start | bytes 393224 | tf_op jit(solution)/shard_map/ppermute | solution.py:35
  37.4 5.0 %collective-permute-start.7 = (bf16[32,2048]{1,0:T(8,128)(2,1)S(1)}, bf16[32,2048]{1,0:T(8,128)(2,1)S(1)}, u32[]{:S(2)}, u32[]{:S(2)}) collective-permute-start(bf16[32,2048]{1,0:T(8,128)(2,1)S(1)} %get-tuple-element.45), channel_id=1, source_target_pairs={{0,2},{1,3},{2,0},{3,1},{4,6},{5,7},{6,4},{7,5},{8,10},{9,11},{10,... | collective-permute-start | bytes 393224 | tf_op jit(solution)/shard_map/ppermute | solution.py:35
  39.1 4.6 %collective-permute-start.15 = (bf16[16,2048]{1,0:T(8,128)(2,1)S(1)}, bf16[16,2048]{1,0:T(8,128)(2,1)S(1)}, u32[]{:S(2)}, u32[]{:S(2)}) collective-permute-start(bf16[16,2048]{1,0:T(8,128)(2,1)S(1)} %get-tuple-element.53), channel_id=1, source_target_pairs={{0,4},{4,0},{8,12},{12,8},{16,20},{20,16},{24,28},{28,24},{1,5},{5... | collective-permute-start | bytes 196616 | tf_op jit(solution)/shard_map/ppermute | solution.py:35
  42.4 5.9 %collective-permute-start.8 = (bf16[16,2048]{1,0:T(8,128)(2,1)S(1)}, bf16[16,2048]{1,0:T(8,128)(2,1)S(1)}, u32[]{:S(2)}, u32[]{:S(2)}) collective-permute-start(bf16[16,2048]{1,0:T(8,128)(2,1)S(1)} %get-tuple-element.47), channel_id=1, source_target_pairs={{0,4},{4,0},{8,12},{12,8},{16,20},{20,16},{24,28},{28,24},{1,5},{5... | collective-permute-start | bytes 196616 | tf_op jit(solution)/shard_map/ppermute | solution.py:35
  43.7 6.7 %collective-permute-start.17 = (bf16[8,2048]{1,0:T(8,128)(2,1)S(1)}, bf16[8,2048]{1,0:T(8,128)(2,1)S(1)}, u32[]{:S(2)}, u32[]{:S(2)}) collective-permute-start(bf16[8,2048]{1,0:T(8,128)(2,1)S(1)} %get-tuple-element.55), channel_id=1, source_target_pairs={{0,24},{4,28},{8,16},{12,20},{16,8},{20,12},{24,0},{28,4},{1,25},{... | collective-permute-start | bytes 98312 | tf_op jit(solution)/shard_map/ppermute | solution.py:35
  48.4 4.8 %collective-permute-start.16 = (bf16[8,2048]{1,0:T(8,128)(2,1)S(1)}, bf16[8,2048]{1,0:T(8,128)(2,1)S(1)}, u32[]{:S(2)}, u32[]{:S(2)}) collective-permute-start(bf16[8,2048]{1,0:T(8,128)(2,1)S(1)} %get-tuple-element.54), channel_id=1, source_target_pairs={{0,16},{4,20},{8,24},{12,28},{16,0},{20,4},{24,8},{28,12},{1,17},{... | collective-permute-start | bytes 98312 | tf_op jit(solution)/shard_map/ppermute | solution.py:35
  48.4 4.8 %collective-permute-start.9 = (bf16[8,2048]{1,0:T(8,128)(2,1)S(1)}, bf16[8,2048]{1,0:T(8,128)(2,1)S(1)}, u32[]{:S(2)}, u32[]{:S(2)}) collective-permute-start(bf16[8,2048]{1,0:T(8,128)(2,1)S(1)} %get-tuple-element.49), channel_id=1, source_target_pairs={{0,8},{4,12},{8,0},{12,4},{16,24},{20,28},{24,16},{28,20},{1,9},{5... | collective-permute-start | bytes 98312 | tf_op jit(solution)/shard_map/ppermute | solution.py:35
where the time goes:
time: 54 us; the launch traced here: 53.8 us
  starting transfers between devices  23.7 us (44%)
  Pallas kernels  15 us (28%)
  waiting for transfers between devices  13.6 us (25%)
  between operations  0.77 us (1%)
  other arithmetic  0.64 us (1%)
    ppermute x18, starting transfers between devices, partner(): return lax.ppermute(block, axis, [(i, i ^ mask) for i in range(count)])  23.7 us
    pallas_call x11, Pallas kernels, kernel_call(): pl.pallas_call(body, out_shape=outs, in_specs=in_specs or [VMEM] * len(op...  15 us
    ppermute x18, waiting for transfers between devices, partner(): return lax.ppermute(block, axis, [(i, i ^ mask) for i in range(count)])  13.6 us
  transfers between devices with their start and end apart: 18, of which 8 were waited for; matrix products, arithmetic and copies ran while one was open for 0% of the time, Pallas kernels for 26%

commit v1 on v0

--- a/solution.py
+++ b/solution.py
@@ -428,27 +428,24 @@
     blocks, w_near = attend(queries, kv_cache, new_kv, lengths, w_out)
     total, sent, more = project(blocks, w_near, w_other, residual, expert_ids, route_level)
     w_in, w_down = fetch(sent, w_in, w_down)
-    w_in, w_down, more = lax.optimization_barrier((w_in, w_down, more))
     weights = (w_in, partner(w_in, "side", 1), w_down, partner(w_down, "side", 1))
     normed, stream = kernel_call(
         norm_kernel,
         (total, more, norm_gain.reshape(1, width)),
         (
             jax.ShapeDtypeStruct(total.shape, jnp.bfloat16),
-            jax.ShapeDtypeStruct((rows, width), jnp.bfloat16),
+            pltpu.VMEM((rows, width), jnp.bfloat16),
         ),
     )
 
     early, late = dev_groups(devs)
     near = {0: normed}
-    for away in late + early[1:]:
+    for away in early[1:] + late:
         near[away] = partner(normed, "dev", away)
-    near_early = [near[away] for away in early]
-    far_early = [partner(jnp.concatenate(near_early), "dev", 1)]
-    near_late = [near[away] for away in late]
-    far_late = [partner(near[away], "dev", 1) for away in late]
     home = []
-    for aways, blocks in ((early, near_early + far_early), (late, near_late + far_late)):
+    for aways in (early, late):
+        blocks = [near[away] for away in aways]
+        blocks += [partner(near[away], "dev", 1) for away in aways]
         kept, sent = run_experts(blocks, weights, rows, width)
         for away, block in zip(aways, homeward(kept, sent, aways, rows)):
             if away:

time: 54 us -> 54.4 us (level)
  starting transfers between devices: 23.7 us -> 25.1 us
  waiting for transfers between devices: 13.6 us -> 12.6 us
  local copies, waits for them, and re-layouts: 0.02 us -> 0.64 us
    ppermute x18 -> x19, starting transfers between devices: 23.7 us -> 25.1 us  [partner(): return lax.ppermute(block, axis, [(i, i ^ mask) for i in range(count)])]
    ppermute x18 -> x19, waiting for transfers between devices: 13.6 us -> 12.6 us  [partner(): return lax.ppermute(block, axis, [(i, i ^ mask) for i in range(count)])]
    unnamed x8 -> x9, local copies, waits for them, and re-layouts: 0.02 us -> 0.64 us
  transfers between devices with their start and end apart: 18 -> 19, of which waited for: 8 -> 9; matrix products, arithmetic and copies ran while one was open for 0% -> 1% of each run, Pallas kernels for 26% -> 20%
where the time goes in v1:
time: 54.4 us; the launch traced here: 54.2 us
  starting transfers between devices  25.1 us (46%)
  Pallas kernels  14.6 us (27%)
  waiting for transfers between devices  12.6 us (23%)
  between operations  0.77 us (1%)
  local copies, waits for them, and re-layouts  0.64 us (1%)
  other arithmetic  0.63 us (1%)
    ppermute x19, starting transfers between devices, partner(): return lax.ppermute(block, axis, [(i, i ^ mask) for i in range(count)])  25.1 us
    pallas_call x11, Pallas kernels, kernel_call(): pl.pallas_call(body, out_shape=outs, in_specs=in_specs or [VMEM] * len(op...  14.6 us
    ppermute x19, waiting for transfers between devices, partner(): return lax.ppermute(block, axis, [(i, i ^ mask) for i in range(count)])  12.6 us
  transfers between devices with their start and end apart: 19, of which 9 were waited for; matrix products, arithmetic and copies ran while one was open for 1% of the time, Pallas kernels for 20%

profile of v1, /device:TPU:0, one launch (start us, length us, event | category | flops | bytes accessed | tf_op | source)
XLA Modules:
  0.0 54.2 jit_solution(1559048291918925045)
XLA Ops:
  0.6 0.6 %collective-permute-start.1 = (bf16[1024,2048]{1,0:T(8,128)(2,1)}, bf16[1024,2048]{1,0:T(8,128)(2,1)S(1)}, u32[]{:S(2)}, u32[]{:S(2)}) collective-permute-start(bf16[1024,2048]{1,0:T(8,128)(2,1)} %w_hbm.1), channel_id=1, source_target_pairs={{0,1},{1,0},{2,3},{3,2},{4,5},{5,4},{6,7},{7,6},{8,9},{9,8},{10,11... | collective-permute-start | bytes 12582920 | tf_op jit(solution)/shard_map/ppermute | solution.py:35
  1.2 4.8 %shard_map.122 = (bf16[1,8,2048]{2,1,0:T(8,128)(2,1)S(1)}, bf16[8,2048]{1,0:T(8,128)(2,1)S(1)}, bf16[8,192,512]{2,1,0:T(8,128)(2,1)S(1)}, bf16[8,512]{1,0:T(8,128)(2,1)S(1)}) custom-call(bf16[8,4096]{1,0:T(8,128)(2,1)} %q_hbm.1, bf16[8,192,1024]{2,1,0:T(8,128)(2,1)} %kv_hbm.1, bf16[8,1024]{1,0:T(8,128)(2,1)} %new_hbm.1, s32[8]{0:T(128)} %length_hbm.3), custom_call_target="tpu_custom_call" | custom-call | tf_op jit(solution)/shard_map/pallas_call | solution.py:18
  6.0 0.0 copy-start
  6.0 0.0 copy-start.2
  6.1 0.0 copy-start.3
  6.1 2.6 %collective-permute-start = (bf16[1,8,2048]{2,1,0:T(8,128)(2,1)S(1)}, bf16[1,8,2048]{2,1,0:T(8,128)(2,1)S(1)}, u32[]{:S(2)}, u32[]{:S(2)}) collective-permute-start(bf16[1,8,2048]{2,1,0:T(8,128)(2,1)S(1)} %get-tuple-element.30), channel_id=1, source_target_pairs={{0,2},{1,3},{2,0},{3,1},{4,6},{5,7},{6,4},{7,5},{8,10},{9,11},{10,... | collective-permute-start | bytes 98312 | tf_op jit(solution)/shard_map/ppermute | solution.py:35
  8.6 2.2 %shard_map.123 = (bf16[1,8,2048]{2,1,0:T(8,128)(2,1)S(1)}, bf16[1024,2048]{1,0:T(8,128)(2,1)S(1)}) custom-call(bf16[8,2048]{1,0:T(8,128)(2,1)S(1)} %get-tuple-element.26.q_ref, bf16[8,192,512]{2,1,0:T(8,128)(2,1)S(1)} %get-tuple-element.27.kv, bf16[8,512]{1,0:T(8,128)(2,1)S(1)} %get-tuple-element.28.new_ref, s32[8]{0:T(128)} %length_hbm.3, ...), custom_call_target="tpu_custom_call" | custom-call | flops 8388608 | bytes 8388608 | tf_op jit(solution)/shard_map/pallas_call | solution.py:18
  10.9 0.0 collective-permute-done.refs_1_
  10.9 0.0 collective-permute-done.1.refs_3_
  10.9 0.0 copy-done
  10.9 0.0 copy-done.2
  10.9 0.0 copy-done.3
  10.9 1.2 %shard_map.124 = (f32[16,2176]{1,0:T(8,128)S(1)}, bf16[16,2176]{1,0:T(8,128)(2,1)S(1)}) custom-call(bf16[1,8,2048]{2,1,0:T(8,128)(2,1)S(1)} %get-tuple-element.29.refs_0_, bf16[1,8,2048]{2,1,0:T(8,128)(2,1)S(1)} %collective-permute-done.refs_1_, bf16[1024,2048]{1,0:T(8,128)(2,1)S(1)} %get-tuple-element.31.refs_2_, ...), custom_call_target="tpu_custom_call" | custom-call | tf_op jit(solution)/shard_map/pallas_call | solution.py:18
  12.1 0.0 copy-start.1
  12.1 2.4 %shard_map.126 = (bf16[2048,768]{1,0:T(8,128)(2,1)S(1)}, bf16[384,2048]{1,0:T(8,128)(2,1)S(1)}) custom-call(bf16[16,2176]{1,0:T(8,128)(2,1)S(1)} %get-tuple-element.33.after_ref, bf16[1,2048,768]{2,1,0:T(8,128)(2,1)} %in_hbm_ref.1, bf16[1,384,2048]{2,1,0:T(8,128)(2,1)} %down_hbm_ref.1), custom_call_target="tpu_custom_call" | custom-call | bytes 8388608 | tf_op jit(solution)/shard_map/pallas_call | solution.py:18
  14.5 0.3 collective-permute-start.6
  14.8 0.3 collective-permute-start.7
  15.1 1.7 %collective-permute-start.2 = (bf16[16,2176]{1,0:T(8,128)(2,1)S(1)}, bf16[16,2176]{1,0:T(8,128)(2,1)S(1)}, u32[]{:S(2)}, u32[]{:S(2)}) collective-permute-start(bf16[16,2176]{1,0:T(8,128)(2,1)S(1)} %get-tuple-element.33.after_ref), channel_id=1, source_target_pairs={{0,2},{1,3},{2,0},{3,1},{4,6},{5,7},{6,4},{7,5},{8,10},{9,11},{10,... | collective-permute-start | bytes 208904 | tf_op jit(solution)/shard_map/ppermute | solution.py:35
  16.8 2.6 %collective-permute-done.2.more_ref = bf16[16,2176]{1,0:T(8,128)(2,1)S(1)} collective-permute-done((bf16[16,2176]{1,0:T(8,128)(2,1)S(1)}, bf16[16,2176]{1,0:T(8,128)(2,1)S(1)}, u32[]{:S(2)}, u32[]{:S(2)}) %collective-permute-start.2) | collective-permute-done | bytes 69664 | tf_op jit(solution)/shard_map/ppermute | solution.py:35
  19.4 0.0 copy-done.1
  19.4 0.1 shard_map.125
  19.5 2.8 %collective-permute-start.11 = (bf16[16,2176]{1,0:T(8,128)(2,1)S(1)}, bf16[16,2176]{1,0:T(8,128)(2,1)S(1)}, u32[]{:S(2)}, u32[]{:S(2)}) collective-permute-start(bf16[16,2176]{1,0:T(8,128)(2,1)S(1)} %get-tuple-element.35.refs_0_), channel_id=1, source_target_pairs={{0,16},{4,20},{8,24},{12,28},{16,0},{20,4},{24,8},{28,12},{1,17},{... | collective-permute-start | bytes 208904 | tf_op jit(solution)/shard_map/ppermute | solution.py:35
  22.4 1.3 %collective-permute-start.12 = (bf16[16,2176]{1,0:T(8,128)(2,1)S(1)}, bf16[16,2176]{1,0:T(8,128)(2,1)S(1)}, u32[]{:S(2)}, u32[]{:S(2)}) collective-permute-start(bf16[16,2176]{1,0:T(8,128)(2,1)S(1)} %get-tuple-element.35.refs_0_), channel_id=1, source_target_pairs={{0,24},{4,28},{8,16},{12,20},{16,8},{20,12},{24,0},{28,4},{1,25},{... | collective-permute-start | bytes 208904 | tf_op jit(solution)/shard_map/ppermute | solution.py:35
  23.7 0.2 collective-permute-start.3
  23.9 1.0 %collective-permute-done.11.refs_0_ = bf16[16,2176]{1,0:T(8,128)(2,1)S(1)} collective-permute-done((bf16[16,2176]{1,0:T(8,128)(2,1)S(1)}, bf16[16,2176]{1,0:T(8,128)(2,1)S(1)}, u32[]{:S(2)}, u32[]{:S(2)}) %collective-permute-start.11) | collective-permute-done | bytes 69664 | tf_op jit(solution)/shard_map/ppermute | solution.py:35
  25.0 1.9 %collective-permute-start.13 = (bf16[16,2176]{1,0:T(8,128)(2,1)S(1)}, bf16[16,2176]{1,0:T(8,128)(2,1)S(1)}, u32[]{:S(2)}, u32[]{:S(2)}) collective-permute-start(bf16[16,2176]{1,0:T(8,128)(2,1)S(1)} %collective-permute-done.11.refs_0_), channel_id=1, source_target_pairs={{0,4},{4,0},{8,12},{12,8},{16,20},{20,16},{24,28},{28,24},{1,5},{5... | collective-permute-start | bytes 208904 | tf_op jit(solution)/shard_map/ppermute | solution.py:35
  26.9 1.7 %collective-permute-done.12.refs_1_ = bf16[16,2176]{1,0:T(8,128)(2,1)S(1)} collective-permute-done((bf16[16,2176]{1,0:T(8,128)(2,1)S(1)}, bf16[16,2176]{1,0:T(8,128)(2,1)S(1)}, u32[]{:S(2)}, u32[]{:S(2)}) %collective-permute-start.12) | collective-permute-done | bytes 69664 | tf_op jit(solution)/shard_map/ppermute | solution.py:35
  28.6 1.5 %collective-permute-start.14 = (bf16[16,2176]{1,0:T(8,128)(2,1)S(1)}, bf16[16,2176]{1,0:T(8,128)(2,1)S(1)}, u32[]{:S(2)}, u32[]{:S(2)}) collective-permute-start(bf16[16,2176]{1,0:T(8,128)(2,1)S(1)} %collective-permute-done.12.refs_1_), channel_id=1, source_target_pairs={{0,4},{4,0},{8,12},{12,8},{16,20},{20,16},{24,28},{28,24},{1,5},{5... | collective-permute-start | bytes 208904 | tf_op jit(solution)/shard_map/ppermute | solution.py:35
  30.1 0.0 collective-permute-done.3.refs_1_
  30.1 0.5 collective-permute-start.4
  30.6 0.0 collective-permute-done.13.refs_2_
  30.6 1.5 %collective-permute-start.5 = (bf16[16,2176]{1,0:T(8,128)(2,1)S(1)}, bf16[16,2176]{1,0:T(8,128)(2,1)S(1)}, u32[]{:S(2)}, u32[]{:S(2)}) collective-permute-start(bf16[16,2176]{1,0:T(8,128)(2,1)S(1)} %collective-permute-done.3.refs_1_), channel_id=1, source_target_pairs={{0,4},{4,0},{8,12},{12,8},{16,20},{20,16},{24,28},{28,24},{1,5},{5... | collective-permute-start | bytes 208904 | tf_op jit(solution)/shard_map/ppermute | solution.py:35
  32.1 0.8 %collective-permute-done.14.refs_3_ = bf16[16,2176]{1,0:T(8,128)(2,1)S(1)} collective-permute-done((bf16[16,2176]{1,0:T(8,128)(2,1)S(1)}, bf16[16,2176]{1,0:T(8,128)(2,1)S(1)}, u32[]{:S(2)}, u32[]{:S(2)}) %collective-permute-start.14) | collective-permute-done | bytes 69664 | tf_op jit(solution)/shard_map/ppermute | solution.py:35
  32.9 0.0 collective-permute-done.7.refs_7_
  32.9 0.0 collective-permute-done.6.refs_5_
  32.9 1.9 %shard_map.130 = (f32[32,2048]{1,0:T(8,128)S(1)}, bf16[32,2048]{1,0:T(8,128)(2,1)S(1)}) custom-call(bf16[16,2176]{1,0:T(8,128)(2,1)S(1)} %collective-permute-done.11.refs_0_, bf16[16,2176]{1,0:T(8,128)(2,1)S(1)} %collective-permute-done.12.refs_1_, bf16[16,2176]{1,0:T(8,128)(2,1)S(1)} %collective-permute-done.13.refs_2_, ...), custom_call_target="tpu_custom_call" | custom-call | flops 1073741824 | bytes 4194304 | tf_op jit(solution)/shard_map/pallas_call | solution.py:18
  34.8 1.6 %collective-permute-start.15 = (bf16[32,2048]{1,0:T(8,128)(2,1)S(1)}, bf16[32,2048]{1,0:T(8,128)(2,1)S(1)}, u32[]{:S(2)}, u32[]{:S(2)}) collective-permute-start(bf16[32,2048]{1,0:T(8,128)(2,1)S(1)} %get-tuple-element.45), channel_id=1, source_target_pairs={{0,2},{1,3},{2,0},{3,1},{4,6},{5,7},{6,4},{7,5},{8,10},{9,11},{10,... | collective-permute-start | bytes 393224 | tf_op jit(solution)/shard_map/ppermute | solution.py:35
  36.3 0.0 collective-permute-done.4.refs_2_
  36.3 0.0 collective-permute-done.5.refs_3_
  36.3 1.9 %shard_map.127 = (f32[32,2048]{1,0:T(8,128)S(1)}, bf16[32,2048]{1,0:T(8,128)(2,1)S(1)}) custom-call(bf16[16,2176]{1,0:T(8,128)(2,1)S(1)} %get-tuple-element.35.refs_0_, bf16[16,2176]{1,0:T(8,128)(2,1)S(1)} %collective-permute-done.3.refs_1_, bf16[16,2176]{1,0:T(8,128)(2,1)S(1)} %collective-permute-done.4.refs_2_, ...), custom_call_target="tpu_custom_call" | custom-call | flops 1073741824 | bytes 4194304 | tf_op jit(solution)/shard_map/pallas_call | solution.py:18
  38.2 0.6 %collective-permute-start.8 = (bf16[32,2048]{1,0:T(8,128)(2,1)S(1)}, bf16[32,2048]{1,0:T(8,128)(2,1)S(1)}, u32[]{:S(2)}, u32[]{:S(2)}) collective-permute-start(bf16[32,2048]{1,0:T(8,128)(2,1)S(1)} %get-tuple-element.39), channel_id=1, source_target_pairs={{0,2},{1,3},{2,0},{3,1},{4,6},{5,7},{6,4},{7,5},{8,10},{9,11},{10,... | collective-permute-start | bytes 393224 | tf_op jit(solution)/shard_map/ppermute | solution.py:35
  38.8 1.9 %collective-permute-done.15.more_ref = bf16[32,2048]{1,0:T(8,128)(2,1)S(1)} collective-permute-done((bf16[32,2048]{1,0:T(8,128)(2,1)S(1)}, bf16[32,2048]{1,0:T(8,128)(2,1)S(1)}, u32[]{:S(2)}, u32[]{:S(2)}) %collective-permute-start.15) | collective-permute-done | bytes 131104 | tf_op jit(solution)/shard_map/ppermute | solution.py:35
  40.8 1.6 %collective-permute-start.16 = (bf16[16,2048]{1,0:T(8,128)(2,1)S(1)}, bf16[16,2048]{1,0:T(8,128)(2,1)S(1)}, u32[]{:S(2)}, u32[]{:S(2)}) collective-permute-start(bf16[16,2048]{1,0:T(8,128)(2,1)S(1)} %get-tuple-element.47), channel_id=1, source_target_pairs={{0,4},{4,0},{8,12},{12,8},{16,20},{20,16},{24,28},{28,24},{1,5},{5... | collective-permute-start | bytes 196616 | tf_op jit(solution)/shard_map/ppermute | solution.py:35
  42.3 0.9 %collective-permute-done.8.more_ref = bf16[32,2048]{1,0:T(8,128)(2,1)S(1)} collective-permute-done((bf16[32,2048]{1,0:T(8,128)(2,1)S(1)}, bf16[32,2048]{1,0:T(8,128)(2,1)S(1)}, u32[]{:S(2)}, u32[]{:S(2)}) %collective-permute-start.8) | collective-permute-done | bytes 131104 | tf_op jit(solution)/shard_map/ppermute | solution.py:35
  43.2 1.6 %collective-permute-start.9 = (bf16[16,2048]{1,0:T(8,128)(2,1)S(1)}, bf16[16,2048]{1,0:T(8,128)(2,1)S(1)}, u32[]{:S(2)}, u32[]{:S(2)}) collective-permute-start(bf16[16,2048]{1,0:T(8,128)(2,1)S(1)} %get-tuple-element.41), channel_id=1, source_target_pairs={{0,4},{4,0},{8,12},{12,8},{16,20},{20,16},{24,28},{28,24},{1,5},{5... | collective-permute-start | bytes 196616 | tf_op jit(solution)/shard_map/ppermute | solution.py:35
  44.8 0.3 collective-permute-done.16.more_ref
  45.1 3.5 %collective-permute-start.18 = (bf16[8,2048]{1,0:T(8,128)(2,1)S(1)}, bf16[8,2048]{1,0:T(8,128)(2,1)S(1)}, u32[]{:S(2)}, u32[]{:S(2)}) collective-permute-start(bf16[8,2048]{1,0:T(8,128)(2,1)S(1)} %get-tuple-element.49), channel_id=1, source_target_pairs={{0,24},{4,28},{8,16},{12,20},{16,8},{20,12},{24,0},{28,4},{1,25},{... | collective-permute-start | bytes 98312 | tf_op jit(solution)/shard_map/ppermute | solution.py:35
  48.7 0.0 collective-permute-start.17
  48.7 0.0 collective-permute-done.9.more_ref
  48.7 1.0 %collective-permute-start.10 = (bf16[8,2048]{1,0:T(8,128)(2,1)S(1)}, bf16[8,2048]{1,0:T(8,128)(2,1)S(1)}, u32[]{:S(2)}, u32[]{:S(2)}) collective-permute-start(bf16[8,2048]{1,0:T(8,128)(2,1)S(1)} %get-tuple-element.43), channel_id=1, source_target_pairs={{0,8},{4,12},{8,0},{12,4},{16,24},{20,28},{24,16},{28,20},{1,9},{5... | collective-permute-start | bytes 98312 | tf_op jit(solution)/shard_map/ppermute | solution.py:35
  49.7 0.6 %copy.13 = bf16[8,2048]{1,0:T(8,128)(2,1)} copy(bf16[8,2048]{1,0:T(8,128)(2,1)S(1)} %get-tuple-element.50) | data formatting | bytes 65536
  50.3 0.6 %collective-permute-done.18 = bf16[8,2048]{1,0:T(8,128)(2,1)S(1)} collective-permute-done((bf16[8,2048]{1,0:T(8,128)(2,1)S(1)}, bf16[8,2048]{1,0:T(8,128)(2,1)S(1)}, u32[]{:S(2)}, u32[]{:S(2)}) %collective-permute-start.18) | collective-permute-done | bytes 32800 | tf_op jit(solution)/shard_map/ppermute | solution.py:35
  50.9 2.7 %collective-permute-done.17 = bf16[8,2048]{1,0:T(8,128)(2,1)S(1)} collective-permute-done((bf16[8,2048]{1,0:T(8,128)(2,1)S(1)}, bf16[8,2048]{1,0:T(8,128)(2,1)S(1)}, u32[]{:S(2)}, u32[]{:S(2)}) %collective-permute-start.17) | collective-permute-done | bytes 32800 | tf_op jit(solution)/shard_map/ppermute | solution.py:35
  53.6 0.0 collective-permute-done.10
  53.6 0.6 %add_convert_fusion = bf16[8,2048]{1,0:T(8,128)(2,1)} fusion(bf16[8,2048]{1,0:T(8,128)(2,1)S(1)} %collective-permute-done.18, bf16[8,2048]{1,0:T(8,128)(2,1)S(1)} %collective-permute-done.17, f32[8,2048]{1,0:T(8,128)S(1)} %get-tuple-element.42, bf16[8,2048]{1,0:T(8,128)(2,1)S(1)} %collective-permute-done.10), kind=kLoop, calls=%fused_computation | loop fusion | flops 114688 | bytes 196608 | tf_op jit(solution)/shard_map/convert_element_type | solution.py:455
  (4 shorter events, 0.1 us)
Async XLA Ops:
  0.6 10.2 %collective-permute-start.1 = (bf16[1024,2048]{1,0:T(8,128)(2,1)}, bf16[1024,2048]{1,0:T(8,128)(2,1)S(1)}, u32[]{:S(2)}, u32[]{:S(2)}) collective-permute-start(bf16[1024,2048]{1,0:T(8,128)(2,1)} %w_hbm.1), channel_id=1, source_target_pairs={{0,1},{1,0},{2,3},{3,2},{4,5},{5,4},{6,7},{7,6},{8,9},{9,8},{10,11... | collective-permute-start | bytes 12582920 | tf_op jit(solution)/shard_map/ppermute | solution.py:35
  6.0 4.8 %copy-start = (bf16[8,2048]{1,0:T(8,128)(2,1)S(1)}, bf16[8,2048]{1,0:T(8,128)(2,1)}, u32[]{:S(2)}) copy-start(bf16[8,2048]{1,0:T(8,128)(2,1)} %refs_4_.1) | copy-start | bytes 98308
  6.0 4.8 %copy-start.2 = (s32[8,8]{1,0:T(8,128)S(1)}, s32[8,8]{1,0:T(8,128)}, u32[]{:S(2)}) copy-start(s32[8,8]{1,0:T(8,128)} %refs_5_.1) | copy-start | bytes 772
  6.1 4.8 %copy-start.3 = (s32[8,8]{1,0:T(8,128)S(1)}, s32[8,8]{1,0:T(8,128)}, u32[]{:S(2)}) copy-start(s32[8,8]{1,0:T(8,128)} %refs_6_.1) | copy-start | bytes 772
  6.1 4.8 %collective-permute-start = (bf16[1,8,2048]{2,1,0:T(8,128)(2,1)S(1)}, bf16[1,8,2048]{2,1,0:T(8,128)(2,1)S(1)}, u32[]{:S(2)}, u32[]{:S(2)}) collective-permute-start(bf16[1,8,2048]{2,1,0:T(8,128)(2,1)S(1)} %get-tuple-element.30), channel_id=1, source_target_pairs={{0,2},{1,3},{2,0},{3,1},{4,6},{5,7},{6,4},{7,5},{8,10},{9,11},{10,... | collective-permute-start | bytes 98312 | tf_op jit(solution)/shard_map/ppermute | solution.py:35
  12.1 7.3 %copy-start.1 = (f32[2048]{0:T(1024)S(1)}, f32[2048]{0:T(1024)}, u32[]{:S(2)}) copy-start(f32[2048]{0:T(1024)} %param.17) | copy-start | bytes 24580
  14.5 18.4 %collective-permute-start.6 = (bf16[2048,768]{1,0:T(8,128)(2,1)S(1)}, bf16[2048,768]{1,0:T(8,128)(2,1)S(1)}, u32[]{:S(2)}, u32[]{:S(2)}) collective-permute-start(bf16[2048,768]{1,0:T(8,128)(2,1)S(1)} %get-tuple-element.36.refs_4_), channel_id=1, source_target_pairs={{0,1},{1,0},{2,3},{3,2},{4,5},{5,4},{6,7},{7,6},{8,9},{9,8},{10,11... | collective-permute-start | bytes 9437192 | tf_op jit(solution)/shard_map/ppermute | solution.py:35
  14.8 18.1 %collective-permute-start.7 = (bf16[384,2048]{1,0:T(8,128)(2,1)S(1)}, bf16[384,2048]{1,0:T(8,128)(2,1)S(1)}, u32[]{:S(2)}, u32[]{:S(2)}) collective-permute-start(bf16[384,2048]{1,0:T(8,128)(2,1)S(1)} %get-tuple-element.37.refs_6_), channel_id=1, source_target_pairs={{0,1},{1,0},{2,3},{3,2},{4,5},{5,4},{6,7},{7,6},{8,9},{9,8},{10,11... | collective-permute-start | bytes 4718600 | tf_op jit(solution)/shard_map/ppermute | solution.py:35
  15.1 4.3 %collective-permute-start.2 = (bf16[16,2176]{1,0:T(8,128)(2,1)S(1)}, bf16[16,2176]{1,0:T(8,128)(2,1)S(1)}, u32[]{:S(2)}, u32[]{:S(2)}) collective-permute-start(bf16[16,2176]{1,0:T(8,128)(2,1)S(1)} %get-tuple-element.33.after_ref), channel_id=1, source_target_pairs={{0,2},{1,3},{2,0},{3,1},{4,6},{5,7},{6,4},{7,5},{8,10},{9,11},{10,... | collective-permute-start | bytes 208904 | tf_op jit(solution)/shard_map/ppermute | solution.py:35
  19.5 5.5 %collective-permute-start.11 = (bf16[16,2176]{1,0:T(8,128)(2,1)S(1)}, bf16[16,2176]{1,0:T(8,128)(2,1)S(1)}, u32[]{:S(2)}, u32[]{:S(2)}) collective-permute-start(bf16[16,2176]{1,0:T(8,128)(2,1)S(1)} %get-tuple-element.35.refs_0_), channel_id=1, source_target_pairs={{0,16},{4,20},{8,24},{12,28},{16,0},{20,4},{24,8},{28,12},{1,17},{... | collective-permute-start | bytes 208904 | tf_op jit(solution)/shard_map/ppermute | solution.py:35
  22.4 6.2 %collective-permute-start.12 = (bf16[16,2176]{1,0:T(8,128)(2,1)S(1)}, bf16[16,2176]{1,0:T(8,128)(2,1)S(1)}, u32[]{:S(2)}, u32[]{:S(2)}) collective-permute-start(bf16[16,2176]{1,0:T(8,128)(2,1)S(1)} %get-tuple-element.35.refs_0_), channel_id=1, source_target_pairs={{0,24},{4,28},{8,16},{12,20},{16,8},{20,12},{24,0},{28,4},{1,25},{... | collective-permute-start | bytes 208904 | tf_op jit(solution)/shard_map/ppermute | solution.py:35
  23.7 6.4 %collective-permute-start.3 = (bf16[16,2176]{1,0:T(8,128)(2,1)S(1)}, bf16[16,2176]{1,0:T(8,128)(2,1)S(1)}, u32[]{:S(2)}, u32[]{:S(2)}) collective-permute-start(bf16[16,2176]{1,0:T(8,128)(2,1)S(1)} %get-tuple-element.35.refs_0_), channel_id=1, source_target_pairs={{0,8},{4,12},{8,0},{12,4},{16,24},{20,28},{24,16},{28,20},{1,9},{5... | collective-permute-start | bytes 208904 | tf_op jit(solution)/shard_map/ppermute | solution.py:35
  25.0 5.6 %collective-permute-start.13 = (bf16[16,2176]{1,0:T(8,128)(2,1)S(1)}, bf16[16,2176]{1,0:T(8,128)(2,1)S(1)}, u32[]{:S(2)}, u32[]{:S(2)}) collective-permute-start(bf16[16,2176]{1,0:T(8,128)(2,1)S(1)} %collective-permute-done.11.refs_0_), channel_id=1, source_target_pairs={{0,4},{4,0},{8,12},{12,8},{16,20},{20,16},{24,28},{28,24},{1,5},{5... | collective-permute-start | bytes 208904 | tf_op jit(solution)/shard_map/ppermute | solution.py:35
  28.6 4.3 %collective-permute-start.14 = (bf16[16,2176]{1,0:T(8,128)(2,1)S(1)}, bf16[16,2176]{1,0:T(8,128)(2,1)S(1)}, u32[]{:S(2)}, u32[]{:S(2)}) collective-permute-start(bf16[16,2176]{1,0:T(8,128)(2,1)S(1)} %collective-permute-done.12.refs_1_), channel_id=1, source_target_pairs={{0,4},{4,0},{8,12},{12,8},{16,20},{20,16},{24,28},{28,24},{1,5},{5... | collective-permute-start | bytes 208904 | tf_op jit(solution)/shard_map/ppermute | solution.py:35
  30.1 6.2 %collective-permute-start.4 = (bf16[16,2176]{1,0:T(8,128)(2,1)S(1)}, bf16[16,2176]{1,0:T(8,128)(2,1)S(1)}, u32[]{:S(2)}, u32[]{:S(2)}) collective-permute-start(bf16[16,2176]{1,0:T(8,128)(2,1)S(1)} %get-tuple-element.35.refs_0_), channel_id=1, source_target_pairs={{0,4},{4,0},{8,12},{12,8},{16,20},{20,16},{24,28},{28,24},{1,5},{5... | collective-permute-start | bytes 208904 | tf_op jit(solution)/shard_map/ppermute | solution.py:35
  30.6 5.7 %collective-permute-start.5 = (bf16[16,2176]{1,0:T(8,128)(2,1)S(1)}, bf16[16,2176]{1,0:T(8,128)(2,1)S(1)}, u32[]{:S(2)}, u32[]{:S(2)}) collective-permute-start(bf16[16,2176]{1,0:T(8,128)(2,1)S(1)} %collective-permute-done.3.refs_1_), channel_id=1, source_target_pairs={{0,4},{4,0},{8,12},{12,8},{16,20},{20,16},{24,28},{28,24},{1,5},{5... | collective-permute-start | bytes 208904 | tf_op jit(solution)/shard_map/ppermute | solution.py:35
  34.8 6.0 %collective-permute-start.15 = (bf16[32,2048]{1,0:T(8,128)(2,1)S(1)}, bf16[32,2048]{1,0:T(8,128)(2,1)S(1)}, u32[]{:S(2)}, u32[]{:S(2)}) collective-permute-start(bf16[32,2048]{1,0:T(8,128)(2,1)S(1)} %get-tuple-element.45), channel_id=1, source_target_pairs={{0,2},{1,3},{2,0},{3,1},{4,6},{5,7},{6,4},{7,5},{8,10},{9,11},{10,... | collective-permute-start | bytes 393224 | tf_op jit(solution)/shard_map/ppermute | solution.py:35
  38.2 5.0 %collective-permute-start.8 = (bf16[32,2048]{1,0:T(8,128)(2,1)S(1)}, bf16[32,2048]{1,0:T(8,128)(2,1)S(1)}, u32[]{:S(2)}, u32[]{:S(2)}) collective-permute-start(bf16[32,2048]{1,0:T(8,128)(2,1)S(1)} %get-tuple-element.39), channel_id=1, source_target_pairs={{0,2},{1,3},{2,0},{3,1},{4,6},{5,7},{6,4},{7,5},{8,10},{9,11},{10,... | collective-permute-start | bytes 393224 | tf_op jit(solution)/shard_map/ppermute | solution.py:35
  40.8 4.3 %collective-permute-start.16 = (bf16[16,2048]{1,0:T(8,128)(2,1)S(1)}, bf16[16,2048]{1,0:T(8,128)(2,1)S(1)}, u32[]{:S(2)}, u32[]{:S(2)}) collective-permute-start(bf16[16,2048]{1,0:T(8,128)(2,1)S(1)} %get-tuple-element.47), channel_id=1, source_target_pairs={{0,4},{4,0},{8,12},{12,8},{16,20},{20,16},{24,28},{28,24},{1,5},{5... | collective-permute-start | bytes 196616 | tf_op jit(solution)/shard_map/ppermute | solution.py:35
  43.2 5.4 %collective-permute-start.9 = (bf16[16,2048]{1,0:T(8,128)(2,1)S(1)}, bf16[16,2048]{1,0:T(8,128)(2,1)S(1)}, u32[]{:S(2)}, u32[]{:S(2)}) collective-permute-start(bf16[16,2048]{1,0:T(8,128)(2,1)S(1)} %get-tuple-element.41), channel_id=1, source_target_pairs={{0,4},{4,0},{8,12},{12,8},{16,20},{20,16},{24,28},{28,24},{1,5},{5... | collective-permute-start | bytes 196616 | tf_op jit(solution)/shard_map/ppermute | solution.py:35
  45.1 5.8 %collective-permute-start.18 = (bf16[8,2048]{1,0:T(8,128)(2,1)S(1)}, bf16[8,2048]{1,0:T(8,128)(2,1)S(1)}, u32[]{:S(2)}, u32[]{:S(2)}) collective-permute-start(bf16[8,2048]{1,0:T(8,128)(2,1)S(1)} %get-tuple-element.49), channel_id=1, source_target_pairs={{0,24},{4,28},{8,16},{12,20},{16,8},{20,12},{24,0},{28,4},{1,25},{... | collective-permute-start | bytes 98312 | tf_op jit(solution)/shard_map/ppermute | solution.py:35
  48.7 4.9 %collective-permute-start.17 = (bf16[8,2048]{1,0:T(8,128)(2,1)S(1)}, bf16[8,2048]{1,0:T(8,128)(2,1)S(1)}, u32[]{:S(2)}, u32[]{:S(2)}) collective-permute-start(bf16[8,2048]{1,0:T(8,128)(2,1)S(1)} %get-tuple-element.48), channel_id=1, source_target_pairs={{0,16},{4,20},{8,24},{12,28},{16,0},{20,4},{24,8},{28,12},{1,17},{... | collective-permute-start | bytes 98312 | tf_op jit(solution)/shard_map/ppermute | solution.py:35
  48.7 4.9 %collective-permute-start.10 = (bf16[8,2048]{1,0:T(8,128)(2,1)S(1)}, bf16[8,2048]{1,0:T(8,128)(2,1)S(1)}, u32[]{:S(2)}, u32[]{:S(2)}) collective-permute-start(bf16[8,2048]{1,0:T(8,128)(2,1)S(1)} %get-tuple-element.43), channel_id=1, source_target_pairs={{0,8},{4,12},{8,0},{12,4},{16,24},{20,28},{24,16},{28,20},{1,9},{5... | collective-permute-start | bytes 98312 | tf_op jit(solution)/shard_map/ppermute | solution.py:35

commit v2 on v1

--- a/solution.py
+++ b/solution.py
@@ -46,7 +46,7 @@
 
 
 def half_copies(which, q_hbm, kv_hbm, new_hbm, q_ref, kv, new_ref, sems, kv_sems):
-    rows, _, span = kv.shape
+    _, _, span = kv.shape
     share = span // 2
     whole = kv_hbm.shape[2] // 2
     keys = pl.ds(pl.multiple_of(which * share, share), share)
@@ -62,16 +62,13 @@
         pltpu.make_async_copy(new_hbm.at[:, values], new_ref.at[:, share:], sems.at[2]),
     ]
     large = [
-        (
-            pltpu.make_async_copy(kv_hbm.at[r, :, keys], kv.at[r, :, :share], kv_sems.at[0, r]),
-            pltpu.make_async_copy(kv_hbm.at[r, :, values], kv.at[r, :, share:], kv_sems.at[1, r]),
-        )
-        for r in range(rows)
+        pltpu.make_async_copy(kv_hbm.at[:, :, keys], kv.at[:, :, :share], kv_sems.at[0]),
+        pltpu.make_async_copy(kv_hbm.at[:, :, values], kv.at[:, :, share:], kv_sems.at[1]),
     ]
     return small, large
 
 
-def attend_heads(q_ref, kv, new_ref, lengths, flat, mixed_flat, key_wait, value_wait, length_wait):
+def attend_heads(q_ref, kv, new_ref, lengths, flat, mixed_flat, value_wait):
     rows, cache, span = kv.shape
     share = span // 2
     kv_heads = share // HD
@@ -96,7 +93,6 @@
     all_scores = []
     for r in range(rows):
         q = asked[r].astype(jnp.bfloat16)
-        key_wait(r)
         all_scores.append(
             jnp.concatenate(
                 [
@@ -111,7 +107,6 @@
                 axis=0,
             )
         )
-    length_wait()
     probs, own_probs = [], []
     for r in range(rows):
         own = jnp.sum(asked[r] * spread(r, 0), axis=1, keepdims=True) * scaling
@@ -123,8 +118,8 @@
         scale = 1.0 / denominator
         probs.append((weights * scale).astype(jnp.bfloat16))
         own_probs.append((own_weight * scale).astype(jnp.bfloat16).astype(jnp.float32))
+    value_wait()
     for r in range(rows):
-        value_wait(r)
         mixed = jnp.concatenate(
             [
                 jnp.dot(
@@ -155,51 +150,22 @@
                 out_ref[d, :, to : to + HD] = mixed_flat[pl.ds(at, rows), :].astype(jnp.bfloat16)
 
 
-def far_kernel(
-    q_hbm, kv_hbm, new_hbm, length_hbm, out_ref, q_near, kv_near, new_near, q_ref, kv, new_ref,
-    lengths, flat, mixed_flat, sems, kv_sems, near_sems, near_kv_sems, length_sem,
+def half_kernel(
+    away, q_hbm, kv_hbm, new_hbm, length_hbm, out_ref, q_ref, kv, new_ref, lengths, flat,
+    mixed_flat, sems, kv_sems, length_sem,
 ):
     here = lax.div(lax.axis_index("side"), lax.axis_size("side") // 2)
     length_copy = pltpu.make_async_copy(length_hbm, lengths, length_sem)
     small, large = half_copies(
-        1 - here, q_hbm, kv_hbm, new_hbm, q_ref, kv, new_ref, sems, kv_sems
-    )
-    near_small, near_large = half_copies(
-        here, q_hbm, kv_hbm, new_hbm, q_near, kv_near, new_near, near_sems, near_kv_sems
-    )
-    start_all(small)
-    start_all([length_copy] + [pair[0] for pair in large])
-    start_all([pair[1] for pair in large])
-    start_all(near_small)
-    for pair in near_large:
-        start_all(pair)
-    wait_all(small)
-    attend_heads(
-        q_ref, kv, new_ref, lengths, flat, mixed_flat,
-        lambda r: large[r][0].wait(), lambda r: large[r][1].wait(), length_copy.wait,
-    )
+        jnp.bitwise_xor(here, away), q_hbm, kv_hbm, new_hbm, q_ref, kv, new_ref, sems, kv_sems
+    )
+    start_all([*small, length_copy, *large])
+    wait_all([*small, length_copy, large[0]])
+    attend_heads(q_ref, kv, new_ref, lengths, flat, mixed_flat, large[1].wait)
     put_pieces(out_ref, mixed_flat)
-    wait_all(near_small)
-    for pair in near_large:
-        wait_all(pair)
-
-
-def near_kernel(
-    q_ref, kv, new_ref, length_hbm, w_hbm, out_ref, w_ref, lengths, flat, mixed_flat, length_sem,
-    w_sem,
-):
-    length_copy = pltpu.make_async_copy(length_hbm, lengths, length_sem)
-    w_copy = pltpu.make_async_copy(w_hbm, w_ref, w_sem)
-    start_all([length_copy, w_copy])
-    nothing = lambda r: None
-    attend_heads(
-        q_ref, kv, new_ref, lengths, flat, mixed_flat, nothing, nothing, length_copy.wait
-    )
-    put_pieces(out_ref, mixed_flat)
-    w_copy.wait()
-
-
-def attend(queries, kv_cache, new_kv, lengths, w_out):
+
+
+def attend(queries, kv_cache, new_kv, lengths):
     rows, features = queries.shape
     chips = lax.axis_size("side") // 2
     q_half = pltpu.VMEM((rows, features // 2), queries.dtype)
@@ -209,32 +175,28 @@
     flat = pltpu.VMEM((rows * features // 2 // HD, HD), jnp.float32)
     smem = pltpu.SMEM(lengths.shape, lengths.dtype)
     dma = pltpu.SemaphoreType.DMA
-    queries, kv_cache, new_kv, lengths, w_out = in_hbm(queries, kv_cache, new_kv, lengths, w_out)
-    sent, q_near, kv_near, new_near = kernel_call(
-        far_kernel,
-        (queries, kv_cache, new_kv, lengths),
-        (pieces, q_half, kv_half, new_half),
-        in_specs=[HBM] * 4,
-        scratch=[
-            q_half, kv_half, new_half, smem, flat, flat,
-            dma((3,)), dma((2, rows)), dma((3,)), dma((2, rows)), dma,
-        ],
-    )
-    received = partner(sent, "side", chips)
-    kept, w_near = kernel_call(
-        near_kernel,
-        (q_near, kv_near, new_near, lengths, w_out),
-        (pieces, pltpu.VMEM(w_out.shape, w_out.dtype)),
-        in_specs=[VMEM] * 3 + [HBM] * 2,
-        scratch=[smem, flat, flat, dma, dma],
-        cost=pl.CostEstimate(flops=8 << 20, bytes_accessed=8 << 20, transcendentals=0),
-    )
+    queries, kv_cache, new_kv, lengths = in_hbm(queries, kv_cache, new_kv, lengths)
+
+    def half(away):
+        return kernel_call(
+            functools.partial(half_kernel, away),
+            (queries, kv_cache, new_kv, lengths),
+            pieces,
+            in_specs=[HBM] * 4,
+            scratch=[
+                q_half, kv_half, new_half, smem, flat, flat, dma((3,)), dma((2,)), dma,
+            ],
+            cost=pl.CostEstimate(flops=8 << 20, bytes_accessed=6 << 20, transcendentals=0),
+        )
+
+    received = partner(half(1), "side", chips)
+    kept = half(0)
     blocks = {0: kept, chips // 2: received}
     bit = chips // 4
     while bit:
         blocks.update({d ^ bit: partner(block, "side", 2 * bit) for d, block in blocks.items()})
         bit //= 2
-    return [blocks[d] for d in range(chips)], w_near
+    return [blocks[d] for d in range(chips)]
 
 
 def project_kernel(*refs):
@@ -283,7 +245,7 @@
         project_kernel,
         (
             *blocks,
-            w_near,
+            pltpu.with_memory_space_constraint(w_near, pltpu.VMEM),
             pltpu.with_memory_space_constraint(w_other, pltpu.VMEM),
             residual,
             expert_ids,
@@ -299,26 +261,6 @@
         swapped = [kept[(d ^ bit) * rows : ((d ^ bit) + 1) * rows] for d in range(chips)]
         more = partner(jnp.concatenate(swapped).astype(jnp.bfloat16), "side", 2 * bit)
     return kept, sent, more
-
-
-def fetch_kernel(after_ref, in_hbm_ref, down_hbm_ref, in_ref, down_ref, sems):
-    copies = [
-        pltpu.make_async_copy(in_hbm_ref.at[0], in_ref, sems.at[0]),
-        pltpu.make_async_copy(down_hbm_ref.at[0], down_ref, sems.at[1]),
-    ]
-    start_all(copies)
-    wait_all(copies)
-
-
-def fetch(after, w_in, w_down):
-    return kernel_call(
-        fetch_kernel,
-        (after, *in_hbm(w_in, w_down)),
-        (pltpu.VMEM(w_in.shape[1:], w_in.dtype), pltpu.VMEM(w_down.shape[1:], w_down.dtype)),
-        in_specs=[VMEM, HBM, HBM],
-        scratch=[pltpu.SemaphoreType.DMA((2,))],
-        cost=pl.CostEstimate(flops=0, bytes_accessed=8 << 20, transcendentals=0),
-    )
 
 
 def norm_kernel(total_ref, more_ref, gain_ref, normed_ref, stream_ref):
@@ -425,10 +367,14 @@
     devs = lax.axis_size("dev")
 
     w_other = partner(w_out, "side", 1)
-    blocks, w_near = attend(queries, kv_cache, new_kv, lengths, w_out)
-    total, sent, more = project(blocks, w_near, w_other, residual, expert_ids, route_level)
-    w_in, w_down = fetch(sent, w_in, w_down)
-    weights = (w_in, partner(w_in, "side", 1), w_down, partner(w_down, "side", 1))
+    in_other = partner(w_in[0], "side", 1)
+    down_other = partner(w_down[0], "side", 1)
+    blocks = attend(queries, kv_cache, new_kv, lengths)
+    total, sent, more = project(blocks, w_out, w_other, residual, expert_ids, route_level)
+    weights = [
+        pltpu.with_memory_space_constraint(x, pltpu.VMEM)
+        for x in (w_in[0], in_other, w_down[0], down_other)
+    ]
     normed, stream = kernel_call(
         norm_kernel,
         (total, more, norm_gain.reshape(1, width)),

time: 54.4 us -> 49.2 us (0.904)
  Pallas kernels: 14.6 us -> 9.85 us
  waiting for transfers between devices: 12.6 us -> 11.6 us
    pallas_call x11 -> x10, Pallas kernels: 14.6 us -> 9.85 us  [kernel_call(): pl.pallas_call(body, out_shape=outs, in_specs=in_specs or [VMEM] * len(op...]
    ppermute x19, waiting for transfers between devices: 12.6 us -> 11.6 us  [partner(): return lax.ppermute(block, axis, [(i, i ^ mask) for i in range(count)])]
where the time goes in v2:
time: 49.2 us; the launch traced here: 49.1 us
  starting transfers between devices  25.5 us (52%)
  waiting for transfers between devices  11.6 us (24%)
  Pallas kernels  9.85 us (20%)
  between operations  0.78 us (2%)
  local copies, waits for them, and re-layouts  0.65 us (1%)
  other arithmetic  0.63 us (1%)
    ppermute x19, starting transfers between devices, partner(): return lax.ppermute(block, axis, [(i, i ^ mask) for i in range(count)])  25.5 us
    ppermute x19, waiting for transfers between devices, partner(): return lax.ppermute(block, axis, [(i, i ^ mask) for i in range(count)])  11.6 us
    pallas_call x10, Pallas kernels, kernel_call(): pl.pallas_call(body, out_shape=outs, in_specs=in_specs or [VMEM] * len(op...  9.85 us
  transfers between devices with their start and end apart: 19, of which 9 were waited for; matrix products, arithmetic and copies ran while one was open for 1% of the time, Pallas kernels for 20%

profile of v2, /device:TPU:0, one launch (start us, length us, event | category | flops | bytes accessed | tf_op | source)
XLA Modules:
  0.0 49.1 jit_solution(744765820183687351)
XLA Ops:
  0.6 0.6 %collective-permute-start.1 = (bf16[1024,2048]{1,0:T(8,128)(2,1)}, bf16[1024,2048]{1,0:T(8,128)(2,1)S(1)}, u32[]{:S(2)}, u32[]{:S(2)}) collective-permute-start(bf16[1024,2048]{1,0:T(8,128)(2,1)} %refs_2_.1), channel_id=1, source_target_pairs={{0,1},{1,0},{2,3},{3,2},{4,5},{5,4},{6,7},{7,6},{8,9},{9,8},{10,11... | collective-permute-start | bytes 12582920 | tf_op jit(solution)/shard_map/ppermute | solution.py:35
  1.2 0.1 collective-permute-start.6
  1.3 0.0 copy-start.2
  1.3 0.0 copy-start.3
  1.3 0.0 copy-start.5
  1.3 0.0 copy-start.6
  1.3 0.5 %collective-permute-start.7 = (bf16[384,2048]{1,0:T(8,128)(2,1)}, bf16[384,2048]{1,0:T(8,128)(2,1)S(1)}, u32[]{:S(2)}, u32[]{:S(2)}) collective-permute-start(bf16[384,2048]{1,0:T(8,128)(2,1)} %bitcast.6), channel_id=1, source_target_pairs={{0,1},{1,0},{2,3},{3,2},{4,5},{5,4},{6,7},{7,6},{8,9},{9,8},{10,11... | collective-permute-start | bytes 4718600 | tf_op jit(solution)/shard_map/ppermute | solution.py:35
  1.8 2.5 %shard_map.123 = bf16[1,8,2048]{2,1,0:T(8,128)(2,1)S(1)} custom-call(bf16[8,4096]{1,0:T(8,128)(2,1)} %q_hbm.3, bf16[8,192,1024]{2,1,0:T(8,128)(2,1)} %kv_hbm.3, bf16[8,1024]{1,0:T(8,128)(2,1)} %new_hbm.3, s32[8]{0:T(128)} %length_hbm.3), custom_call_target="tpu_custom_call" | custom-call | flops 8388608 | bytes 6291456 | tf_op jit(solution)/shard_map/pallas_call | solution.py:18
  4.3 2.5 %collective-permute-start = (bf16[1,8,2048]{2,1,0:T(8,128)(2,1)S(1)}, bf16[1,8,2048]{2,1,0:T(8,128)(2,1)S(1)}, u32[]{:S(2)}, u32[]{:S(2)}) collective-permute-start(bf16[1,8,2048]{2,1,0:T(8,128)(2,1)S(1)} %shard_map.123), channel_id=1, source_target_pairs={{0,2},{1,3},{2,0},{3,1},{4,6},{5,7},{6,4},{7,5},{8,10},{9,11},{10,... | collective-permute-start | bytes 98312 | tf_op jit(solution)/shard_map/ppermute | solution.py:35
  6.8 2.2 %shard_map.122.refs_0_ = bf16[1,8,2048]{2,1,0:T(8,128)(2,1)S(1)} custom-call(bf16[8,4096]{1,0:T(8,128)(2,1)} %q_hbm.3, bf16[8,192,1024]{2,1,0:T(8,128)(2,1)} %kv_hbm.3, bf16[8,1024]{1,0:T(8,128)(2,1)} %new_hbm.3, s32[8]{0:T(128)} %length_hbm.3), custom_call_target="tpu_custom_call" | custom-call | flops 8388608 | bytes 6291456 | tf_op jit(solution)/shard_map/pallas_call | solution.py:18
  9.1 0.0 copy-start.4
  9.1 0.0 copy-start
  9.1 0.0 copy-start.1
  9.1 0.0 collective-permute-done.refs_1_
  9.1 0.0 collective-permute-done.1.refs_3_
  9.1 0.0 copy-done.2
  9.1 0.0 copy-done.3
  9.1 0.0 copy-done.5
  9.1 0.0 copy-done.6
  9.2 1.2 %shard_map.124 = (f32[16,2176]{1,0:T(8,128)S(1)}, bf16[16,2176]{1,0:T(8,128)(2,1)S(1)}) custom-call(bf16[1,8,2048]{2,1,0:T(8,128)(2,1)S(1)} %shard_map.122.refs_0_, bf16[1,8,2048]{2,1,0:T(8,128)(2,1)S(1)} %collective-permute-done.refs_1_, bf16[1024,2048]{1,0:T(8,128)(2,1)S(1)} %copy-done.2, bf16[1024,2048]{1,0:T(8,128)(2,1)S(1)} %collective-permute-done.1.refs_3_, ...), custom_call_target="tpu_custom_call" | custom-call | tf_op jit(solution)/shard_map/pallas_call | solution.py:18
  10.4 1.9 %collective-permute-start.2 = (bf16[16,2176]{1,0:T(8,128)(2,1)S(1)}, bf16[16,2176]{1,0:T(8,128)(2,1)S(1)}, u32[]{:S(2)}, u32[]{:S(2)}) collective-permute-start(bf16[16,2176]{1,0:T(8,128)(2,1)S(1)} %get-tuple-element.19), channel_id=1, source_target_pairs={{0,2},{1,3},{2,0},{3,1},{4,6},{5,7},{6,4},{7,5},{8,10},{9,11},{10,... | collective-permute-start | bytes 208904 | tf_op jit(solution)/shard_map/ppermute | solution.py:35
  12.3 2.5 %collective-permute-done.2.more_ref = bf16[16,2176]{1,0:T(8,128)(2,1)S(1)} collective-permute-done((bf16[16,2176]{1,0:T(8,128)(2,1)S(1)}, bf16[16,2176]{1,0:T(8,128)(2,1)S(1)}, u32[]{:S(2)}, u32[]{:S(2)}) %collective-permute-start.2) | collective-permute-done | bytes 69664 | tf_op jit(solution)/shard_map/ppermute | solution.py:35
  14.7 0.0 copy-done.4
  14.7 0.1 shard_map.125
  14.9 3.0 %collective-permute-start.11 = (bf16[16,2176]{1,0:T(8,128)(2,1)S(1)}, bf16[16,2176]{1,0:T(8,128)(2,1)S(1)}, u32[]{:S(2)}, u32[]{:S(2)}) collective-permute-start(bf16[16,2176]{1,0:T(8,128)(2,1)S(1)} %get-tuple-element.21.refs_0_), channel_id=1, source_target_pairs={{0,16},{4,20},{8,24},{12,28},{16,0},{20,4},{24,8},{28,12},{1,17},{... | collective-permute-start | bytes 208904 | tf_op jit(solution)/shard_map/ppermute | solution.py:35
  17.9 1.3 %collective-permute-start.12 = (bf16[16,2176]{1,0:T(8,128)(2,1)S(1)}, bf16[16,2176]{1,0:T(8,128)(2,1)S(1)}, u32[]{:S(2)}, u32[]{:S(2)}) collective-permute-start(bf16[16,2176]{1,0:T(8,128)(2,1)S(1)} %get-tuple-element.21.refs_0_), channel_id=1, source_target_pairs={{0,24},{4,28},{8,16},{12,20},{16,8},{20,12},{24,0},{28,4},{1,25},{... | collective-permute-start | bytes 208904 | tf_op jit(solution)/shard_map/ppermute | solution.py:35
  19.2 0.2 collective-permute-start.3
  19.4 0.9 %collective-permute-done.11.refs_0_ = bf16[16,2176]{1,0:T(8,128)(2,1)S(1)} collective-permute-done((bf16[16,2176]{1,0:T(8,128)(2,1)S(1)}, bf16[16,2176]{1,0:T(8,128)(2,1)S(1)}, u32[]{:S(2)}, u32[]{:S(2)}) %collective-permute-start.11) | collective-permute-done | bytes 69664 | tf_op jit(solution)/shard_map/ppermute | solution.py:35
  20.3 2.0 %collective-permute-start.13 = (bf16[16,2176]{1,0:T(8,128)(2,1)S(1)}, bf16[16,2176]{1,0:T(8,128)(2,1)S(1)}, u32[]{:S(2)}, u32[]{:S(2)}) collective-permute-start(bf16[16,2176]{1,0:T(8,128)(2,1)S(1)} %collective-permute-done.11.refs_0_), channel_id=1, source_target_pairs={{0,4},{4,0},{8,12},{12,8},{16,20},{20,16},{24,28},{28,24},{1,5},{5... | collective-permute-start | bytes 208904 | tf_op jit(solution)/shard_map/ppermute | solution.py:35
  22.3 1.7 %collective-permute-done.12.refs_1_ = bf16[16,2176]{1,0:T(8,128)(2,1)S(1)} collective-permute-done((bf16[16,2176]{1,0:T(8,128)(2,1)S(1)}, bf16[16,2176]{1,0:T(8,128)(2,1)S(1)}, u32[]{:S(2)}, u32[]{:S(2)}) %collective-permute-start.12) | collective-permute-done | bytes 69664 | tf_op jit(solution)/shard_map/ppermute | solution.py:35
  24.1 1.5 %collective-permute-start.14 = (bf16[16,2176]{1,0:T(8,128)(2,1)S(1)}, bf16[16,2176]{1,0:T(8,128)(2,1)S(1)}, u32[]{:S(2)}, u32[]{:S(2)}) collective-permute-start(bf16[16,2176]{1,0:T(8,128)(2,1)S(1)} %collective-permute-done.12.refs_1_), channel_id=1, source_target_pairs={{0,4},{4,0},{8,12},{12,8},{16,20},{20,16},{24,28},{28,24},{1,5},{5... | collective-permute-start | bytes 208904 | tf_op jit(solution)/shard_map/ppermute | solution.py:35
  25.6 0.0 collective-permute-done.7.refs_7_
  25.6 0.5 %collective-permute-start.4 = (bf16[16,2176]{1,0:T(8,128)(2,1)S(1)}, bf16[16,2176]{1,0:T(8,128)(2,1)S(1)}, u32[]{:S(2)}, u32[]{:S(2)}) collective-permute-start(bf16[16,2176]{1,0:T(8,128)(2,1)S(1)} %get-tuple-element.21.refs_0_), channel_id=1, source_target_pairs={{0,4},{4,0},{8,12},{12,8},{16,20},{20,16},{24,28},{28,24},{1,5},{5... | collective-permute-start | bytes 208904 | tf_op jit(solution)/shard_map/ppermute | solution.py:35
  26.1 0.0 collective-permute-done.3.refs_1_
  26.1 1.5 %collective-permute-start.5 = (bf16[16,2176]{1,0:T(8,128)(2,1)S(1)}, bf16[16,2176]{1,0:T(8,128)(2,1)S(1)}, u32[]{:S(2)}, u32[]{:S(2)}) collective-permute-start(bf16[16,2176]{1,0:T(8,128)(2,1)S(1)} %collective-permute-done.3.refs_1_), channel_id=1, source_target_pairs={{0,4},{4,0},{8,12},{12,8},{16,20},{20,16},{24,28},{28,24},{1,5},{5... | collective-permute-start | bytes 208904 | tf_op jit(solution)/shard_map/ppermute | solution.py:35
  27.6 0.0 collective-permute-done.6.refs_5_
  27.6 0.0 collective-permute-done.13.refs_2_
  27.6 0.8 %collective-permute-done.14.refs_3_ = bf16[16,2176]{1,0:T(8,128)(2,1)S(1)} collective-permute-done((bf16[16,2176]{1,0:T(8,128)(2,1)S(1)}, bf16[16,2176]{1,0:T(8,128)(2,1)S(1)}, u32[]{:S(2)}, u32[]{:S(2)}) %collective-permute-start.14) | collective-permute-done | bytes 69664 | tf_op jit(solution)/shard_map/ppermute | solution.py:35
  28.4 0.0 copy-done
  28.4 0.0 copy-done.1
  28.4 1.9 %shard_map.129 = (f32[32,2048]{1,0:T(8,128)S(1)}, bf16[32,2048]{1,0:T(8,128)(2,1)S(1)}) custom-call(bf16[16,2176]{1,0:T(8,128)(2,1)S(1)} %collective-permute-done.11.refs_0_, bf16[16,2176]{1,0:T(8,128)(2,1)S(1)} %collective-permute-done.12.refs_1_, bf16[16,2176]{1,0:T(8,128)(2,1)S(1)} %collective-permute-done.13.refs_2_, ...), custom_call_target="tpu_custom_call" | custom-call | flops 1073741824 | bytes 4194304 | tf_op jit(solution)/shard_map/pallas_call | solution.py:18
  30.3 1.6 %collective-permute-start.15 = (bf16[32,2048]{1,0:T(8,128)(2,1)S(1)}, bf16[32,2048]{1,0:T(8,128)(2,1)S(1)}, u32[]{:S(2)}, u32[]{:S(2)}) collective-permute-start(bf16[32,2048]{1,0:T(8,128)(2,1)S(1)} %get-tuple-element.29), channel_id=1, source_target_pairs={{0,2},{1,3},{2,0},{3,1},{4,6},{5,7},{6,4},{7,5},{8,10},{9,11},{10,... | collective-permute-start | bytes 393224 | tf_op jit(solution)/shard_map/ppermute | solution.py:35
  31.8 0.0 collective-permute-done.4.refs_2_
  31.8 0.0 collective-permute-done.5.refs_3_
  31.8 1.8 %shard_map.126 = (f32[32,2048]{1,0:T(8,128)S(1)}, bf16[32,2048]{1,0:T(8,128)(2,1)S(1)}) custom-call(bf16[16,2176]{1,0:T(8,128)(2,1)S(1)} %get-tuple-element.21.refs_0_, bf16[16,2176]{1,0:T(8,128)(2,1)S(1)} %collective-permute-done.3.refs_1_, bf16[16,2176]{1,0:T(8,128)(2,1)S(1)} %collective-permute-done.4.refs_2_, ...), custom_call_target="tpu_custom_call" | custom-call | flops 1073741824 | bytes 4194304 | tf_op jit(solution)/shard_map/pallas_call | solution.py:18
  33.7 0.6 %collective-permute-start.8 = (bf16[32,2048]{1,0:T(8,128)(2,1)S(1)}, bf16[32,2048]{1,0:T(8,128)(2,1)S(1)}, u32[]{:S(2)}, u32[]{:S(2)}) collective-permute-start(bf16[32,2048]{1,0:T(8,128)(2,1)S(1)} %get-tuple-element.23), channel_id=1, source_target_pairs={{0,2},{1,3},{2,0},{3,1},{4,6},{5,7},{6,4},{7,5},{8,10},{9,11},{10,... | collective-permute-start | bytes 393224 | tf_op jit(solution)/shard_map/ppermute | solution.py:35
  34.3 1.9 %collective-permute-done.15.more_ref = bf16[32,2048]{1,0:T(8,128)(2,1)S(1)} collective-permute-done((bf16[32,2048]{1,0:T(8,128)(2,1)S(1)}, bf16[32,2048]{1,0:T(8,128)(2,1)S(1)}, u32[]{:S(2)}, u32[]{:S(2)}) %collective-permute-start.15) | collective-permute-done | bytes 131104 | tf_op jit(solution)/shard_map/ppermute | solution.py:35
  36.2 1.6 %collective-permute-start.16 = (bf16[16,2048]{1,0:T(8,128)(2,1)S(1)}, bf16[16,2048]{1,0:T(8,128)(2,1)S(1)}, u32[]{:S(2)}, u32[]{:S(2)}) collective-permute-start(bf16[16,2048]{1,0:T(8,128)(2,1)S(1)} %get-tuple-element.31), channel_id=1, source_target_pairs={{0,4},{4,0},{8,12},{12,8},{16,20},{20,16},{24,28},{28,24},{1,5},{5... | collective-permute-start | bytes 196616 | tf_op jit(solution)/shard_map/ppermute | solution.py:35
  37.8 0.9 %collective-permute-done.8.more_ref = bf16[32,2048]{1,0:T(8,128)(2,1)S(1)} collective-permute-done((bf16[32,2048]{1,0:T(8,128)(2,1)S(1)}, bf16[32,2048]{1,0:T(8,128)(2,1)S(1)}, u32[]{:S(2)}, u32[]{:S(2)}) %collective-permute-start.8) | collective-permute-done | bytes 131104 | tf_op jit(solution)/shard_map/ppermute | solution.py:35
  38.7 1.6 %collective-permute-start.9 = (bf16[16,2048]{1,0:T(8,128)(2,1)S(1)}, bf16[16,2048]{1,0:T(8,128)(2,1)S(1)}, u32[]{:S(2)}, u32[]{:S(2)}) collective-permute-start(bf16[16,2048]{1,0:T(8,128)(2,1)S(1)} %get-tuple-element.25), channel_id=1, source_target_pairs={{0,4},{4,0},{8,12},{12,8},{16,20},{20,16},{24,28},{28,24},{1,5},{5... | collective-permute-start | bytes 196616 | tf_op jit(solution)/shard_map/ppermute | solution.py:35
  40.3 0.2 collective-permute-done.16.more_ref
  40.5 3.0 %collective-permute-start.18 = (bf16[8,2048]{1,0:T(8,128)(2,1)S(1)}, bf16[8,2048]{1,0:T(8,128)(2,1)S(1)}, u32[]{:S(2)}, u32[]{:S(2)}) collective-permute-start(bf16[8,2048]{1,0:T(8,128)(2,1)S(1)} %get-tuple-element.33), channel_id=1, source_target_pairs={{0,24},{4,28},{8,16},{12,20},{16,8},{20,12},{24,0},{28,4},{1,25},{... | collective-permute-start | bytes 98312 | tf_op jit(solution)/shard_map/ppermute | solution.py:35
  43.6 0.5 %collective-permute-start.17 = (bf16[8,2048]{1,0:T(8,128)(2,1)S(1)}, bf16[8,2048]{1,0:T(8,128)(2,1)S(1)}, u32[]{:S(2)}, u32[]{:S(2)}) collective-permute-start(bf16[8,2048]{1,0:T(8,128)(2,1)S(1)} %get-tuple-element.32), channel_id=1, source_target_pairs={{0,16},{4,20},{8,24},{12,28},{16,0},{20,4},{24,8},{28,12},{1,17},{... | collective-permute-start | bytes 98312 | tf_op jit(solution)/shard_map/ppermute | solution.py:35
  44.1 0.0 collective-permute-done.9.more_ref
  44.1 1.0 %collective-permute-start.10 = (bf16[8,2048]{1,0:T(8,128)(2,1)S(1)}, bf16[8,2048]{1,0:T(8,128)(2,1)S(1)}, u32[]{:S(2)}, u32[]{:S(2)}) collective-permute-start(bf16[8,2048]{1,0:T(8,128)(2,1)S(1)} %get-tuple-element.27), channel_id=1, source_target_pairs={{0,8},{4,12},{8,0},{12,4},{16,24},{20,28},{24,16},{28,20},{1,9},{5... | collective-permute-start | bytes 98312 | tf_op jit(solution)/shard_map/ppermute | solution.py:35
  45.1 0.6 %copy.13 = bf16[8,2048]{1,0:T(8,128)(2,1)} copy(bf16[8,2048]{1,0:T(8,128)(2,1)S(1)} %get-tuple-element.34) | data formatting | bytes 65536
  45.7 0.6 %collective-permute-done.18 = bf16[8,2048]{1,0:T(8,128)(2,1)S(1)} collective-permute-done((bf16[8,2048]{1,0:T(8,128)(2,1)S(1)}, bf16[8,2048]{1,0:T(8,128)(2,1)S(1)}, u32[]{:S(2)}, u32[]{:S(2)}) %collective-permute-start.18) | collective-permute-done | bytes 32800 | tf_op jit(solution)/shard_map/ppermute | solution.py:35
  46.3 2.1 %collective-permute-done.17 = bf16[8,2048]{1,0:T(8,128)(2,1)S(1)} collective-permute-done((bf16[8,2048]{1,0:T(8,128)(2,1)S(1)}, bf16[8,2048]{1,0:T(8,128)(2,1)S(1)}, u32[]{:S(2)}, u32[]{:S(2)}) %collective-permute-start.17) | collective-permute-done | bytes 32800 | tf_op jit(solution)/shard_map/ppermute | solution.py:35
  48.4 0.0 collective-permute-done.10
  48.4 0.6 %add_convert_fusion = bf16[8,2048]{1,0:T(8,128)(2,1)} fusion(bf16[8,2048]{1,0:T(8,128)(2,1)S(1)} %collective-permute-done.18, bf16[8,2048]{1,0:T(8,128)(2,1)S(1)} %collective-permute-done.17, f32[8,2048]{1,0:T(8,128)S(1)} %get-tuple-element.26, bf16[8,2048]{1,0:T(8,128)(2,1)S(1)} %collective-permute-done.10), kind=kLoop, calls=%fused_computation | loop fusion | flops 114688 | bytes 196608 | tf_op jit(solution)/shard_map/convert_element_type | solution.py:401
  (4 shorter events, 0.1 us)
Async XLA Ops:
  0.6 8.5 %collective-permute-start.1 = (bf16[1024,2048]{1,0:T(8,128)(2,1)}, bf16[1024,2048]{1,0:T(8,128)(2,1)S(1)}, u32[]{:S(2)}, u32[]{:S(2)}) collective-permute-start(bf16[1024,2048]{1,0:T(8,128)(2,1)} %refs_2_.1), channel_id=1, source_target_pairs={{0,1},{1,0},{2,3},{3,2},{4,5},{5,4},{6,7},{7,6},{8,9},{9,8},{10,11... | collective-permute-start | bytes 12582920 | tf_op jit(solution)/shard_map/ppermute | solution.py:35
  1.2 26.4 %collective-permute-start.6 = (bf16[2048,768]{1,0:T(8,128)(2,1)}, bf16[2048,768]{1,0:T(8,128)(2,1)S(1)}, u32[]{:S(2)}, u32[]{:S(2)}) collective-permute-start(bf16[2048,768]{1,0:T(8,128)(2,1)} %bitcast.3), channel_id=1, source_target_pairs={{0,1},{1,0},{2,3},{3,2},{4,5},{5,4},{6,7},{7,6},{8,9},{9,8},{10,11... | collective-permute-start | bytes 9437192 | tf_op jit(solution)/shard_map/ppermute | solution.py:35
  1.3 7.8 %copy-start.2 = (bf16[1024,2048]{1,0:T(8,128)(2,1)S(1)}, bf16[1024,2048]{1,0:T(8,128)(2,1)}, u32[]{:S(2)}) copy-start(bf16[1024,2048]{1,0:T(8,128)(2,1)} %refs_2_.1) | copy-start | bytes 12582916
  1.3 7.9 %copy-start.3 = (bf16[8,2048]{1,0:T(8,128)(2,1)S(1)}, bf16[8,2048]{1,0:T(8,128)(2,1)}, u32[]{:S(2)}) copy-start(bf16[8,2048]{1,0:T(8,128)(2,1)} %refs_4_.1) | copy-start | bytes 98308
  1.3 7.9 %copy-start.5 = (s32[8,8]{1,0:T(8,128)S(1)}, s32[8,8]{1,0:T(8,128)}, u32[]{:S(2)}) copy-start(s32[8,8]{1,0:T(8,128)} %refs_5_.1) | copy-start | bytes 772
  1.3 7.9 %copy-start.6 = (s32[8,8]{1,0:T(8,128)S(1)}, s32[8,8]{1,0:T(8,128)}, u32[]{:S(2)}) copy-start(s32[8,8]{1,0:T(8,128)} %refs_6_.1) | copy-start | bytes 772
  1.3 24.3 %collective-permute-start.7 = (bf16[384,2048]{1,0:T(8,128)(2,1)}, bf16[384,2048]{1,0:T(8,128)(2,1)S(1)}, u32[]{:S(2)}, u32[]{:S(2)}) collective-permute-start(bf16[384,2048]{1,0:T(8,128)(2,1)} %bitcast.6), channel_id=1, source_target_pairs={{0,1},{1,0},{2,3},{3,2},{4,5},{5,4},{6,7},{7,6},{8,9},{9,8},{10,11... | collective-permute-start | bytes 4718600 | tf_op jit(solution)/shard_map/ppermute | solution.py:35
  4.3 4.8 %collective-permute-start = (bf16[1,8,2048]{2,1,0:T(8,128)(2,1)S(1)}, bf16[1,8,2048]{2,1,0:T(8,128)(2,1)S(1)}, u32[]{:S(2)}, u32[]{:S(2)}) collective-permute-start(bf16[1,8,2048]{2,1,0:T(8,128)(2,1)S(1)} %shard_map.123), channel_id=1, source_target_pairs={{0,2},{1,3},{2,0},{3,1},{4,6},{5,7},{6,4},{7,5},{8,10},{9,11},{10,... | collective-permute-start | bytes 98312 | tf_op jit(solution)/shard_map/ppermute | solution.py:35
  9.1 5.7 %copy-start.4 = (f32[2048]{0:T(1024)S(1)}, f32[2048]{0:T(1024)}, u32[]{:S(2)}) copy-start(f32[2048]{0:T(1024)} %param.17) | copy-start | bytes 24580
  9.1 19.3 %copy-start = (bf16[1,2048,768]{2,1,0:T(8,128)(2,1)S(1)}, bf16[1,2048,768]{2,1,0:T(8,128)(2,1)}, u32[]{:S(2)}) copy-start(bf16[1,2048,768]{2,1,0:T(8,128)(2,1)} %param.20) | copy-start | bytes 9437188
  9.1 19.3 %copy-start.1 = (bf16[1,384,2048]{2,1,0:T(8,128)(2,1)S(1)}, bf16[1,384,2048]{2,1,0:T(8,128)(2,1)}, u32[]{:S(2)}) copy-start(bf16[1,384,2048]{2,1,0:T(8,128)(2,1)} %param.21) | copy-start | bytes 4718596
  10.4 4.4 %collective-permute-start.2 = (bf16[16,2176]{1,0:T(8,128)(2,1)S(1)}, bf16[16,2176]{1,0:T(8,128)(2,1)S(1)}, u32[]{:S(2)}, u32[]{:S(2)}) collective-permute-start(bf16[16,2176]{1,0:T(8,128)(2,1)S(1)} %get-tuple-element.19), channel_id=1, source_target_pairs={{0,2},{1,3},{2,0},{3,1},{4,6},{5,7},{6,4},{7,5},{8,10},{9,11},{10,... | collective-permute-start | bytes 208904 | tf_op jit(solution)/shard_map/ppermute | solution.py:35
  14.9 5.5 %collective-permute-start.11 = (bf16[16,2176]{1,0:T(8,128)(2,1)S(1)}, bf16[16,2176]{1,0:T(8,128)(2,1)S(1)}, u32[]{:S(2)}, u32[]{:S(2)}) collective-permute-start(bf16[16,2176]{1,0:T(8,128)(2,1)S(1)} %get-tuple-element.21.refs_0_), channel_id=1, source_target_pairs={{0,16},{4,20},{8,24},{12,28},{16,0},{20,4},{24,8},{28,12},{1,17},{... | collective-permute-start | bytes 208904 | tf_op jit(solution)/shard_map/ppermute | solution.py:35
  17.9 6.2 %collective-permute-start.12 = (bf16[16,2176]{1,0:T(8,128)(2,1)S(1)}, bf16[16,2176]{1,0:T(8,128)(2,1)S(1)}, u32[]{:S(2)}, u32[]{:S(2)}) collective-permute-start(bf16[16,2176]{1,0:T(8,128)(2,1)S(1)} %get-tuple-element.21.refs_0_), channel_id=1, source_target_pairs={{0,24},{4,28},{8,16},{12,20},{16,8},{20,12},{24,0},{28,4},{1,25},{... | collective-permute-start | bytes 208904 | tf_op jit(solution)/shard_map/ppermute | solution.py:35
  19.2 6.9 %collective-permute-start.3 = (bf16[16,2176]{1,0:T(8,128)(2,1)S(1)}, bf16[16,2176]{1,0:T(8,128)(2,1)S(1)}, u32[]{:S(2)}, u32[]{:S(2)}) collective-permute-start(bf16[16,2176]{1,0:T(8,128)(2,1)S(1)} %get-tuple-element.21.refs_0_), channel_id=1, source_target_pairs={{0,8},{4,12},{8,0},{12,4},{16,24},{20,28},{24,16},{28,20},{1,9},{5... | collective-permute-start | bytes 208904 | tf_op jit(solution)/shard_map/ppermute | solution.py:35
  20.3 7.3 %collective-permute-start.13 = (bf16[16,2176]{1,0:T(8,128)(2,1)S(1)}, bf16[16,2176]{1,0:T(8,128)(2,1)S(1)}, u32[]{:S(2)}, u32[]{:S(2)}) collective-permute-start(bf16[16,2176]{1,0:T(8,128)(2,1)S(1)} %collective-permute-done.11.refs_0_), channel_id=1, source_target_pairs={{0,4},{4,0},{8,12},{12,8},{16,20},{20,16},{24,28},{28,24},{1,5},{5... | collective-permute-start | bytes 208904 | tf_op jit(solution)/shard_map/ppermute | solution.py:35
  24.1 4.3 %collective-permute-start.14 = (bf16[16,2176]{1,0:T(8,128)(2,1)S(1)}, bf16[16,2176]{1,0:T(8,128)(2,1)S(1)}, u32[]{:S(2)}, u32[]{:S(2)}) collective-permute-start(bf16[16,2176]{1,0:T(8,128)(2,1)S(1)} %collective-permute-done.12.refs_1_), channel_id=1, source_target_pairs={{0,4},{4,0},{8,12},{12,8},{16,20},{20,16},{24,28},{28,24},{1,5},{5... | collective-permute-start | bytes 208904 | tf_op jit(solution)/shard_map/ppermute | solution.py:35
  25.6 6.2 %collective-permute-start.4 = (bf16[16,2176]{1,0:T(8,128)(2,1)S(1)}, bf16[16,2176]{1,0:T(8,128)(2,1)S(1)}, u32[]{:S(2)}, u32[]{:S(2)}) collective-permute-start(bf16[16,2176]{1,0:T(8,128)(2,1)S(1)} %get-tuple-element.21.refs_0_), channel_id=1, source_target_pairs={{0,4},{4,0},{8,12},{12,8},{16,20},{20,16},{24,28},{28,24},{1,5},{5... | collective-permute-start | bytes 208904 | tf_op jit(solution)/shard_map/ppermute | solution.py:35
  26.1 5.7 %collective-permute-start.5 = (bf16[16,2176]{1,0:T(8,128)(2,1)S(1)}, bf16[16,2176]{1,0:T(8,128)(2,1)S(1)}, u32[]{:S(2)}, u32[]{:S(2)}) collective-permute-start(bf16[16,2176]{1,0:T(8,128)(2,1)S(1)} %collective-permute-done.3.refs_1_), channel_id=1, source_target_pairs={{0,4},{4,0},{8,12},{12,8},{16,20},{20,16},{24,28},{28,24},{1,5},{5... | collective-permute-start | bytes 208904 | tf_op jit(solution)/shard_map/ppermute | solution.py:35
  30.3 5.9 %collective-permute-start.15 = (bf16[32,2048]{1,0:T(8,128)(2,1)S(1)}, bf16[32,2048]{1,0:T(8,128)(2,1)S(1)}, u32[]{:S(2)}, u32[]{:S(2)}) collective-permute-start(bf16[32,2048]{1,0:T(8,128)(2,1)S(1)} %get-tuple-element.29), channel_id=1, source_target_pairs={{0,2},{1,3},{2,0},{3,1},{4,6},{5,7},{6,4},{7,5},{8,10},{9,11},{10,... | collective-permute-start | bytes 393224 | tf_op jit(solution)/shard_map/ppermute | solution.py:35
  33.7 5.0 %collective-permute-start.8 = (bf16[32,2048]{1,0:T(8,128)(2,1)S(1)}, bf16[32,2048]{1,0:T(8,128)(2,1)S(1)}, u32[]{:S(2)}, u32[]{:S(2)}) collective-permute-start(bf16[32,2048]{1,0:T(8,128)(2,1)S(1)} %get-tuple-element.23), channel_id=1, source_target_pairs={{0,2},{1,3},{2,0},{3,1},{4,6},{5,7},{6,4},{7,5},{8,10},{9,11},{10,... | collective-permute-start | bytes 393224 | tf_op jit(solution)/shard_map/ppermute | solution.py:35
  36.2 4.3 %collective-permute-start.16 = (bf16[16,2048]{1,0:T(8,128)(2,1)S(1)}, bf16[16,2048]{1,0:T(8,128)(2,1)S(1)}, u32[]{:S(2)}, u32[]{:S(2)}) collective-permute-start(bf16[16,2048]{1,0:T(8,128)(2,1)S(1)} %get-tuple-element.31), channel_id=1, source_target_pairs={{0,4},{4,0},{8,12},{12,8},{16,20},{20,16},{24,28},{28,24},{1,5},{5... | collective-permute-start | bytes 196616 | tf_op jit(solution)/shard_map/ppermute | solution.py:35
  38.7 5.3 %collective-permute-start.9 = (bf16[16,2048]{1,0:T(8,128)(2,1)S(1)}, bf16[16,2048]{1,0:T(8,128)(2,1)S(1)}, u32[]{:S(2)}, u32[]{:S(2)}) collective-permute-start(bf16[16,2048]{1,0:T(8,128)(2,1)S(1)} %get-tuple-element.25), channel_id=1, source_target_pairs={{0,4},{4,0},{8,12},{12,8},{16,20},{20,16},{24,28},{28,24},{1,5},{5... | collective-permute-start | bytes 196616 | tf_op jit(solution)/shard_map/ppermute | solution.py:35
  40.5 5.8 %collective-permute-start.18 = (bf16[8,2048]{1,0:T(8,128)(2,1)S(1)}, bf16[8,2048]{1,0:T(8,128)(2,1)S(1)}, u32[]{:S(2)}, u32[]{:S(2)}) collective-permute-start(bf16[8,2048]{1,0:T(8,128)(2,1)S(1)} %get-tuple-element.33), channel_id=1, source_target_pairs={{0,24},{4,28},{8,16},{12,20},{16,8},{20,12},{24,0},{28,4},{1,25},{... | collective-permute-start | bytes 98312 | tf_op jit(solution)/shard_map/ppermute | solution.py:35
  43.6 4.9 %collective-permute-start.17 = (bf16[8,2048]{1,0:T(8,128)(2,1)S(1)}, bf16[8,2048]{1,0:T(8,128)(2,1)S(1)}, u32[]{:S(2)}, u32[]{:S(2)}) collective-permute-start(bf16[8,2048]{1,0:T(8,128)(2,1)S(1)} %get-tuple-element.32), channel_id=1, source_target_pairs={{0,16},{4,20},{8,24},{12,28},{16,0},{20,4},{24,8},{28,12},{1,17},{... | collective-permute-start | bytes 98312 | tf_op jit(solution)/shard_map/ppermute | solution.py:35
  44.1 4.3 %collective-permute-start.10 = (bf16[8,2048]{1,0:T(8,128)(2,1)S(1)}, bf16[8,2048]{1,0:T(8,128)(2,1)S(1)}, u32[]{:S(2)}, u32[]{:S(2)}) collective-permute-start(bf16[8,2048]{1,0:T(8,128)(2,1)S(1)} %get-tuple-element.27), channel_id=1, source_target_pairs={{0,8},{4,12},{8,0},{12,4},{16,24},{20,28},{24,16},{28,20},{1,9},{5... | collective-permute-start | bytes 98312 | tf_op jit(solution)/shard_map/ppermute | solution.py:35

commit v3 on v2

--- a/solution.py
+++ b/solution.py
@@ -33,6 +33,13 @@
 def partner(block, axis, mask):
     count = lax.axis_size(axis)
     return lax.ppermute(block, axis, [(i, i ^ mask) for i in range(count)])
+
+
+def across(block, over_dev, over_side):
+    side = lax.axis_size("side")
+    mask = over_dev * side + 2 * over_side + 1
+    count = lax.axis_size("dev") * side
+    return lax.ppermute(block, ("dev", "side"), [(i, i ^ mask) for i in range(count)])
 
 
 def start_all(copies):
@@ -134,7 +141,7 @@
         mixed_flat[pl.ds(r, heads, stride=rows), :] = mixed + own_probs[r] * spread(r, share)
 
 
-def put_pieces(out_ref, mixed_flat):
+def put_pieces(out_ref, mixed_flat, away):
     pieces, rows, columns = out_ref.shape
     heads = columns // HD // 2
     mine = lax.axis_index("side")
@@ -143,7 +150,8 @@
     for d in range(pieces):
         chip = jnp.bitwise_xor(low, d)
         for other in range(2):
-            first = (2 * chip + jnp.bitwise_xor(core, other)) * heads
+            flips = (other + away + d.bit_count()) % 2
+            first = (2 * chip + jnp.bitwise_xor(core, flips)) * heads
             for h in range(heads):
                 at = pl.multiple_of((first + h) * rows, rows)
                 to = (other * heads + h) * HD
@@ -162,7 +170,7 @@
     start_all([*small, length_copy, *large])
     wait_all([*small, length_copy, large[0]])
     attend_heads(q_ref, kv, new_ref, lengths, flat, mixed_flat, large[1].wait)
-    put_pieces(out_ref, mixed_flat)
+    put_pieces(out_ref, mixed_flat, away)
 
 
 def attend(queries, kv_cache, new_kv, lengths):
@@ -189,12 +197,12 @@
             cost=pl.CostEstimate(flops=8 << 20, bytes_accessed=6 << 20, transcendentals=0),
         )
 
-    received = partner(half(1), "side", chips)
+    received = across(half(1), 0, chips // 2)
     kept = half(0)
     blocks = {0: kept, chips // 2: received}
     bit = chips // 4
     while bit:
-        blocks.update({d ^ bit: partner(block, "side", 2 * bit) for d, block in blocks.items()})
+        blocks.update({d ^ bit: across(block, 0, bit) for d, block in blocks.items()})
         bit //= 2
     return [blocks[d] for d in range(chips)]
 
@@ -254,12 +262,12 @@
         (jax.ShapeDtypeStruct(shape, jnp.float32), jax.ShapeDtypeStruct(shape, jnp.bfloat16)),
     )
     bit = 1
-    more = partner(sent, "side", 2 * bit)
+    more = across(sent, 0, bit)
     while 2 * bit < chips:
         kept = kept + more.astype(jnp.float32)
         bit *= 2
         swapped = [kept[(d ^ bit) * rows : ((d ^ bit) + 1) * rows] for d in range(chips)]
-        more = partner(jnp.concatenate(swapped).astype(jnp.bfloat16), "side", 2 * bit)
+        more = across(jnp.concatenate(swapped).astype(jnp.bfloat16), 0, bit)
     return kept, sent, more
 
 
@@ -335,19 +343,20 @@
 def homeward(kept, sent, aways, rows):
     bit = lax.axis_size("side") // 4
     while bit:
-        more = partner(sent, "side", 2 * bit)
+        more = across(sent, 0, bit)
         half = kept.shape[0] // 2
         pieces = ((half, jnp.float32), (half, jnp.bfloat16))
         kept, sent = merge(kept, more, pieces)
         bit //= 2
-    more = partner(sent, "dev", 1)
+    more = across(sent, 1, 0)
     pieces = tuple((rows, jnp.bfloat16 if away else jnp.float32) for away in aways)
     return merge(kept, more, pieces)
 
 
 def dev_groups(devs):
-    upper = list(range(0, devs, 2))
-    return upper[: len(upper) // 2], upper[len(upper) // 2 :]
+    far = list(range(devs - 2, 0, -2))
+    middle = len(far) // 2
+    return [0] + far[:middle], far[middle:]
 
 
 def body(
@@ -386,16 +395,17 @@
 
     early, late = dev_groups(devs)
     near = {0: normed}
-    for away in early[1:] + late:
-        near[away] = partner(normed, "dev", away)
+    for away in early + late:
+        if away:
+            near[away] = across(normed, away, 0)
     home = []
     for aways in (early, late):
         blocks = [near[away] for away in aways]
-        blocks += [partner(near[away], "dev", 1) for away in aways]
+        blocks += [across(near[away], 1, 0) for away in aways]
         kept, sent = run_experts(blocks, weights, rows, width)
         for away, block in zip(aways, homeward(kept, sent, aways, rows)):
             if away:
-                block = partner(block, "dev", away).astype(jnp.float32)
+                block = across(block, away, 0).astype(jnp.float32)
             home.append(block)
     expert_sum = functools.reduce(jnp.add, home)
     return (stream, expert_sum.astype(jnp.bfloat16))

time: 49.2 us -> 50.5 us (1.026)
  starting transfers between devices: 25.5 us -> 28.7 us
  waiting for transfers between devices: 11.6 us -> 9.62 us
    ppermute x0 -> x16, starting transfers between devices: none -> 27.5 us  [across(): lax.ppermute(block, ('dev', 'side'), [(i, i ^ mask) for i in range(count)])]
    ppermute x19 -> x3, starting transfers between devices: 25.5 us -> 1.13 us  [partner(): return lax.ppermute(block, axis, [(i, i ^ mask) for i in range(count)])]
    ppermute x19 -> x3, waiting for transfers between devices: 11.6 us -> 0.01 us  [partner(): return lax.ppermute(block, axis, [(i, i ^ mask) for i in range(count)])]
    ppermute x0 -> x16, waiting for transfers between devices: none -> 9.61 us  [across(): lax.ppermute(block, ('dev', 'side'), [(i, i ^ mask) for i in range(count)])]
  transfers between devices with their start and end apart: 19 -> 19, of which waited for: 9 -> 7; matrix products, arithmetic and copies ran while one was open for 1% -> 1% of each run, Pallas kernels for 20% -> 20%
where the time goes in v3:
time: 50.5 us; the launch traced here: 50.2 us
  starting transfers between devices  28.7 us (57%)
  Pallas kernels  9.86 us (20%)
  waiting for transfers between devices  9.62 us (19%)
  between operations  0.78 us (2%)
  local copies, waits for them, and re-layouts  0.65 us (1%)
  other arithmetic  0.63 us (1%)
    ppermute x16, starting transfers between devices, across(): lax.ppermute(block, ('dev', 'side'), [(i, i ^ mask) for i in range(count)])  27.5 us
    pallas_call x10, Pallas kernels, kernel_call(): pl.pallas_call(body, out_shape=outs, in_specs=in_specs or [VMEM] * len(op...  9.86 us
    ppermute x16, waiting for transfers between devices, across(): lax.ppermute(block, ('dev', 'side'), [(i, i ^ mask) for i in range(count)])  9.61 us
    ppermute x3, starting transfers between devices, partner(): return lax.ppermute(block, axis, [(i, i ^ mask) for i in range(count)])  1.13 us
  transfers between devices with their start and end apart: 19, of which 7 were waited for; matrix products, arithmetic and copies ran while one was open for 1% of the time, Pallas kernels for 20%

profile of v3, /device:TPU:0, one launch (start us, length us, event | category | flops | bytes accessed | tf_op | source)
XLA Modules:
  0.0 50.2 jit_solution(5160081683044005999)
XLA Ops:
  0.6 0.6 %collective-permute-start.1 = (bf16[1024,2048]{1,0:T(8,128)(2,1)}, bf16[1024,2048]{1,0:T(8,128)(2,1)S(1)}, u32[]{:S(2)}, u32[]{:S(2)}) collective-permute-start(bf16[1024,2048]{1,0:T(8,128)(2,1)} %refs_2_.1), channel_id=1, source_target_pairs={{0,1},{1,0},{2,3},{3,2},{4,5},{5,4},{6,7},{7,6},{8,9},{9,8},{10,11... | collective-permute-start | bytes 12582920 | tf_op jit(solution)/shard_map/ppermute | solution.py:35
  1.2 0.1 collective-permute-start.6
  1.3 0.0 copy-start.2
  1.3 0.0 copy-start.3
  1.3 0.0 copy-start.5
  1.3 0.0 copy-start.6
  1.3 0.5 collective-permute-start.7
  1.8 2.5 %shard_map.123 = bf16[1,8,2048]{2,1,0:T(8,128)(2,1)S(1)} custom-call(bf16[8,4096]{1,0:T(8,128)(2,1)} %q_hbm.3, bf16[8,192,1024]{2,1,0:T(8,128)(2,1)} %kv_hbm.3, bf16[8,1024]{1,0:T(8,128)(2,1)} %new_hbm.3, s32[8]{0:T(128)} %length_hbm.3), custom_call_target="tpu_custom_call" | custom-call | flops 8388608 | bytes 6291456 | tf_op jit(solution)/shard_map/pallas_call | solution.py:18
  4.3 2.7 %collective-permute-start = (bf16[1,8,2048]{2,1,0:T(8,128)(2,1)S(1)}, bf16[1,8,2048]{2,1,0:T(8,128)(2,1)S(1)}, u32[]{:S(2)}, u32[]{:S(2)}) collective-permute-start(bf16[1,8,2048]{2,1,0:T(8,128)(2,1)S(1)} %shard_map.123), channel_id=1, source_target_pairs={{0,3},{1,2},{2,1},{3,0},{4,7},{5,6},{6,5},{7,4},{8,11},{9,10},{10,... | collective-permute-start | bytes 98312 | tf_op jit(solution)/shard_map/ppermute | solution.py:42
  6.9 2.2 %shard_map.122.refs_0_ = bf16[1,8,2048]{2,1,0:T(8,128)(2,1)S(1)} custom-call(bf16[8,4096]{1,0:T(8,128)(2,1)} %q_hbm.3, bf16[8,192,1024]{2,1,0:T(8,128)(2,1)} %kv_hbm.3, bf16[8,1024]{1,0:T(8,128)(2,1)} %new_hbm.3, s32[8]{0:T(128)} %length_hbm.3), custom_call_target="tpu_custom_call" | custom-call | flops 8388608 | bytes 6291456 | tf_op jit(solution)/shard_map/pallas_call | solution.py:18
  9.2 0.0 copy-start.4
  9.2 0.0 copy-start
  9.2 0.0 copy-start.1
  9.2 0.0 collective-permute-done.refs_1_
  9.2 0.0 collective-permute-done.1.refs_3_
  9.2 0.0 copy-done.2
  9.3 0.0 copy-done.3
  9.3 0.0 copy-done.5
  9.3 0.0 copy-done.6
  9.3 1.2 %shard_map.124 = (f32[16,2176]{1,0:T(8,128)S(1)}, bf16[16,2176]{1,0:T(8,128)(2,1)S(1)}) custom-call(bf16[1,8,2048]{2,1,0:T(8,128)(2,1)S(1)} %shard_map.122.refs_0_, bf16[1,8,2048]{2,1,0:T(8,128)(2,1)S(1)} %collective-permute-done.refs_1_, bf16[1024,2048]{1,0:T(8,128)(2,1)S(1)} %copy-done.2, bf16[1024,2048]{1,0:T(8,128)(2,1)S(1)} %collective-permute-done.1.refs_3_, ...), custom_call_target="tpu_custom_call" | custom-call | tf_op jit(solution)/shard_map/pallas_call | solution.py:18
  10.5 1.5 %collective-permute-start.2 = (bf16[16,2176]{1,0:T(8,128)(2,1)S(1)}, bf16[16,2176]{1,0:T(8,128)(2,1)S(1)}, u32[]{:S(2)}, u32[]{:S(2)}) collective-permute-start(bf16[16,2176]{1,0:T(8,128)(2,1)S(1)} %get-tuple-element.19), channel_id=1, source_target_pairs={{0,3},{1,2},{2,1},{3,0},{4,7},{5,6},{6,5},{7,4},{8,11},{9,10},{10,... | collective-permute-start | bytes 208904 | tf_op jit(solution)/shard_map/ppermute | solution.py:42
  12.0 2.7 %collective-permute-done.2.more_ref = bf16[16,2176]{1,0:T(8,128)(2,1)S(1)} collective-permute-done((bf16[16,2176]{1,0:T(8,128)(2,1)S(1)}, bf16[16,2176]{1,0:T(8,128)(2,1)S(1)}, u32[]{:S(2)}, u32[]{:S(2)}) %collective-permute-start.2) | collective-permute-done | bytes 69664 | tf_op jit(solution)/shard_map/ppermute | solution.py:42
  14.7 0.0 copy-done.4
  14.7 0.1 shard_map.125
  14.8 2.7 %collective-permute-start.11 = (bf16[16,2176]{1,0:T(8,128)(2,1)S(1)}, bf16[16,2176]{1,0:T(8,128)(2,1)S(1)}, u32[]{:S(2)}, u32[]{:S(2)}) collective-permute-start(bf16[16,2176]{1,0:T(8,128)(2,1)S(1)} %get-tuple-element.21.refs_0_), channel_id=1, source_target_pairs={{0,17},{1,16},{2,19},{3,18},{4,21},{5,20},{6,23},{7,22},{8,25},{9,... | collective-permute-start | bytes 208904 | tf_op jit(solution)/shard_map/ppermute | solution.py:42
  17.5 1.6 %collective-permute-start.12 = (bf16[16,2176]{1,0:T(8,128)(2,1)S(1)}, bf16[16,2176]{1,0:T(8,128)(2,1)S(1)}, u32[]{:S(2)}, u32[]{:S(2)}) collective-permute-start(bf16[16,2176]{1,0:T(8,128)(2,1)S(1)} %get-tuple-element.21.refs_0_), channel_id=1, source_target_pairs={{0,9},{1,8},{2,11},{3,10},{4,13},{5,12},{6,15},{7,14},{8,1},{9,0},... | collective-permute-start | bytes 208904 | tf_op jit(solution)/shard_map/ppermute | solution.py:42
  19.0 0.0 collective-permute-start.3
  19.0 0.9 %collective-permute-done.11.refs_0_ = bf16[16,2176]{1,0:T(8,128)(2,1)S(1)} collective-permute-done((bf16[16,2176]{1,0:T(8,128)(2,1)S(1)}, bf16[16,2176]{1,0:T(8,128)(2,1)S(1)}, u32[]{:S(2)}, u32[]{:S(2)}) %collective-permute-start.11) | collective-permute-done | bytes 69664 | tf_op jit(solution)/shard_map/ppermute | solution.py:42
  19.9 3.2 %collective-permute-start.13 = (bf16[16,2176]{1,0:T(8,128)(2,1)S(1)}, bf16[16,2176]{1,0:T(8,128)(2,1)S(1)}, u32[]{:S(2)}, u32[]{:S(2)}) collective-permute-start(bf16[16,2176]{1,0:T(8,128)(2,1)S(1)} %collective-permute-done.11.refs_0_), channel_id=1, source_target_pairs={{0,5},{1,4},{2,7},{3,6},{4,1},{5,0},{6,3},{7,2},{8,13},{9,12},{10,... | collective-permute-start | bytes 208904 | tf_op jit(solution)/shard_map/ppermute | solution.py:42
  23.1 0.0 collective-permute-done.12.refs_1_
  23.1 0.2 collective-permute-start.14
  23.3 0.0 collective-permute-done.7.refs_7_
  23.3 1.5 %collective-permute-start.4 = (bf16[16,2176]{1,0:T(8,128)(2,1)S(1)}, bf16[16,2176]{1,0:T(8,128)(2,1)S(1)}, u32[]{:S(2)}, u32[]{:S(2)}) collective-permute-start(bf16[16,2176]{1,0:T(8,128)(2,1)S(1)} %get-tuple-element.21.refs_0_), channel_id=1, source_target_pairs={{0,5},{1,4},{2,7},{3,6},{4,1},{5,0},{6,3},{7,2},{8,13},{9,12},{10,... | collective-permute-start | bytes 208904 | tf_op jit(solution)/shard_map/ppermute | solution.py:42
  24.8 0.2 collective-permute-done.3.refs_1_
  25.0 1.3 %collective-permute-start.5 = (bf16[16,2176]{1,0:T(8,128)(2,1)S(1)}, bf16[16,2176]{1,0:T(8,128)(2,1)S(1)}, u32[]{:S(2)}, u32[]{:S(2)}) collective-permute-start(bf16[16,2176]{1,0:T(8,128)(2,1)S(1)} %collective-permute-done.3.refs_1_), channel_id=1, source_target_pairs={{0,5},{1,4},{2,7},{3,6},{4,1},{5,0},{6,3},{7,2},{8,13},{9,12},{10,... | collective-permute-start | bytes 208904 | tf_op jit(solution)/shard_map/ppermute | solution.py:42
  26.2 0.0 collective-permute-done.6.refs_5_
  26.2 0.0 collective-permute-done.13.refs_2_
  26.3 1.0 %collective-permute-done.14.refs_3_ = bf16[16,2176]{1,0:T(8,128)(2,1)S(1)} collective-permute-done((bf16[16,2176]{1,0:T(8,128)(2,1)S(1)}, bf16[16,2176]{1,0:T(8,128)(2,1)S(1)}, u32[]{:S(2)}, u32[]{:S(2)}) %collective-permute-start.14) | collective-permute-done | bytes 69664 | tf_op jit(solution)/shard_map/ppermute | solution.py:42
  27.3 0.0 copy-done
  27.3 0.0 copy-done.1
  27.3 1.9 %shard_map.129 = (f32[32,2048]{1,0:T(8,128)S(1)}, bf16[32,2048]{1,0:T(8,128)(2,1)S(1)}) custom-call(bf16[16,2176]{1,0:T(8,128)(2,1)S(1)} %collective-permute-done.11.refs_0_, bf16[16,2176]{1,0:T(8,128)(2,1)S(1)} %collective-permute-done.12.refs_1_, bf16[16,2176]{1,0:T(8,128)(2,1)S(1)} %collective-permute-done.13.refs_2_, ...), custom_call_target="tpu_custom_call" | custom-call | flops 1073741824 | bytes 4194304 | tf_op jit(solution)/shard_map/pallas_call | solution.py:18
  29.2 1.8 %collective-permute-start.15 = (bf16[32,2048]{1,0:T(8,128)(2,1)S(1)}, bf16[32,2048]{1,0:T(8,128)(2,1)S(1)}, u32[]{:S(2)}, u32[]{:S(2)}) collective-permute-start(bf16[32,2048]{1,0:T(8,128)(2,1)S(1)} %get-tuple-element.29), channel_id=1, source_target_pairs={{0,3},{1,2},{2,1},{3,0},{4,7},{5,6},{6,5},{7,4},{8,11},{9,10},{10,... | collective-permute-start | bytes 393224 | tf_op jit(solution)/shard_map/ppermute | solution.py:42
  31.0 0.0 collective-permute-done.4.refs_2_
  31.0 0.0 collective-permute-done.5.refs_3_
  31.0 1.8 %shard_map.126 = (f32[32,2048]{1,0:T(8,128)S(1)}, bf16[32,2048]{1,0:T(8,128)(2,1)S(1)}) custom-call(bf16[16,2176]{1,0:T(8,128)(2,1)S(1)} %get-tuple-element.21.refs_0_, bf16[16,2176]{1,0:T(8,128)(2,1)S(1)} %collective-permute-done.3.refs_1_, bf16[16,2176]{1,0:T(8,128)(2,1)S(1)} %collective-permute-done.4.refs_2_, ...), custom_call_target="tpu_custom_call" | custom-call | flops 1073741824 | bytes 4194304 | tf_op jit(solution)/shard_map/pallas_call | solution.py:18
  32.8 0.6 %collective-permute-start.8 = (bf16[32,2048]{1,0:T(8,128)(2,1)S(1)}, bf16[32,2048]{1,0:T(8,128)(2,1)S(1)}, u32[]{:S(2)}, u32[]{:S(2)}) collective-permute-start(bf16[32,2048]{1,0:T(8,128)(2,1)S(1)} %get-tuple-element.23), channel_id=1, source_target_pairs={{0,3},{1,2},{2,1},{3,0},{4,7},{5,6},{6,5},{7,4},{8,11},{9,10},{10,... | collective-permute-start | bytes 393224 | tf_op jit(solution)/shard_map/ppermute | solution.py:42
  33.4 0.8 %collective-permute-done.15.more_ref = bf16[32,2048]{1,0:T(8,128)(2,1)S(1)} collective-permute-done((bf16[32,2048]{1,0:T(8,128)(2,1)S(1)}, bf16[32,2048]{1,0:T(8,128)(2,1)S(1)}, u32[]{:S(2)}, u32[]{:S(2)}) %collective-permute-start.15) | collective-permute-done | bytes 131104 | tf_op jit(solution)/shard_map/ppermute | solution.py:42
  34.3 2.1 %collective-permute-start.16 = (bf16[16,2048]{1,0:T(8,128)(2,1)S(1)}, bf16[16,2048]{1,0:T(8,128)(2,1)S(1)}, u32[]{:S(2)}, u32[]{:S(2)}) collective-permute-start(bf16[16,2048]{1,0:T(8,128)(2,1)S(1)} %get-tuple-element.31), channel_id=1, source_target_pairs={{0,5},{1,4},{2,7},{3,6},{4,1},{5,0},{6,3},{7,2},{8,13},{9,12},{10,... | collective-permute-start | bytes 196616 | tf_op jit(solution)/shard_map/ppermute | solution.py:42
  36.3 2.3 %collective-permute-done.8.more_ref = bf16[32,2048]{1,0:T(8,128)(2,1)S(1)} collective-permute-done((bf16[32,2048]{1,0:T(8,128)(2,1)S(1)}, bf16[32,2048]{1,0:T(8,128)(2,1)S(1)}, u32[]{:S(2)}, u32[]{:S(2)}) %collective-permute-start.8) | collective-permute-done | bytes 131104 | tf_op jit(solution)/shard_map/ppermute | solution.py:42
  38.6 0.3 collective-permute-start.9
  39.0 0.0 collective-permute-done.16.more_ref
  39.0 1.1 %collective-permute-start.18 = (bf16[8,2048]{1,0:T(8,128)(2,1)S(1)}, bf16[8,2048]{1,0:T(8,128)(2,1)S(1)}, u32[]{:S(2)}, u32[]{:S(2)}) collective-permute-start(bf16[8,2048]{1,0:T(8,128)(2,1)S(1)} %get-tuple-element.33), channel_id=1, source_target_pairs={{0,9},{1,8},{2,11},{3,10},{4,13},{5,12},{6,15},{7,14},{8,1},{9,0},... | collective-permute-start | bytes 98312 | tf_op jit(solution)/shard_map/ppermute | solution.py:42
  40.1 4.2 %collective-permute-start.17 = (bf16[8,2048]{1,0:T(8,128)(2,1)S(1)}, bf16[8,2048]{1,0:T(8,128)(2,1)S(1)}, u32[]{:S(2)}, u32[]{:S(2)}) collective-permute-start(bf16[8,2048]{1,0:T(8,128)(2,1)S(1)} %get-tuple-element.32), channel_id=1, source_target_pairs={{0,17},{1,16},{2,19},{3,18},{4,21},{5,20},{6,23},{7,22},{8,25},{9,... | collective-permute-start | bytes 98312 | tf_op jit(solution)/shard_map/ppermute | solution.py:42
  44.3 0.0 collective-permute-done.9.more_ref
  44.4 2.8 %collective-permute-start.10 = (bf16[8,2048]{1,0:T(8,128)(2,1)S(1)}, bf16[8,2048]{1,0:T(8,128)(2,1)S(1)}, u32[]{:S(2)}, u32[]{:S(2)}) collective-permute-start(bf16[8,2048]{1,0:T(8,128)(2,1)S(1)} %get-tuple-element.27), channel_id=1, source_target_pairs={{0,25},{1,24},{2,27},{3,26},{4,29},{5,28},{6,31},{7,30},{8,17},{9,... | collective-permute-start | bytes 98312 | tf_op jit(solution)/shard_map/ppermute | solution.py:42
  47.2 0.6 %copy.13 = bf16[8,2048]{1,0:T(8,128)(2,1)} copy(bf16[8,2048]{1,0:T(8,128)(2,1)S(1)} %get-tuple-element.34) | data formatting | bytes 65536
  47.8 0.0 collective-permute-done.18
  47.8 0.0 collective-permute-done.17
  47.8 1.8 %collective-permute-done.10 = bf16[8,2048]{1,0:T(8,128)(2,1)S(1)} collective-permute-done((bf16[8,2048]{1,0:T(8,128)(2,1)S(1)}, bf16[8,2048]{1,0:T(8,128)(2,1)S(1)}, u32[]{:S(2)}, u32[]{:S(2)}) %collective-permute-start.10) | collective-permute-done | bytes 32800 | tf_op jit(solution)/shard_map/ppermute | solution.py:42
  49.6 0.6 %add_convert_fusion = bf16[8,2048]{1,0:T(8,128)(2,1)} fusion(bf16[8,2048]{1,0:T(8,128)(2,1)S(1)} %collective-permute-done.18, bf16[8,2048]{1,0:T(8,128)(2,1)S(1)} %collective-permute-done.17, f32[8,2048]{1,0:T(8,128)S(1)} %get-tuple-element.26, bf16[8,2048]{1,0:T(8,128)(2,1)S(1)} %collective-permute-done.10), kind=kLoop, calls=%fused_computation | loop fusion | flops 114688 | bytes 196608 | tf_op jit(solution)/shard_map/convert_element_type | solution.py:411
  (4 shorter events, 0.1 us)
Async XLA Ops:
  0.6 8.6 %collective-permute-start.1 = (bf16[1024,2048]{1,0:T(8,128)(2,1)}, bf16[1024,2048]{1,0:T(8,128)(2,1)S(1)}, u32[]{:S(2)}, u32[]{:S(2)}) collective-permute-start(bf16[1024,2048]{1,0:T(8,128)(2,1)} %refs_2_.1), channel_id=1, source_target_pairs={{0,1},{1,0},{2,3},{3,2},{4,5},{5,4},{6,7},{7,6},{8,9},{9,8},{10,11... | collective-permute-start | bytes 12582920 | tf_op jit(solution)/shard_map/ppermute | solution.py:35
  1.2 25.1 %collective-permute-start.6 = (bf16[2048,768]{1,0:T(8,128)(2,1)}, bf16[2048,768]{1,0:T(8,128)(2,1)S(1)}, u32[]{:S(2)}, u32[]{:S(2)}) collective-permute-start(bf16[2048,768]{1,0:T(8,128)(2,1)} %bitcast.3), channel_id=1, source_target_pairs={{0,1},{1,0},{2,3},{3,2},{4,5},{5,4},{6,7},{7,6},{8,9},{9,8},{10,11... | collective-permute-start | bytes 9437192 | tf_op jit(solution)/shard_map/ppermute | solution.py:35
  1.3 8.0 %copy-start.2 = (bf16[1024,2048]{1,0:T(8,128)(2,1)S(1)}, bf16[1024,2048]{1,0:T(8,128)(2,1)}, u32[]{:S(2)}) copy-start(bf16[1024,2048]{1,0:T(8,128)(2,1)} %refs_2_.1) | copy-start | bytes 12582916
  1.3 8.0 %copy-start.3 = (bf16[8,2048]{1,0:T(8,128)(2,1)S(1)}, bf16[8,2048]{1,0:T(8,128)(2,1)}, u32[]{:S(2)}) copy-start(bf16[8,2048]{1,0:T(8,128)(2,1)} %refs_4_.1) | copy-start | bytes 98308
  1.3 8.0 %copy-start.5 = (s32[8,8]{1,0:T(8,128)S(1)}, s32[8,8]{1,0:T(8,128)}, u32[]{:S(2)}) copy-start(s32[8,8]{1,0:T(8,128)} %refs_5_.1) | copy-start | bytes 772
  1.3 8.0 %copy-start.6 = (s32[8,8]{1,0:T(8,128)S(1)}, s32[8,8]{1,0:T(8,128)}, u32[]{:S(2)}) copy-start(s32[8,8]{1,0:T(8,128)} %refs_6_.1) | copy-start | bytes 772
  1.3 22.0 %collective-permute-start.7 = (bf16[384,2048]{1,0:T(8,128)(2,1)}, bf16[384,2048]{1,0:T(8,128)(2,1)S(1)}, u32[]{:S(2)}, u32[]{:S(2)}) collective-permute-start(bf16[384,2048]{1,0:T(8,128)(2,1)} %bitcast.6), channel_id=1, source_target_pairs={{0,1},{1,0},{2,3},{3,2},{4,5},{5,4},{6,7},{7,6},{8,9},{9,8},{10,11... | collective-permute-start | bytes 4718600 | tf_op jit(solution)/shard_map/ppermute | solution.py:35
  4.3 4.9 %collective-permute-start = (bf16[1,8,2048]{2,1,0:T(8,128)(2,1)S(1)}, bf16[1,8,2048]{2,1,0:T(8,128)(2,1)S(1)}, u32[]{:S(2)}, u32[]{:S(2)}) collective-permute-start(bf16[1,8,2048]{2,1,0:T(8,128)(2,1)S(1)} %shard_map.123), channel_id=1, source_target_pairs={{0,3},{1,2},{2,1},{3,0},{4,7},{5,6},{6,5},{7,4},{8,11},{9,10},{10,... | collective-permute-start | bytes 98312 | tf_op jit(solution)/shard_map/ppermute | solution.py:42
  9.2 5.5 %copy-start.4 = (f32[2048]{0:T(1024)S(1)}, f32[2048]{0:T(1024)}, u32[]{:S(2)}) copy-start(f32[2048]{0:T(1024)} %param.17) | copy-start | bytes 24580
  9.2 18.1 %copy-start = (bf16[1,2048,768]{2,1,0:T(8,128)(2,1)S(1)}, bf16[1,2048,768]{2,1,0:T(8,128)(2,1)}, u32[]{:S(2)}) copy-start(bf16[1,2048,768]{2,1,0:T(8,128)(2,1)} %param.20) | copy-start | bytes 9437188
  9.2 18.1 %copy-start.1 = (bf16[1,384,2048]{2,1,0:T(8,128)(2,1)S(1)}, bf16[1,384,2048]{2,1,0:T(8,128)(2,1)}, u32[]{:S(2)}) copy-start(bf16[1,384,2048]{2,1,0:T(8,128)(2,1)} %param.21) | copy-start | bytes 4718596
  10.5 4.2 %collective-permute-start.2 = (bf16[16,2176]{1,0:T(8,128)(2,1)S(1)}, bf16[16,2176]{1,0:T(8,128)(2,1)S(1)}, u32[]{:S(2)}, u32[]{:S(2)}) collective-permute-start(bf16[16,2176]{1,0:T(8,128)(2,1)S(1)} %get-tuple-element.19), channel_id=1, source_target_pairs={{0,3},{1,2},{2,1},{3,0},{4,7},{5,6},{6,5},{7,4},{8,11},{9,10},{10,... | collective-permute-start | bytes 208904 | tf_op jit(solution)/shard_map/ppermute | solution.py:42
  14.8 5.1 %collective-permute-start.11 = (bf16[16,2176]{1,0:T(8,128)(2,1)S(1)}, bf16[16,2176]{1,0:T(8,128)(2,1)S(1)}, u32[]{:S(2)}, u32[]{:S(2)}) collective-permute-start(bf16[16,2176]{1,0:T(8,128)(2,1)S(1)} %get-tuple-element.21.refs_0_), channel_id=1, source_target_pairs={{0,17},{1,16},{2,19},{3,18},{4,21},{5,20},{6,23},{7,22},{8,25},{9,... | collective-permute-start | bytes 208904 | tf_op jit(solution)/shard_map/ppermute | solution.py:42
  17.5 5.6 %collective-permute-start.12 = (bf16[16,2176]{1,0:T(8,128)(2,1)S(1)}, bf16[16,2176]{1,0:T(8,128)(2,1)S(1)}, u32[]{:S(2)}, u32[]{:S(2)}) collective-permute-start(bf16[16,2176]{1,0:T(8,128)(2,1)S(1)} %get-tuple-element.21.refs_0_), channel_id=1, source_target_pairs={{0,9},{1,8},{2,11},{3,10},{4,13},{5,12},{6,15},{7,14},{8,1},{9,0},... | collective-permute-start | bytes 208904 | tf_op jit(solution)/shard_map/ppermute | solution.py:42
  19.0 6.0 %collective-permute-start.3 = (bf16[16,2176]{1,0:T(8,128)(2,1)S(1)}, bf16[16,2176]{1,0:T(8,128)(2,1)S(1)}, u32[]{:S(2)}, u32[]{:S(2)}) collective-permute-start(bf16[16,2176]{1,0:T(8,128)(2,1)S(1)} %get-tuple-element.21.refs_0_), channel_id=1, source_target_pairs={{0,25},{1,24},{2,27},{3,26},{4,29},{5,28},{6,31},{7,30},{8,17},{9,... | collective-permute-start | bytes 208904 | tf_op jit(solution)/shard_map/ppermute | solution.py:42
  19.9 6.4 %collective-permute-start.13 = (bf16[16,2176]{1,0:T(8,128)(2,1)S(1)}, bf16[16,2176]{1,0:T(8,128)(2,1)S(1)}, u32[]{:S(2)}, u32[]{:S(2)}) collective-permute-start(bf16[16,2176]{1,0:T(8,128)(2,1)S(1)} %collective-permute-done.11.refs_0_), channel_id=1, source_target_pairs={{0,5},{1,4},{2,7},{3,6},{4,1},{5,0},{6,3},{7,2},{8,13},{9,12},{10,... | collective-permute-start | bytes 208904 | tf_op jit(solution)/shard_map/ppermute | solution.py:42
  23.1 4.2 %collective-permute-start.14 = (bf16[16,2176]{1,0:T(8,128)(2,1)S(1)}, bf16[16,2176]{1,0:T(8,128)(2,1)S(1)}, u32[]{:S(2)}, u32[]{:S(2)}) collective-permute-start(bf16[16,2176]{1,0:T(8,128)(2,1)S(1)} %collective-permute-done.12.refs_1_), channel_id=1, source_target_pairs={{0,5},{1,4},{2,7},{3,6},{4,1},{5,0},{6,3},{7,2},{8,13},{9,12},{10,... | collective-permute-start | bytes 208904 | tf_op jit(solution)/shard_map/ppermute | solution.py:42
  23.3 7.7 %collective-permute-start.4 = (bf16[16,2176]{1,0:T(8,128)(2,1)S(1)}, bf16[16,2176]{1,0:T(8,128)(2,1)S(1)}, u32[]{:S(2)}, u32[]{:S(2)}) collective-permute-start(bf16[16,2176]{1,0:T(8,128)(2,1)S(1)} %get-tuple-element.21.refs_0_), channel_id=1, source_target_pairs={{0,5},{1,4},{2,7},{3,6},{4,1},{5,0},{6,3},{7,2},{8,13},{9,12},{10,... | collective-permute-start | bytes 208904 | tf_op jit(solution)/shard_map/ppermute | solution.py:42
  25.0 6.0 %collective-permute-start.5 = (bf16[16,2176]{1,0:T(8,128)(2,1)S(1)}, bf16[16,2176]{1,0:T(8,128)(2,1)S(1)}, u32[]{:S(2)}, u32[]{:S(2)}) collective-permute-start(bf16[16,2176]{1,0:T(8,128)(2,1)S(1)} %collective-permute-done.3.refs_1_), channel_id=1, source_target_pairs={{0,5},{1,4},{2,7},{3,6},{4,1},{5,0},{6,3},{7,2},{8,13},{9,12},{10,... | collective-permute-start | bytes 208904 | tf_op jit(solution)/shard_map/ppermute | solution.py:42
  29.2 5.1 %collective-permute-start.15 = (bf16[32,2048]{1,0:T(8,128)(2,1)S(1)}, bf16[32,2048]{1,0:T(8,128)(2,1)S(1)}, u32[]{:S(2)}, u32[]{:S(2)}) collective-permute-start(bf16[32,2048]{1,0:T(8,128)(2,1)S(1)} %get-tuple-element.29), channel_id=1, source_target_pairs={{0,3},{1,2},{2,1},{3,0},{4,7},{5,6},{6,5},{7,4},{8,11},{9,10},{10,... | collective-permute-start | bytes 393224 | tf_op jit(solution)/shard_map/ppermute | solution.py:42
  32.8 5.8 %collective-permute-start.8 = (bf16[32,2048]{1,0:T(8,128)(2,1)S(1)}, bf16[32,2048]{1,0:T(8,128)(2,1)S(1)}, u32[]{:S(2)}, u32[]{:S(2)}) collective-permute-start(bf16[32,2048]{1,0:T(8,128)(2,1)S(1)} %get-tuple-element.23), channel_id=1, source_target_pairs={{0,3},{1,2},{2,1},{3,0},{4,7},{5,6},{6,5},{7,4},{8,11},{9,10},{10,... | collective-permute-start | bytes 393224 | tf_op jit(solution)/shard_map/ppermute | solution.py:42
  34.3 4.7 %collective-permute-start.16 = (bf16[16,2048]{1,0:T(8,128)(2,1)S(1)}, bf16[16,2048]{1,0:T(8,128)(2,1)S(1)}, u32[]{:S(2)}, u32[]{:S(2)}) collective-permute-start(bf16[16,2048]{1,0:T(8,128)(2,1)S(1)} %get-tuple-element.31), channel_id=1, source_target_pairs={{0,5},{1,4},{2,7},{3,6},{4,1},{5,0},{6,3},{7,2},{8,13},{9,12},{10,... | collective-permute-start | bytes 196616 | tf_op jit(solution)/shard_map/ppermute | solution.py:42
  38.6 5.7 %collective-permute-start.9 = (bf16[16,2048]{1,0:T(8,128)(2,1)S(1)}, bf16[16,2048]{1,0:T(8,128)(2,1)S(1)}, u32[]{:S(2)}, u32[]{:S(2)}) collective-permute-start(bf16[16,2048]{1,0:T(8,128)(2,1)S(1)} %get-tuple-element.25), channel_id=1, source_target_pairs={{0,5},{1,4},{2,7},{3,6},{4,1},{5,0},{6,3},{7,2},{8,13},{9,12},{10,... | collective-permute-start | bytes 196616 | tf_op jit(solution)/shard_map/ppermute | solution.py:42
  39.0 8.8 %collective-permute-start.18 = (bf16[8,2048]{1,0:T(8,128)(2,1)S(1)}, bf16[8,2048]{1,0:T(8,128)(2,1)S(1)}, u32[]{:S(2)}, u32[]{:S(2)}) collective-permute-start(bf16[8,2048]{1,0:T(8,128)(2,1)S(1)} %get-tuple-element.33), channel_id=1, source_target_pairs={{0,9},{1,8},{2,11},{3,10},{4,13},{5,12},{6,15},{7,14},{8,1},{9,0},... | collective-permute-start | bytes 98312 | tf_op jit(solution)/shard_map/ppermute | solution.py:42
  40.1 7.7 %collective-permute-start.17 = (bf16[8,2048]{1,0:T(8,128)(2,1)S(1)}, bf16[8,2048]{1,0:T(8,128)(2,1)S(1)}, u32[]{:S(2)}, u32[]{:S(2)}) collective-permute-start(bf16[8,2048]{1,0:T(8,128)(2,1)S(1)} %get-tuple-element.32), channel_id=1, source_target_pairs={{0,17},{1,16},{2,19},{3,18},{4,21},{5,20},{6,23},{7,22},{8,25},{9,... | collective-permute-start | bytes 98312 | tf_op jit(solution)/shard_map/ppermute | solution.py:42
  44.4 5.2 %collective-permute-start.10 = (bf16[8,2048]{1,0:T(8,128)(2,1)S(1)}, bf16[8,2048]{1,0:T(8,128)(2,1)S(1)}, u32[]{:S(2)}, u32[]{:S(2)}) collective-permute-start(bf16[8,2048]{1,0:T(8,128)(2,1)S(1)} %get-tuple-element.27), channel_id=1, source_target_pairs={{0,25},{1,24},{2,27},{3,26},{4,29},{5,28},{6,31},{7,30},{8,17},{9,... | collective-permute-start | bytes 98312 | tf_op jit(solution)/shard_map/ppermute | solution.py:42

commit v4 on v3

--- a/solution.py
+++ b/solution.py
@@ -40,6 +40,24 @@
     mask = over_dev * side + 2 * over_side + 1
     count = lax.axis_size("dev") * side
     return lax.ppermute(block, ("dev", "side"), [(i, i ^ mask) for i in range(count)])
+
+
+def device_class(dev, member):
+    ones = dev & 1
+    for bit in range((lax.axis_size("side") - 1).bit_length()):
+        ones = ones + ((member >> bit) & 1)
+    return ones & 1
+
+
+def apart(block, distances):
+    devs, side = lax.axis_size("dev"), lax.axis_size("side")
+    route = []
+    for dev in range(devs):
+        for member in range(side):
+            over_dev, over_side = distances[device_class(dev, member)]
+            here = dev * side + member
+            route.append((here, here ^ (over_dev * side + 2 * over_side + 1)))
+    return lax.ppermute(block, ("dev", "side"), route)
 
 
 def start_all(copies):
@@ -283,9 +301,9 @@
 
 
 def expert_kernel(rows, *refs):
-    kept_ref, sent_ref = refs[-2:]
-    in_own, in_other, down_own, down_other = refs[-6:-2]
-    blocks = refs[:-6]
+    kept_ref, sent_ref, result = refs[-3:]
+    in_own, in_other, down_own, down_other = refs[-7:-3]
+    blocks = refs[:-7]
     width = kept_ref.shape[1]
     units = down_own.shape[0]
     chips = lax.axis_size("side") // 2
@@ -301,28 +319,35 @@
         gate_up = jnp.dot(tokens, w_ref[...], preferred_element_type=jnp.float32)
         gate = gate_up[:, :units]
         hidden.append((gate / (1.0 + jnp.exp(-gate)) * gate_up[:, units:]).astype(jnp.bfloat16))
-    result = jnp.dot(hidden[0], down_own[...], preferred_element_type=jnp.float32) + jnp.dot(
+    total = jnp.dot(hidden[0], down_own[...], preferred_element_type=jnp.float32) + jnp.dot(
         hidden[1], down_other[...], preferred_element_type=jnp.float32
     )
-    result = result * share
-    count = tokens.shape[0] // (chips * rows)
-    for d in range(chips):
-        for i in range(count):
-            start = (i * chips + d) * rows
-            piece = result[start : start + rows]
-            to = ((d % (chips // 2)) * count + i) * rows
-            if d < chips // 2:
-                kept_ref[to : to + rows, :] = piece
-            else:
-                sent_ref[to : to + rows, :] = piece.astype(jnp.bfloat16)
+    result[...] = total * share
+    kind = device_class(lax.axis_index("dev"), lax.axis_index("side"))
+    nearby = len(blocks) // 2
+    slots = 2 * nearby * chips
+    for slot in range(slots):
+        index, upper = slot % nearby, slot // nearby
+        starts = []
+        for chip, far in ((upper // 2, upper % 2), (upper % chips, upper // chips)):
+            starts.append(((far * nearby + index) * chips + chip) * rows)
+        start = pl.multiple_of(jnp.where(kind == 0, starts[0], starts[1]), rows)
+        piece = result[pl.ds(start, rows), :]
+        to = slot % (slots // 2) * rows
+        if slot < slots // 2:
+            kept_ref[to : to + rows, :] = piece
+        else:
+            sent_ref[to : to + rows, :] = piece.astype(jnp.bfloat16)
 
 
 def run_experts(blocks, weights, rows, width):
-    shape = (sum(block.shape[0] for block in blocks) // 2, width)
+    count = sum(block.shape[0] for block in blocks)
+    shape = (count // 2, width)
     return kernel_call(
         functools.partial(expert_kernel, rows),
         (*blocks, *weights),
         (jax.ShapeDtypeStruct(shape, jnp.float32), jax.ShapeDtypeStruct(shape, jnp.bfloat16)),
+        scratch=[pltpu.VMEM((count, width), jnp.float32)],
         cost=pl.CostEstimate(flops=1 << 30, bytes_accessed=4 << 20, transcendentals=0),
     )
 
@@ -341,16 +366,21 @@
 
 
 def homeward(kept, sent, aways, rows):
-    bit = lax.axis_size("side") // 4
-    while bit:
-        more = across(sent, 0, bit)
+    over_side = []
+    chips = lax.axis_size("side") // 2
+    while chips > 1:
+        chips //= 2
+        over_side.append((0, chips))
+    first, second = over_side + [(1, 0)], [(1, 0)] + over_side
+    for step, distances in enumerate(zip(first, second)):
+        more = apart(sent, distances)
         half = kept.shape[0] // 2
         pieces = ((half, jnp.float32), (half, jnp.bfloat16))
-        kept, sent = merge(kept, more, pieces)
-        bit //= 2
-    more = across(sent, 1, 0)
-    pieces = tuple((rows, jnp.bfloat16 if away else jnp.float32) for away in aways)
-    return merge(kept, more, pieces)
+        if step + 1 == len(first):
+            pieces = tuple((rows, jnp.bfloat16 if away else jnp.float32) for away in aways)
+        parts = merge(kept, more, pieces)
+        kept, sent = parts[0], parts[-1]
+    return parts
 
 
 def dev_groups(devs):

time: 50.5 us -> 49.6 us (0.982)
    ppermute x16 -> x12, starting transfers between devices: 27.5 us -> 22.1 us  [across(): lax.ppermute(block, ('dev', 'side'), [(i, i ^ mask) for i in range(count)])]
    ppermute x0 -> x4, starting transfers between devices: none -> 5.09 us  [apart(): return lax.ppermute(block, ('dev', 'side'), route)]
    ppermute x16 -> x12, waiting for transfers between devices: 9.61 us -> 7.42 us  [across(): lax.ppermute(block, ('dev', 'side'), [(i, i ^ mask) for i in range(count)])]
    ppermute x0 -> x4, waiting for transfers between devices: none -> 1.76 us  [apart(): return lax.ppermute(block, ('dev', 'side'), route)]
where the time goes in v4:
time: 49.6 us; the launch traced here: 49.4 us
  starting transfers between devices  28.3 us (57%)
  Pallas kernels  9.89 us (20%)
  waiting for transfers between devices  9.18 us (19%)
  between operations  0.77 us (2%)
  local copies, waits for them, and re-layouts  0.65 us (1%)
  other arithmetic  0.63 us (1%)
    ppermute x12, starting transfers between devices, across(): lax.ppermute(block, ('dev', 'side'), [(i, i ^ mask) for i in range(count)])  22.1 us
    pallas_call x10, Pallas kernels, kernel_call(): pl.pallas_call(body, out_shape=outs, in_specs=in_specs or [VMEM] * len(op...  9.89 us
    ppermute x12, waiting for transfers between devices, across(): lax.ppermute(block, ('dev', 'side'), [(i, i ^ mask) for i in range(count)])  7.42 us
    ppermute x4, starting transfers between devices, apart(): return lax.ppermute(block, ('dev', 'side'), route)  5.09 us
    ppermute x4, waiting for transfers between devices, apart(): return lax.ppermute(block, ('dev', 'side'), route)  1.76 us
    ppermute x3, starting transfers between devices, partner(): return lax.ppermute(block, axis, [(i, i ^ mask) for i in range(count)])  1.13 us
  transfers between devices with their start and end apart: 19, of which 7 were waited for; matrix products, arithmetic and copies ran while one was open for 1% of the time, Pallas kernels for 20%

profile of v4, /device:TPU:0, one launch (start us, length us, event | category | flops | bytes accessed | tf_op | source)
XLA Modules:
  0.0 49.4 jit_solution(9456360326512224250)
XLA Ops:
  0.6 0.6 %collective-permute-start.1 = (bf16[1024,2048]{1,0:T(8,128)(2,1)}, bf16[1024,2048]{1,0:T(8,128)(2,1)S(1)}, u32[]{:S(2)}, u32[]{:S(2)}) collective-permute-start(bf16[1024,2048]{1,0:T(8,128)(2,1)} %refs_2_.1), channel_id=1, source_target_pairs={{0,1},{1,0},{2,3},{3,2},{4,5},{5,4},{6,7},{7,6},{8,9},{9,8},{10,11... | collective-permute-start | bytes 12582920 | tf_op jit(solution)/shard_map/ppermute | solution.py:35
  1.2 0.1 collective-permute-start.6
  1.3 0.0 copy-start.2
  1.3 0.0 copy-start.3
  1.3 0.0 copy-start.5
  1.3 0.0 copy-start.6
  1.3 0.5 %collective-permute-start.7 = (bf16[384,2048]{1,0:T(8,128)(2,1)}, bf16[384,2048]{1,0:T(8,128)(2,1)S(1)}, u32[]{:S(2)}, u32[]{:S(2)}) collective-permute-start(bf16[384,2048]{1,0:T(8,128)(2,1)} %bitcast.6), channel_id=1, source_target_pairs={{0,1},{1,0},{2,3},{3,2},{4,5},{5,4},{6,7},{7,6},{8,9},{9,8},{10,11... | collective-permute-start | bytes 4718600 | tf_op jit(solution)/shard_map/ppermute | solution.py:35
  1.8 2.5 %shard_map.123 = bf16[1,8,2048]{2,1,0:T(8,128)(2,1)S(1)} custom-call(bf16[8,4096]{1,0:T(8,128)(2,1)} %q_hbm.3, bf16[8,192,1024]{2,1,0:T(8,128)(2,1)} %kv_hbm.3, bf16[8,1024]{1,0:T(8,128)(2,1)} %new_hbm.3, s32[8]{0:T(128)} %length_hbm.3), custom_call_target="tpu_custom_call" | custom-call | flops 8388608 | bytes 6291456 | tf_op jit(solution)/shard_map/pallas_call | solution.py:18
  4.3 2.7 %collective-permute-start = (bf16[1,8,2048]{2,1,0:T(8,128)(2,1)S(1)}, bf16[1,8,2048]{2,1,0:T(8,128)(2,1)S(1)}, u32[]{:S(2)}, u32[]{:S(2)}) collective-permute-start(bf16[1,8,2048]{2,1,0:T(8,128)(2,1)S(1)} %shard_map.123), channel_id=1, source_target_pairs={{0,3},{1,2},{2,1},{3,0},{4,7},{5,6},{6,5},{7,4},{8,11},{9,10},{10,... | collective-permute-start | bytes 98312 | tf_op jit(solution)/shard_map/ppermute | solution.py:42
  6.9 2.2 %shard_map.122.refs_0_ = bf16[1,8,2048]{2,1,0:T(8,128)(2,1)S(1)} custom-call(bf16[8,4096]{1,0:T(8,128)(2,1)} %q_hbm.3, bf16[8,192,1024]{2,1,0:T(8,128)(2,1)} %kv_hbm.3, bf16[8,1024]{1,0:T(8,128)(2,1)} %new_hbm.3, s32[8]{0:T(128)} %length_hbm.3), custom_call_target="tpu_custom_call" | custom-call | flops 8388608 | bytes 6291456 | tf_op jit(solution)/shard_map/pallas_call | solution.py:18
  9.2 0.0 copy-start.4
  9.2 0.0 copy-start
  9.2 0.0 copy-start.1
  9.2 0.0 collective-permute-done.refs_1_
  9.2 0.0 collective-permute-done.1.refs_3_
  9.2 0.0 copy-done.2
  9.3 0.0 copy-done.3
  9.3 0.0 copy-done.5
  9.3 0.0 copy-done.6
  9.3 1.2 %shard_map.124 = (f32[16,2176]{1,0:T(8,128)S(1)}, bf16[16,2176]{1,0:T(8,128)(2,1)S(1)}) custom-call(bf16[1,8,2048]{2,1,0:T(8,128)(2,1)S(1)} %shard_map.122.refs_0_, bf16[1,8,2048]{2,1,0:T(8,128)(2,1)S(1)} %collective-permute-done.refs_1_, bf16[1024,2048]{1,0:T(8,128)(2,1)S(1)} %copy-done.2, bf16[1024,2048]{1,0:T(8,128)(2,1)S(1)} %collective-permute-done.1.refs_3_, ...), custom_call_target="tpu_custom_call" | custom-call | tf_op jit(solution)/shard_map/pallas_call | solution.py:18
  10.5 1.5 %collective-permute-start.2 = (bf16[16,2176]{1,0:T(8,128)(2,1)S(1)}, bf16[16,2176]{1,0:T(8,128)(2,1)S(1)}, u32[]{:S(2)}, u32[]{:S(2)}) collective-permute-start(bf16[16,2176]{1,0:T(8,128)(2,1)S(1)} %get-tuple-element.19), channel_id=1, source_target_pairs={{0,3},{1,2},{2,1},{3,0},{4,7},{5,6},{6,5},{7,4},{8,11},{9,10},{10,... | collective-permute-start | bytes 208904 | tf_op jit(solution)/shard_map/ppermute | solution.py:42
  12.0 2.7 %collective-permute-done.2.more_ref = bf16[16,2176]{1,0:T(8,128)(2,1)S(1)} collective-permute-done((bf16[16,2176]{1,0:T(8,128)(2,1)S(1)}, bf16[16,2176]{1,0:T(8,128)(2,1)S(1)}, u32[]{:S(2)}, u32[]{:S(2)}) %collective-permute-start.2) | collective-permute-done | bytes 69664 | tf_op jit(solution)/shard_map/ppermute | solution.py:42
  14.7 0.0 copy-done.4
  14.7 0.1 shard_map.125
  14.8 2.7 %collective-permute-start.11 = (bf16[16,2176]{1,0:T(8,128)(2,1)S(1)}, bf16[16,2176]{1,0:T(8,128)(2,1)S(1)}, u32[]{:S(2)}, u32[]{:S(2)}) collective-permute-start(bf16[16,2176]{1,0:T(8,128)(2,1)S(1)} %get-tuple-element.21.refs_0_), channel_id=1, source_target_pairs={{0,17},{1,16},{2,19},{3,18},{4,21},{5,20},{6,23},{7,22},{8,25},{9,... | collective-permute-start | bytes 208904 | tf_op jit(solution)/shard_map/ppermute | solution.py:42
  17.5 1.6 %collective-permute-start.12 = (bf16[16,2176]{1,0:T(8,128)(2,1)S(1)}, bf16[16,2176]{1,0:T(8,128)(2,1)S(1)}, u32[]{:S(2)}, u32[]{:S(2)}) collective-permute-start(bf16[16,2176]{1,0:T(8,128)(2,1)S(1)} %get-tuple-element.21.refs_0_), channel_id=1, source_target_pairs={{0,9},{1,8},{2,11},{3,10},{4,13},{5,12},{6,15},{7,14},{8,1},{9,0},... | collective-permute-start | bytes 208904 | tf_op jit(solution)/shard_map/ppermute | solution.py:42
  19.0 0.0 collective-permute-start.3
  19.0 0.9 %collective-permute-done.11.refs_0_ = bf16[16,2176]{1,0:T(8,128)(2,1)S(1)} collective-permute-done((bf16[16,2176]{1,0:T(8,128)(2,1)S(1)}, bf16[16,2176]{1,0:T(8,128)(2,1)S(1)}, u32[]{:S(2)}, u32[]{:S(2)}) %collective-permute-start.11) | collective-permute-done | bytes 69664 | tf_op jit(solution)/shard_map/ppermute | solution.py:42
  19.9 3.2 %collective-permute-start.13 = (bf16[16,2176]{1,0:T(8,128)(2,1)S(1)}, bf16[16,2176]{1,0:T(8,128)(2,1)S(1)}, u32[]{:S(2)}, u32[]{:S(2)}) collective-permute-start(bf16[16,2176]{1,0:T(8,128)(2,1)S(1)} %collective-permute-done.11.refs_0_), channel_id=1, source_target_pairs={{0,5},{1,4},{2,7},{3,6},{4,1},{5,0},{6,3},{7,2},{8,13},{9,12},{10,... | collective-permute-start | bytes 208904 | tf_op jit(solution)/shard_map/ppermute | solution.py:42
  23.1 0.0 collective-permute-done.12.refs_1_
  23.1 0.2 collective-permute-start.14
  23.3 0.0 collective-permute-done.7.refs_7_
  23.3 1.5 %collective-permute-start.4 = (bf16[16,2176]{1,0:T(8,128)(2,1)S(1)}, bf16[16,2176]{1,0:T(8,128)(2,1)S(1)}, u32[]{:S(2)}, u32[]{:S(2)}) collective-permute-start(bf16[16,2176]{1,0:T(8,128)(2,1)S(1)} %get-tuple-element.21.refs_0_), channel_id=1, source_target_pairs={{0,5},{1,4},{2,7},{3,6},{4,1},{5,0},{6,3},{7,2},{8,13},{9,12},{10,... | collective-permute-start | bytes 208904 | tf_op jit(solution)/shard_map/ppermute | solution.py:42
  24.8 0.2 collective-permute-done.3.refs_1_
  25.0 1.3 %collective-permute-start.5 = (bf16[16,2176]{1,0:T(8,128)(2,1)S(1)}, bf16[16,2176]{1,0:T(8,128)(2,1)S(1)}, u32[]{:S(2)}, u32[]{:S(2)}) collective-permute-start(bf16[16,2176]{1,0:T(8,128)(2,1)S(1)} %collective-permute-done.3.refs_1_), channel_id=1, source_target_pairs={{0,5},{1,4},{2,7},{3,6},{4,1},{5,0},{6,3},{7,2},{8,13},{9,12},{10,... | collective-permute-start | bytes 208904 | tf_op jit(solution)/shard_map/ppermute | solution.py:42
  26.2 0.0 collective-permute-done.6.refs_5_
  26.2 0.0 collective-permute-done.13.refs_2_
  26.3 1.0 %collective-permute-done.14.refs_3_ = bf16[16,2176]{1,0:T(8,128)(2,1)S(1)} collective-permute-done((bf16[16,2176]{1,0:T(8,128)(2,1)S(1)}, bf16[16,2176]{1,0:T(8,128)(2,1)S(1)}, u32[]{:S(2)}, u32[]{:S(2)}) %collective-permute-start.14) | collective-permute-done | bytes 69664 | tf_op jit(solution)/shard_map/ppermute | solution.py:42
  27.3 0.0 copy-done
  27.3 0.0 copy-done.1
  27.3 1.9 %shard_map.129 = (f32[32,2048]{1,0:T(8,128)S(1)}, bf16[32,2048]{1,0:T(8,128)(2,1)S(1)}) custom-call(bf16[16,2176]{1,0:T(8,128)(2,1)S(1)} %collective-permute-done.11.refs_0_, bf16[16,2176]{1,0:T(8,128)(2,1)S(1)} %collective-permute-done.12.refs_1_, bf16[16,2176]{1,0:T(8,128)(2,1)S(1)} %collective-permute-done.13.refs_2_, ...), custom_call_target="tpu_custom_call" | custom-call | flops 1073741824 | bytes 4194304 | tf_op jit(solution)/shard_map/pallas_call | solution.py:18
  29.2 1.8 %collective-permute-start.15 = (bf16[32,2048]{1,0:T(8,128)(2,1)S(1)}, bf16[32,2048]{1,0:T(8,128)(2,1)S(1)}, u32[]{:S(2)}, u32[]{:S(2)}) collective-permute-start(bf16[32,2048]{1,0:T(8,128)(2,1)S(1)} %get-tuple-element.29), channel_id=1, source_target_pairs={{0,3},{1,4},{2,7},{3,0},{4,1},{5,6},{6,5},{7,2},{8,11},{9,12},{10,... | collective-permute-start | bytes 393224 | tf_op jit(solution)/shard_map/ppermute | solution.py:60
  31.0 0.0 collective-permute-done.4.refs_2_
  31.0 0.0 collective-permute-done.5.refs_3_
  31.0 1.9 %shard_map.126 = (f32[32,2048]{1,0:T(8,128)S(1)}, bf16[32,2048]{1,0:T(8,128)(2,1)S(1)}) custom-call(bf16[16,2176]{1,0:T(8,128)(2,1)S(1)} %get-tuple-element.21.refs_0_, bf16[16,2176]{1,0:T(8,128)(2,1)S(1)} %collective-permute-done.3.refs_1_, bf16[16,2176]{1,0:T(8,128)(2,1)S(1)} %collective-permute-done.4.refs_2_, ...), custom_call_target="tpu_custom_call" | custom-call | flops 1073741824 | bytes 4194304 | tf_op jit(solution)/shard_map/pallas_call | solution.py:18
  32.8 0.6 %collective-permute-start.8 = (bf16[32,2048]{1,0:T(8,128)(2,1)S(1)}, bf16[32,2048]{1,0:T(8,128)(2,1)S(1)}, u32[]{:S(2)}, u32[]{:S(2)}) collective-permute-start(bf16[32,2048]{1,0:T(8,128)(2,1)S(1)} %get-tuple-element.23), channel_id=1, source_target_pairs={{0,3},{1,4},{2,7},{3,0},{4,1},{5,6},{6,5},{7,2},{8,11},{9,12},{10,... | collective-permute-start | bytes 393224 | tf_op jit(solution)/shard_map/ppermute | solution.py:60
  33.4 0.2 collective-permute-done.15.more_ref
  33.7 2.1 %collective-permute-start.16 = (bf16[16,2048]{1,0:T(8,128)(2,1)S(1)}, bf16[16,2048]{1,0:T(8,128)(2,1)S(1)}, u32[]{:S(2)}, u32[]{:S(2)}) collective-permute-start(bf16[16,2048]{1,0:T(8,128)(2,1)S(1)} %get-tuple-element.31), channel_id=1, source_target_pairs={{0,5},{1,2},{2,1},{3,6},{4,7},{5,0},{6,3},{7,4},{8,13},{9,10},{10,... | collective-permute-start | bytes 196616 | tf_op jit(solution)/shard_map/ppermute | solution.py:60
  35.8 1.5 %collective-permute-done.8.more_ref = bf16[32,2048]{1,0:T(8,128)(2,1)S(1)} collective-permute-done((bf16[32,2048]{1,0:T(8,128)(2,1)S(1)}, bf16[32,2048]{1,0:T(8,128)(2,1)S(1)}, u32[]{:S(2)}, u32[]{:S(2)}) %collective-permute-start.8) | collective-permute-done | bytes 131104 | tf_op jit(solution)/shard_map/ppermute | solution.py:60
  37.3 0.6 %collective-permute-start.9 = (bf16[16,2048]{1,0:T(8,128)(2,1)S(1)}, bf16[16,2048]{1,0:T(8,128)(2,1)S(1)}, u32[]{:S(2)}, u32[]{:S(2)}) collective-permute-start(bf16[16,2048]{1,0:T(8,128)(2,1)S(1)} %get-tuple-element.25), channel_id=1, source_target_pairs={{0,5},{1,2},{2,1},{3,6},{4,7},{5,0},{6,3},{7,4},{8,13},{9,10},{10,... | collective-permute-start | bytes 196616 | tf_op jit(solution)/shard_map/ppermute | solution.py:60
  38.0 0.0 collective-permute-done.16.more_ref
  38.0 1.6 %collective-permute-start.18 = (bf16[8,2048]{1,0:T(8,128)(2,1)S(1)}, bf16[8,2048]{1,0:T(8,128)(2,1)S(1)}, u32[]{:S(2)}, u32[]{:S(2)}) collective-permute-start(bf16[8,2048]{1,0:T(8,128)(2,1)S(1)} %get-tuple-element.33), channel_id=1, source_target_pairs={{0,9},{1,8},{2,11},{3,10},{4,13},{5,12},{6,15},{7,14},{8,1},{9,0},... | collective-permute-start | bytes 98312 | tf_op jit(solution)/shard_map/ppermute | solution.py:42
  39.6 4.0 %collective-permute-start.17 = (bf16[8,2048]{1,0:T(8,128)(2,1)S(1)}, bf16[8,2048]{1,0:T(8,128)(2,1)S(1)}, u32[]{:S(2)}, u32[]{:S(2)}) collective-permute-start(bf16[8,2048]{1,0:T(8,128)(2,1)S(1)} %get-tuple-element.32), channel_id=1, source_target_pairs={{0,17},{1,16},{2,19},{3,18},{4,21},{5,20},{6,23},{7,22},{8,25},{9,... | collective-permute-start | bytes 98312 | tf_op jit(solution)/shard_map/ppermute | solution.py:42
  43.6 0.0 collective-permute-done.9.more_ref
  43.6 1.9 %collective-permute-start.10 = (bf16[8,2048]{1,0:T(8,128)(2,1)S(1)}, bf16[8,2048]{1,0:T(8,128)(2,1)S(1)}, u32[]{:S(2)}, u32[]{:S(2)}) collective-permute-start(bf16[8,2048]{1,0:T(8,128)(2,1)S(1)} %get-tuple-element.27), channel_id=1, source_target_pairs={{0,25},{1,24},{2,27},{3,26},{4,29},{5,28},{6,31},{7,30},{8,17},{9,... | collective-permute-start | bytes 98312 | tf_op jit(solution)/shard_map/ppermute | solution.py:42
  45.5 0.6 %copy.13 = bf16[8,2048]{1,0:T(8,128)(2,1)} copy(bf16[8,2048]{1,0:T(8,128)(2,1)S(1)} %get-tuple-element.34) | data formatting | bytes 65536
  46.1 0.0 collective-permute-done.18
  46.1 0.0 collective-permute-done.17
  46.1 2.7 %collective-permute-done.10 = bf16[8,2048]{1,0:T(8,128)(2,1)S(1)} collective-permute-done((bf16[8,2048]{1,0:T(8,128)(2,1)S(1)}, bf16[8,2048]{1,0:T(8,128)(2,1)S(1)}, u32[]{:S(2)}, u32[]{:S(2)}) %collective-permute-start.10) | collective-permute-done | bytes 32800 | tf_op jit(solution)/shard_map/ppermute | solution.py:42
  48.8 0.6 %add_convert_fusion = bf16[8,2048]{1,0:T(8,128)(2,1)} fusion(bf16[8,2048]{1,0:T(8,128)(2,1)S(1)} %collective-permute-done.18, bf16[8,2048]{1,0:T(8,128)(2,1)S(1)} %collective-permute-done.17, f32[8,2048]{1,0:T(8,128)S(1)} %get-tuple-element.26, bf16[8,2048]{1,0:T(8,128)(2,1)S(1)} %collective-permute-done.10), kind=kLoop, calls=%fused_computation | loop fusion | flops 114688 | bytes 196608 | tf_op jit(solution)/shard_map/convert_element_type | solution.py:441
  (4 shorter events, 0.1 us)
Async XLA Ops:
  0.6 8.6 %collective-permute-start.1 = (bf16[1024,2048]{1,0:T(8,128)(2,1)}, bf16[1024,2048]{1,0:T(8,128)(2,1)S(1)}, u32[]{:S(2)}, u32[]{:S(2)}) collective-permute-start(bf16[1024,2048]{1,0:T(8,128)(2,1)} %refs_2_.1), channel_id=1, source_target_pairs={{0,1},{1,0},{2,3},{3,2},{4,5},{5,4},{6,7},{7,6},{8,9},{9,8},{10,11... | collective-permute-start | bytes 12582920 | tf_op jit(solution)/shard_map/ppermute | solution.py:35
  1.2 25.1 %collective-permute-start.6 = (bf16[2048,768]{1,0:T(8,128)(2,1)}, bf16[2048,768]{1,0:T(8,128)(2,1)S(1)}, u32[]{:S(2)}, u32[]{:S(2)}) collective-permute-start(bf16[2048,768]{1,0:T(8,128)(2,1)} %bitcast.3), channel_id=1, source_target_pairs={{0,1},{1,0},{2,3},{3,2},{4,5},{5,4},{6,7},{7,6},{8,9},{9,8},{10,11... | collective-permute-start | bytes 9437192 | tf_op jit(solution)/shard_map/ppermute | solution.py:35
  1.3 8.0 %copy-start.2 = (bf16[1024,2048]{1,0:T(8,128)(2,1)S(1)}, bf16[1024,2048]{1,0:T(8,128)(2,1)}, u32[]{:S(2)}) copy-start(bf16[1024,2048]{1,0:T(8,128)(2,1)} %refs_2_.1) | copy-start | bytes 12582916
  1.3 8.0 %copy-start.3 = (bf16[8,2048]{1,0:T(8,128)(2,1)S(1)}, bf16[8,2048]{1,0:T(8,128)(2,1)}, u32[]{:S(2)}) copy-start(bf16[8,2048]{1,0:T(8,128)(2,1)} %refs_4_.1) | copy-start | bytes 98308
  1.3 8.0 %copy-start.5 = (s32[8,8]{1,0:T(8,128)S(1)}, s32[8,8]{1,0:T(8,128)}, u32[]{:S(2)}) copy-start(s32[8,8]{1,0:T(8,128)} %refs_5_.1) | copy-start | bytes 772
  1.3 8.0 %copy-start.6 = (s32[8,8]{1,0:T(8,128)S(1)}, s32[8,8]{1,0:T(8,128)}, u32[]{:S(2)}) copy-start(s32[8,8]{1,0:T(8,128)} %refs_6_.1) | copy-start | bytes 772
  1.3 22.0 %collective-permute-start.7 = (bf16[384,2048]{1,0:T(8,128)(2,1)}, bf16[384,2048]{1,0:T(8,128)(2,1)S(1)}, u32[]{:S(2)}, u32[]{:S(2)}) collective-permute-start(bf16[384,2048]{1,0:T(8,128)(2,1)} %bitcast.6), channel_id=1, source_target_pairs={{0,1},{1,0},{2,3},{3,2},{4,5},{5,4},{6,7},{7,6},{8,9},{9,8},{10,11... | collective-permute-start | bytes 4718600 | tf_op jit(solution)/shard_map/ppermute | solution.py:35
  4.3 4.9 %collective-permute-start = (bf16[1,8,2048]{2,1,0:T(8,128)(2,1)S(1)}, bf16[1,8,2048]{2,1,0:T(8,128)(2,1)S(1)}, u32[]{:S(2)}, u32[]{:S(2)}) collective-permute-start(bf16[1,8,2048]{2,1,0:T(8,128)(2,1)S(1)} %shard_map.123), channel_id=1, source_target_pairs={{0,3},{1,2},{2,1},{3,0},{4,7},{5,6},{6,5},{7,4},{8,11},{9,10},{10,... | collective-permute-start | bytes 98312 | tf_op jit(solution)/shard_map/ppermute | solution.py:42
  9.2 5.5 %copy-start.4 = (f32[2048]{0:T(1024)S(1)}, f32[2048]{0:T(1024)}, u32[]{:S(2)}) copy-start(f32[2048]{0:T(1024)} %param.17) | copy-start | bytes 24580
  9.2 18.1 %copy-start = (bf16[1,2048,768]{2,1,0:T(8,128)(2,1)S(1)}, bf16[1,2048,768]{2,1,0:T(8,128)(2,1)}, u32[]{:S(2)}) copy-start(bf16[1,2048,768]{2,1,0:T(8,128)(2,1)} %param.20) | copy-start | bytes 9437188
  9.2 18.1 %copy-start.1 = (bf16[1,384,2048]{2,1,0:T(8,128)(2,1)S(1)}, bf16[1,384,2048]{2,1,0:T(8,128)(2,1)}, u32[]{:S(2)}) copy-start(bf16[1,384,2048]{2,1,0:T(8,128)(2,1)} %param.21) | copy-start | bytes 4718596
  10.5 4.2 %collective-permute-start.2 = (bf16[16,2176]{1,0:T(8,128)(2,1)S(1)}, bf16[16,2176]{1,0:T(8,128)(2,1)S(1)}, u32[]{:S(2)}, u32[]{:S(2)}) collective-permute-start(bf16[16,2176]{1,0:T(8,128)(2,1)S(1)} %get-tuple-element.19), channel_id=1, source_target_pairs={{0,3},{1,2},{2,1},{3,0},{4,7},{5,6},{6,5},{7,4},{8,11},{9,10},{10,... | collective-permute-start | bytes 208904 | tf_op jit(solution)/shard_map/ppermute | solution.py:42
  14.8 5.1 %collective-permute-start.11 = (bf16[16,2176]{1,0:T(8,128)(2,1)S(1)}, bf16[16,2176]{1,0:T(8,128)(2,1)S(1)}, u32[]{:S(2)}, u32[]{:S(2)}) collective-permute-start(bf16[16,2176]{1,0:T(8,128)(2,1)S(1)} %get-tuple-element.21.refs_0_), channel_id=1, source_target_pairs={{0,17},{1,16},{2,19},{3,18},{4,21},{5,20},{6,23},{7,22},{8,25},{9,... | collective-permute-start | bytes 208904 | tf_op jit(solution)/shard_map/ppermute | solution.py:42
  17.5 5.6 %collective-permute-start.12 = (bf16[16,2176]{1,0:T(8,128)(2,1)S(1)}, bf16[16,2176]{1,0:T(8,128)(2,1)S(1)}, u32[]{:S(2)}, u32[]{:S(2)}) collective-permute-start(bf16[16,2176]{1,0:T(8,128)(2,1)S(1)} %get-tuple-element.21.refs_0_), channel_id=1, source_target_pairs={{0,9},{1,8},{2,11},{3,10},{4,13},{5,12},{6,15},{7,14},{8,1},{9,0},... | collective-permute-start | bytes 208904 | tf_op jit(solution)/shard_map/ppermute | solution.py:42
  19.0 6.0 %collective-permute-start.3 = (bf16[16,2176]{1,0:T(8,128)(2,1)S(1)}, bf16[16,2176]{1,0:T(8,128)(2,1)S(1)}, u32[]{:S(2)}, u32[]{:S(2)}) collective-permute-start(bf16[16,2176]{1,0:T(8,128)(2,1)S(1)} %get-tuple-element.21.refs_0_), channel_id=1, source_target_pairs={{0,25},{1,24},{2,27},{3,26},{4,29},{5,28},{6,31},{7,30},{8,17},{9,... | collective-permute-start | bytes 208904 | tf_op jit(solution)/shard_map/ppermute | solution.py:42
  19.9 6.4 %collective-permute-start.13 = (bf16[16,2176]{1,0:T(8,128)(2,1)S(1)}, bf16[16,2176]{1,0:T(8,128)(2,1)S(1)}, u32[]{:S(2)}, u32[]{:S(2)}) collective-permute-start(bf16[16,2176]{1,0:T(8,128)(2,1)S(1)} %collective-permute-done.11.refs_0_), channel_id=1, source_target_pairs={{0,5},{1,4},{2,7},{3,6},{4,1},{5,0},{6,3},{7,2},{8,13},{9,12},{10,... | collective-permute-start | bytes 208904 | tf_op jit(solution)/shard_map/ppermute | solution.py:42
  23.1 4.2 %collective-permute-start.14 = (bf16[16,2176]{1,0:T(8,128)(2,1)S(1)}, bf16[16,2176]{1,0:T(8,128)(2,1)S(1)}, u32[]{:S(2)}, u32[]{:S(2)}) collective-permute-start(bf16[16,2176]{1,0:T(8,128)(2,1)S(1)} %collective-permute-done.12.refs_1_), channel_id=1, source_target_pairs={{0,5},{1,4},{2,7},{3,6},{4,1},{5,0},{6,3},{7,2},{8,13},{9,12},{10,... | collective-permute-start | bytes 208904 | tf_op jit(solution)/shard_map/ppermute | solution.py:42
  23.3 7.7 %collective-permute-start.4 = (bf16[16,2176]{1,0:T(8,128)(2,1)S(1)}, bf16[16,2176]{1,0:T(8,128)(2,1)S(1)}, u32[]{:S(2)}, u32[]{:S(2)}) collective-permute-start(bf16[16,2176]{1,0:T(8,128)(2,1)S(1)} %get-tuple-element.21.refs_0_), channel_id=1, source_target_pairs={{0,5},{1,4},{2,7},{3,6},{4,1},{5,0},{6,3},{7,2},{8,13},{9,12},{10,... | collective-permute-start | bytes 208904 | tf_op jit(solution)/shard_map/ppermute | solution.py:42
  25.0 6.0 %collective-permute-start.5 = (bf16[16,2176]{1,0:T(8,128)(2,1)S(1)}, bf16[16,2176]{1,0:T(8,128)(2,1)S(1)}, u32[]{:S(2)}, u32[]{:S(2)}) collective-permute-start(bf16[16,2176]{1,0:T(8,128)(2,1)S(1)} %collective-permute-done.3.refs_1_), channel_id=1, source_target_pairs={{0,5},{1,4},{2,7},{3,6},{4,1},{5,0},{6,3},{7,2},{8,13},{9,12},{10,... | collective-permute-start | bytes 208904 | tf_op jit(solution)/shard_map/ppermute | solution.py:42
  29.2 4.5 %collective-permute-start.15 = (bf16[32,2048]{1,0:T(8,128)(2,1)S(1)}, bf16[32,2048]{1,0:T(8,128)(2,1)S(1)}, u32[]{:S(2)}, u32[]{:S(2)}) collective-permute-start(bf16[32,2048]{1,0:T(8,128)(2,1)S(1)} %get-tuple-element.29), channel_id=1, source_target_pairs={{0,3},{1,4},{2,7},{3,0},{4,1},{5,6},{6,5},{7,2},{8,11},{9,12},{10,... | collective-permute-start | bytes 393224 | tf_op jit(solution)/shard_map/ppermute | solution.py:60
  32.8 4.5 %collective-permute-start.8 = (bf16[32,2048]{1,0:T(8,128)(2,1)S(1)}, bf16[32,2048]{1,0:T(8,128)(2,1)S(1)}, u32[]{:S(2)}, u32[]{:S(2)}) collective-permute-start(bf16[32,2048]{1,0:T(8,128)(2,1)S(1)} %get-tuple-element.23), channel_id=1, source_target_pairs={{0,3},{1,4},{2,7},{3,0},{4,1},{5,6},{6,5},{7,2},{8,11},{9,12},{10,... | collective-permute-start | bytes 393224 | tf_op jit(solution)/shard_map/ppermute | solution.py:60
  33.7 4.3 %collective-permute-start.16 = (bf16[16,2048]{1,0:T(8,128)(2,1)S(1)}, bf16[16,2048]{1,0:T(8,128)(2,1)S(1)}, u32[]{:S(2)}, u32[]{:S(2)}) collective-permute-start(bf16[16,2048]{1,0:T(8,128)(2,1)S(1)} %get-tuple-element.31), channel_id=1, source_target_pairs={{0,5},{1,2},{2,1},{3,6},{4,7},{5,0},{6,3},{7,4},{8,13},{9,10},{10,... | collective-permute-start | bytes 196616 | tf_op jit(solution)/shard_map/ppermute | solution.py:60
  37.3 6.2 %collective-permute-start.9 = (bf16[16,2048]{1,0:T(8,128)(2,1)S(1)}, bf16[16,2048]{1,0:T(8,128)(2,1)S(1)}, u32[]{:S(2)}, u32[]{:S(2)}) collective-permute-start(bf16[16,2048]{1,0:T(8,128)(2,1)S(1)} %get-tuple-element.25), channel_id=1, source_target_pairs={{0,5},{1,2},{2,1},{3,6},{4,7},{5,0},{6,3},{7,4},{8,13},{9,10},{10,... | collective-permute-start | bytes 196616 | tf_op jit(solution)/shard_map/ppermute | solution.py:60
  38.0 8.1 %collective-permute-start.18 = (bf16[8,2048]{1,0:T(8,128)(2,1)S(1)}, bf16[8,2048]{1,0:T(8,128)(2,1)S(1)}, u32[]{:S(2)}, u32[]{:S(2)}) collective-permute-start(bf16[8,2048]{1,0:T(8,128)(2,1)S(1)} %get-tuple-element.33), channel_id=1, source_target_pairs={{0,9},{1,8},{2,11},{3,10},{4,13},{5,12},{6,15},{7,14},{8,1},{9,0},... | collective-permute-start | bytes 98312 | tf_op jit(solution)/shard_map/ppermute | solution.py:42
  39.6 6.6 %collective-permute-start.17 = (bf16[8,2048]{1,0:T(8,128)(2,1)S(1)}, bf16[8,2048]{1,0:T(8,128)(2,1)S(1)}, u32[]{:S(2)}, u32[]{:S(2)}) collective-permute-start(bf16[8,2048]{1,0:T(8,128)(2,1)S(1)} %get-tuple-element.32), channel_id=1, source_target_pairs={{0,17},{1,16},{2,19},{3,18},{4,21},{5,20},{6,23},{7,22},{8,25},{9,... | collective-permute-start | bytes 98312 | tf_op jit(solution)/shard_map/ppermute | solution.py:42
  43.6 5.2 %collective-permute-start.10 = (bf16[8,2048]{1,0:T(8,128)(2,1)S(1)}, bf16[8,2048]{1,0:T(8,128)(2,1)S(1)}, u32[]{:S(2)}, u32[]{:S(2)}) collective-permute-start(bf16[8,2048]{1,0:T(8,128)(2,1)S(1)} %get-tuple-element.27), channel_id=1, source_target_pairs={{0,25},{1,24},{2,27},{3,26},{4,29},{5,28},{6,31},{7,30},{8,17},{9,... | collective-permute-start | bytes 98312 | tf_op jit(solution)/shard_map/ppermute | solution.py:42

commit v5 on v4

--- a/solution.py
+++ b/solution.py
@@ -300,7 +300,7 @@
     stream_ref[...] = stream[:rows].astype(jnp.bfloat16)
 
 
-def expert_kernel(rows, *refs):
+def expert_kernel(rows, turn, *refs):
     kept_ref, sent_ref, result = refs[-3:]
     in_own, in_other, down_own, down_other = refs[-7:-3]
     blocks = refs[:-7]
@@ -323,7 +323,7 @@
         hidden[1], down_other[...], preferred_element_type=jnp.float32
     )
     result[...] = total * share
-    kind = device_class(lax.axis_index("dev"), lax.axis_index("side"))
+    kind = device_class(lax.axis_index("dev"), lax.axis_index("side")) ^ turn
     nearby = len(blocks) // 2
     slots = 2 * nearby * chips
     for slot in range(slots):
@@ -340,11 +340,11 @@
             sent_ref[to : to + rows, :] = piece.astype(jnp.bfloat16)
 
 
-def run_experts(blocks, weights, rows, width):
+def run_experts(name, blocks, weights, rows, width):
     count = sum(block.shape[0] for block in blocks)
     shape = (count // 2, width)
     return kernel_call(
-        functools.partial(expert_kernel, rows),
+        functools.partial(expert_kernel, rows, int(name == "experts_late")),
         (*blocks, *weights),
         (jax.ShapeDtypeStruct(shape, jnp.float32), jax.ShapeDtypeStruct(shape, jnp.bfloat16)),
         scratch=[pltpu.VMEM((count, width), jnp.float32)],
@@ -365,13 +365,15 @@
     return kernel_call(merge_kernel, (kept, more), outs)
 
 
-def homeward(kept, sent, aways, rows):
+def homeward(kept, sent, group, aways, rows):
     over_side = []
     chips = lax.axis_size("side") // 2
     while chips > 1:
         chips //= 2
         over_side.append((0, chips))
     first, second = over_side + [(1, 0)], [(1, 0)] + over_side
+    if group == "late":
+        first, second = second, first
     for step, distances in enumerate(zip(first, second)):
         more = apart(sent, distances)
         half = kept.shape[0] // 2
@@ -429,11 +431,11 @@
         if away:
             near[away] = across(normed, away, 0)
     home = []
-    for aways in (early, late):
+    for group, aways in (("early", early), ("late", late)):
         blocks = [near[away] for away in aways]
         blocks += [across(near[away], 1, 0) for away in aways]
-        kept, sent = run_experts(blocks, weights, rows, width)
-        for away, block in zip(aways, homeward(kept, sent, aways, rows)):
+        kept, sent = run_experts(f"experts_{group}", blocks, weights, rows, width)
+        for away, block in zip(aways, homeward(kept, sent, group, aways, rows)):
             if away:
                 block = across(block, away, 0).astype(jnp.float32)
             home.append(block)

time: 49.6 us -> 48.8 us (0.984)
  starting transfers between devices: 28.3 us -> 27.4 us
    ppermute x4, waiting for transfers between devices: 1.76 us -> 2.79 us  [apart(): return lax.ppermute(block, ('dev', 'side'), route)]
    ppermute x12, waiting for transfers between devices: 7.42 us -> 6.53 us  [across(): lax.ppermute(block, ('dev', 'side'), [(i, i ^ mask) for i in range(count)])]
    ppermute x4, starting transfers between devices: 5.09 us -> 4.41 us  [apart(): return lax.ppermute(block, ('dev', 'side'), route)]
  transfers between devices with their start and end apart: 19 -> 19, of which waited for: 7 -> 8; matrix products, arithmetic and copies ran while one was open for 1% -> 1% of each run, Pallas kernels for 20% -> 20%
where the time goes in v5:
time: 48.8 us; the launch traced here: 48.7 us
  starting transfers between devices  27.4 us (56%)
  Pallas kernels  9.88 us (20%)
  waiting for transfers between devices  9.33 us (19%)
  between operations  0.77 us (2%)
  local copies, waits for them, and re-layouts  0.65 us (1%)
  other arithmetic  0.63 us (1%)
    ppermute x12, starting transfers between devices, across(): lax.ppermute(block, ('dev', 'side'), [(i, i ^ mask) for i in range(count)])  21.9 us
    pallas_call x10, Pallas kernels, kernel_call(): pl.pallas_call(body, out_shape=outs, in_specs=in_specs or [VMEM] * len(op...  9.88 us
    ppermute x12, waiting for transfers between devices, across(): lax.ppermute(block, ('dev', 'side'), [(i, i ^ mask) for i in range(count)])  6.53 us
    ppermute x4, starting transfers between devices, apart(): return lax.ppermute(block, ('dev', 'side'), route)  4.41 us
    ppermute x4, waiting for transfers between devices, apart(): return lax.ppermute(block, ('dev', 'side'), route)  2.79 us
    ppermute x3, starting transfers between devices, partner(): return lax.ppermute(block, axis, [(i, i ^ mask) for i in range(count)])  1.13 us
  transfers between devices with their start and end apart: 19, of which 8 were waited for; matrix products, arithmetic and copies ran while one was open for 1% of the time, Pallas kernels for 20%

profile of v5, /device:TPU:0, one launch (start us, length us, event | category | flops | bytes accessed | tf_op | source)
XLA Modules:
  0.0 48.7 jit_solution(13465910798643429905)
XLA Ops:
  0.6 0.6 %collective-permute-start.1 = (bf16[1024,2048]{1,0:T(8,128)(2,1)}, bf16[1024,2048]{1,0:T(8,128)(2,1)S(1)}, u32[]{:S(2)}, u32[]{:S(2)}) collective-permute-start(bf16[1024,2048]{1,0:T(8,128)(2,1)} %refs_2_.1), channel_id=1, source_target_pairs={{0,1},{1,0},{2,3},{3,2},{4,5},{5,4},{6,7},{7,6},{8,9},{9,8},{10,11... | collective-permute-start | bytes 12582920 | tf_op jit(solution)/shard_map/ppermute | solution.py:35
  1.2 0.1 collective-permute-start.6
  1.3 0.0 copy-start.2
  1.3 0.0 copy-start.3
  1.3 0.0 copy-start.5
  1.3 0.0 copy-start.6
  1.3 0.5 %collective-permute-start.7 = (bf16[384,2048]{1,0:T(8,128)(2,1)}, bf16[384,2048]{1,0:T(8,128)(2,1)S(1)}, u32[]{:S(2)}, u32[]{:S(2)}) collective-permute-start(bf16[384,2048]{1,0:T(8,128)(2,1)} %bitcast.6), channel_id=1, source_target_pairs={{0,1},{1,0},{2,3},{3,2},{4,5},{5,4},{6,7},{7,6},{8,9},{9,8},{10,11... | collective-permute-start | bytes 4718600 | tf_op jit(solution)/shard_map/ppermute | solution.py:35
  1.8 2.5 %shard_map.123 = bf16[1,8,2048]{2,1,0:T(8,128)(2,1)S(1)} custom-call(bf16[8,4096]{1,0:T(8,128)(2,1)} %q_hbm.3, bf16[8,192,1024]{2,1,0:T(8,128)(2,1)} %kv_hbm.3, bf16[8,1024]{1,0:T(8,128)(2,1)} %new_hbm.3, s32[8]{0:T(128)} %length_hbm.3), custom_call_target="tpu_custom_call" | custom-call | flops 8388608 | bytes 6291456 | tf_op jit(solution)/shard_map/pallas_call | solution.py:18
  4.3 2.7 %collective-permute-start = (bf16[1,8,2048]{2,1,0:T(8,128)(2,1)S(1)}, bf16[1,8,2048]{2,1,0:T(8,128)(2,1)S(1)}, u32[]{:S(2)}, u32[]{:S(2)}) collective-permute-start(bf16[1,8,2048]{2,1,0:T(8,128)(2,1)S(1)} %shard_map.123), channel_id=1, source_target_pairs={{0,3},{1,2},{2,1},{3,0},{4,7},{5,6},{6,5},{7,4},{8,11},{9,10},{10,... | collective-permute-start | bytes 98312 | tf_op jit(solution)/shard_map/ppermute | solution.py:42
  6.9 2.2 %shard_map.122.refs_0_ = bf16[1,8,2048]{2,1,0:T(8,128)(2,1)S(1)} custom-call(bf16[8,4096]{1,0:T(8,128)(2,1)} %q_hbm.3, bf16[8,192,1024]{2,1,0:T(8,128)(2,1)} %kv_hbm.3, bf16[8,1024]{1,0:T(8,128)(2,1)} %new_hbm.3, s32[8]{0:T(128)} %length_hbm.3), custom_call_target="tpu_custom_call" | custom-call | flops 8388608 | bytes 6291456 | tf_op jit(solution)/shard_map/pallas_call | solution.py:18
  9.2 0.0 copy-start.4
  9.2 0.0 copy-start
  9.2 0.0 copy-start.1
  9.2 0.0 collective-permute-done.refs_1_
  9.2 0.0 collective-permute-done.1.refs_3_
  9.2 0.0 copy-done.2
  9.3 0.0 copy-done.3
  9.3 0.0 copy-done.5
  9.3 0.0 copy-done.6
  9.3 1.2 %shard_map.124 = (f32[16,2176]{1,0:T(8,128)S(1)}, bf16[16,2176]{1,0:T(8,128)(2,1)S(1)}) custom-call(bf16[1,8,2048]{2,1,0:T(8,128)(2,1)S(1)} %shard_map.122.refs_0_, bf16[1,8,2048]{2,1,0:T(8,128)(2,1)S(1)} %collective-permute-done.refs_1_, bf16[1024,2048]{1,0:T(8,128)(2,1)S(1)} %copy-done.2, bf16[1024,2048]{1,0:T(8,128)(2,1)S(1)} %collective-permute-done.1.refs_3_, ...), custom_call_target="tpu_custom_call" | custom-call | tf_op jit(solution)/shard_map/pallas_call | solution.py:18
  10.5 1.5 %collective-permute-start.2 = (bf16[16,2176]{1,0:T(8,128)(2,1)S(1)}, bf16[16,2176]{1,0:T(8,128)(2,1)S(1)}, u32[]{:S(2)}, u32[]{:S(2)}) collective-permute-start(bf16[16,2176]{1,0:T(8,128)(2,1)S(1)} %get-tuple-element.19), channel_id=1, source_target_pairs={{0,3},{1,2},{2,1},{3,0},{4,7},{5,6},{6,5},{7,4},{8,11},{9,10},{10,... | collective-permute-start | bytes 208904 | tf_op jit(solution)/shard_map/ppermute | solution.py:42
  12.0 2.7 %collective-permute-done.2.more_ref = bf16[16,2176]{1,0:T(8,128)(2,1)S(1)} collective-permute-done((bf16[16,2176]{1,0:T(8,128)(2,1)S(1)}, bf16[16,2176]{1,0:T(8,128)(2,1)S(1)}, u32[]{:S(2)}, u32[]{:S(2)}) %collective-permute-start.2) | collective-permute-done | bytes 69664 | tf_op jit(solution)/shard_map/ppermute | solution.py:42
  14.7 0.0 copy-done.4
  14.7 0.1 shard_map.125
  14.8 2.7 %collective-permute-start.11 = (bf16[16,2176]{1,0:T(8,128)(2,1)S(1)}, bf16[16,2176]{1,0:T(8,128)(2,1)S(1)}, u32[]{:S(2)}, u32[]{:S(2)}) collective-permute-start(bf16[16,2176]{1,0:T(8,128)(2,1)S(1)} %get-tuple-element.21.refs_0_), channel_id=1, source_target_pairs={{0,17},{1,16},{2,19},{3,18},{4,21},{5,20},{6,23},{7,22},{8,25},{9,... | collective-permute-start | bytes 208904 | tf_op jit(solution)/shard_map/ppermute | solution.py:42
  17.5 1.6 %collective-permute-start.12 = (bf16[16,2176]{1,0:T(8,128)(2,1)S(1)}, bf16[16,2176]{1,0:T(8,128)(2,1)S(1)}, u32[]{:S(2)}, u32[]{:S(2)}) collective-permute-start(bf16[16,2176]{1,0:T(8,128)(2,1)S(1)} %get-tuple-element.21.refs_0_), channel_id=1, source_target_pairs={{0,9},{1,8},{2,11},{3,10},{4,13},{5,12},{6,15},{7,14},{8,1},{9,0},... | collective-permute-start | bytes 208904 | tf_op jit(solution)/shard_map/ppermute | solution.py:42
  19.0 0.0 collective-permute-start.3
  19.0 0.9 %collective-permute-done.11.refs_0_ = bf16[16,2176]{1,0:T(8,128)(2,1)S(1)} collective-permute-done((bf16[16,2176]{1,0:T(8,128)(2,1)S(1)}, bf16[16,2176]{1,0:T(8,128)(2,1)S(1)}, u32[]{:S(2)}, u32[]{:S(2)}) %collective-permute-start.11) | collective-permute-done | bytes 69664 | tf_op jit(solution)/shard_map/ppermute | solution.py:42
  19.9 3.2 %collective-permute-start.13 = (bf16[16,2176]{1,0:T(8,128)(2,1)S(1)}, bf16[16,2176]{1,0:T(8,128)(2,1)S(1)}, u32[]{:S(2)}, u32[]{:S(2)}) collective-permute-start(bf16[16,2176]{1,0:T(8,128)(2,1)S(1)} %collective-permute-done.11.refs_0_), channel_id=1, source_target_pairs={{0,5},{1,4},{2,7},{3,6},{4,1},{5,0},{6,3},{7,2},{8,13},{9,12},{10,... | collective-permute-start | bytes 208904 | tf_op jit(solution)/shard_map/ppermute | solution.py:42
  23.1 0.0 collective-permute-done.12.refs_1_
  23.1 0.2 collective-permute-start.14
  23.3 0.0 collective-permute-done.7.refs_7_
  23.3 1.5 %collective-permute-start.4 = (bf16[16,2176]{1,0:T(8,128)(2,1)S(1)}, bf16[16,2176]{1,0:T(8,128)(2,1)S(1)}, u32[]{:S(2)}, u32[]{:S(2)}) collective-permute-start(bf16[16,2176]{1,0:T(8,128)(2,1)S(1)} %get-tuple-element.21.refs_0_), channel_id=1, source_target_pairs={{0,5},{1,4},{2,7},{3,6},{4,1},{5,0},{6,3},{7,2},{8,13},{9,12},{10,... | collective-permute-start | bytes 208904 | tf_op jit(solution)/shard_map/ppermute | solution.py:42
  24.8 0.2 collective-permute-done.3.refs_1_
  25.0 1.3 %collective-permute-start.5 = (bf16[16,2176]{1,0:T(8,128)(2,1)S(1)}, bf16[16,2176]{1,0:T(8,128)(2,1)S(1)}, u32[]{:S(2)}, u32[]{:S(2)}) collective-permute-start(bf16[16,2176]{1,0:T(8,128)(2,1)S(1)} %collective-permute-done.3.refs_1_), channel_id=1, source_target_pairs={{0,5},{1,4},{2,7},{3,6},{4,1},{5,0},{6,3},{7,2},{8,13},{9,12},{10,... | collective-permute-start | bytes 208904 | tf_op jit(solution)/shard_map/ppermute | solution.py:42
  26.2 0.0 collective-permute-done.6.refs_5_
  26.2 0.0 collective-permute-done.13.refs_2_
  26.3 1.0 %collective-permute-done.14.refs_3_ = bf16[16,2176]{1,0:T(8,128)(2,1)S(1)} collective-permute-done((bf16[16,2176]{1,0:T(8,128)(2,1)S(1)}, bf16[16,2176]{1,0:T(8,128)(2,1)S(1)}, u32[]{:S(2)}, u32[]{:S(2)}) %collective-permute-start.14) | collective-permute-done | bytes 69664 | tf_op jit(solution)/shard_map/ppermute | solution.py:42
  27.3 0.0 copy-done
  27.3 0.0 copy-done.1
  27.3 1.9 %shard_map.129 = (f32[32,2048]{1,0:T(8,128)S(1)}, bf16[32,2048]{1,0:T(8,128)(2,1)S(1)}) custom-call(bf16[16,2176]{1,0:T(8,128)(2,1)S(1)} %collective-permute-done.11.refs_0_, bf16[16,2176]{1,0:T(8,128)(2,1)S(1)} %collective-permute-done.12.refs_1_, bf16[16,2176]{1,0:T(8,128)(2,1)S(1)} %collective-permute-done.13.refs_2_, ...), custom_call_target="tpu_custom_call" | custom-call | flops 1073741824 | bytes 4194304 | tf_op jit(solution)/shard_map/pallas_call | solution.py:18
  29.2 2.1 %collective-permute-start.15 = (bf16[32,2048]{1,0:T(8,128)(2,1)S(1)}, bf16[32,2048]{1,0:T(8,128)(2,1)S(1)}, u32[]{:S(2)}, u32[]{:S(2)}) collective-permute-start(bf16[32,2048]{1,0:T(8,128)(2,1)S(1)} %get-tuple-element.29), channel_id=1, source_target_pairs={{0,5},{1,2},{2,1},{3,6},{4,7},{5,0},{6,3},{7,4},{8,13},{9,10},{10,... | collective-permute-start | bytes 393224 | tf_op jit(solution)/shard_map/ppermute | solution.py:60
  31.3 0.0 collective-permute-done.4.refs_2_
  31.3 0.0 collective-permute-done.5.refs_3_
  31.3 1.9 %shard_map.126 = (f32[32,2048]{1,0:T(8,128)S(1)}, bf16[32,2048]{1,0:T(8,128)(2,1)S(1)}) custom-call(bf16[16,2176]{1,0:T(8,128)(2,1)S(1)} %get-tuple-element.21.refs_0_, bf16[16,2176]{1,0:T(8,128)(2,1)S(1)} %collective-permute-done.3.refs_1_, bf16[16,2176]{1,0:T(8,128)(2,1)S(1)} %collective-permute-done.4.refs_2_, ...), custom_call_target="tpu_custom_call" | custom-call | flops 1073741824 | bytes 4194304 | tf_op jit(solution)/shard_map/pallas_call | solution.py:18
  33.1 0.3 collective-permute-start.8
  33.5 0.5 collective-permute-done.15.more_ref
  34.0 1.5 %collective-permute-start.16 = (bf16[16,2048]{1,0:T(8,128)(2,1)S(1)}, bf16[16,2048]{1,0:T(8,128)(2,1)S(1)}, u32[]{:S(2)}, u32[]{:S(2)}) collective-permute-start(bf16[16,2048]{1,0:T(8,128)(2,1)S(1)} %get-tuple-element.31), channel_id=1, source_target_pairs={{0,3},{1,4},{2,7},{3,0},{4,1},{5,6},{6,5},{7,2},{8,11},{9,12},{10,... | collective-permute-start | bytes 196616 | tf_op jit(solution)/shard_map/ppermute | solution.py:60
  35.5 2.1 %collective-permute-done.8.more_ref = bf16[32,2048]{1,0:T(8,128)(2,1)S(1)} collective-permute-done((bf16[32,2048]{1,0:T(8,128)(2,1)S(1)}, bf16[32,2048]{1,0:T(8,128)(2,1)S(1)}, u32[]{:S(2)}, u32[]{:S(2)}) %collective-permute-start.8) | collective-permute-done | bytes 131104 | tf_op jit(solution)/shard_map/ppermute | solution.py:60
  37.6 0.5 %collective-permute-start.9 = (bf16[16,2048]{1,0:T(8,128)(2,1)S(1)}, bf16[16,2048]{1,0:T(8,128)(2,1)S(1)}, u32[]{:S(2)}, u32[]{:S(2)}) collective-permute-start(bf16[16,2048]{1,0:T(8,128)(2,1)S(1)} %get-tuple-element.25), channel_id=1, source_target_pairs={{0,5},{1,2},{2,1},{3,6},{4,7},{5,0},{6,3},{7,4},{8,13},{9,10},{10,... | collective-permute-start | bytes 196616 | tf_op jit(solution)/shard_map/ppermute | solution.py:60
  38.1 0.2 collective-permute-done.16.more_ref
  38.3 0.9 %collective-permute-start.18 = (bf16[8,2048]{1,0:T(8,128)(2,1)S(1)}, bf16[8,2048]{1,0:T(8,128)(2,1)S(1)}, u32[]{:S(2)}, u32[]{:S(2)}) collective-permute-start(bf16[8,2048]{1,0:T(8,128)(2,1)S(1)} %get-tuple-element.33), channel_id=1, source_target_pairs={{0,9},{1,8},{2,11},{3,10},{4,13},{5,12},{6,15},{7,14},{8,1},{9,0},... | collective-permute-start | bytes 98312 | tf_op jit(solution)/shard_map/ppermute | solution.py:42
  39.3 3.5 %collective-permute-start.17 = (bf16[8,2048]{1,0:T(8,128)(2,1)S(1)}, bf16[8,2048]{1,0:T(8,128)(2,1)S(1)}, u32[]{:S(2)}, u32[]{:S(2)}) collective-permute-start(bf16[8,2048]{1,0:T(8,128)(2,1)S(1)} %get-tuple-element.32), channel_id=1, source_target_pairs={{0,17},{1,16},{2,19},{3,18},{4,21},{5,20},{6,23},{7,22},{8,25},{9,... | collective-permute-start | bytes 98312 | tf_op jit(solution)/shard_map/ppermute | solution.py:42
  42.8 0.0 collective-permute-done.9.more_ref
  42.8 2.8 %collective-permute-start.10 = (bf16[8,2048]{1,0:T(8,128)(2,1)S(1)}, bf16[8,2048]{1,0:T(8,128)(2,1)S(1)}, u32[]{:S(2)}, u32[]{:S(2)}) collective-permute-start(bf16[8,2048]{1,0:T(8,128)(2,1)S(1)} %get-tuple-element.27), channel_id=1, source_target_pairs={{0,25},{1,24},{2,27},{3,26},{4,29},{5,28},{6,31},{7,30},{8,17},{9,... | collective-permute-start | bytes 98312 | tf_op jit(solution)/shard_map/ppermute | solution.py:42
  45.6 0.6 %copy.13 = bf16[8,2048]{1,0:T(8,128)(2,1)} copy(bf16[8,2048]{1,0:T(8,128)(2,1)S(1)} %get-tuple-element.34) | data formatting | bytes 65536
  46.2 0.0 collective-permute-done.18
  46.2 0.0 collective-permute-done.17
  46.2 1.8 %collective-permute-done.10 = bf16[8,2048]{1,0:T(8,128)(2,1)S(1)} collective-permute-done((bf16[8,2048]{1,0:T(8,128)(2,1)S(1)}, bf16[8,2048]{1,0:T(8,128)(2,1)S(1)}, u32[]{:S(2)}, u32[]{:S(2)}) %collective-permute-start.10) | collective-permute-done | bytes 32800 | tf_op jit(solution)/shard_map/ppermute | solution.py:42
  48.0 0.6 %add_convert_fusion = bf16[8,2048]{1,0:T(8,128)(2,1)} fusion(bf16[8,2048]{1,0:T(8,128)(2,1)S(1)} %collective-permute-done.18, bf16[8,2048]{1,0:T(8,128)(2,1)S(1)} %collective-permute-done.17, f32[8,2048]{1,0:T(8,128)S(1)} %get-tuple-element.26, bf16[8,2048]{1,0:T(8,128)(2,1)S(1)} %collective-permute-done.10), kind=kLoop, calls=%fused_computation | loop fusion | flops 114688 | bytes 196608 | tf_op jit(solution)/shard_map/convert_element_type | solution.py:443
  (4 shorter events, 0.1 us)
Async XLA Ops:
  0.6 8.6 %collective-permute-start.1 = (bf16[1024,2048]{1,0:T(8,128)(2,1)}, bf16[1024,2048]{1,0:T(8,128)(2,1)S(1)}, u32[]{:S(2)}, u32[]{:S(2)}) collective-permute-start(bf16[1024,2048]{1,0:T(8,128)(2,1)} %refs_2_.1), channel_id=1, source_target_pairs={{0,1},{1,0},{2,3},{3,2},{4,5},{5,4},{6,7},{7,6},{8,9},{9,8},{10,11... | collective-permute-start | bytes 12582920 | tf_op jit(solution)/shard_map/ppermute | solution.py:35
  1.2 25.1 %collective-permute-start.6 = (bf16[2048,768]{1,0:T(8,128)(2,1)}, bf16[2048,768]{1,0:T(8,128)(2,1)S(1)}, u32[]{:S(2)}, u32[]{:S(2)}) collective-permute-start(bf16[2048,768]{1,0:T(8,128)(2,1)} %bitcast.3), channel_id=1, source_target_pairs={{0,1},{1,0},{2,3},{3,2},{4,5},{5,4},{6,7},{7,6},{8,9},{9,8},{10,11... | collective-permute-start | bytes 9437192 | tf_op jit(solution)/shard_map/ppermute | solution.py:35
  1.3 8.0 %copy-start.2 = (bf16[1024,2048]{1,0:T(8,128)(2,1)S(1)}, bf16[1024,2048]{1,0:T(8,128)(2,1)}, u32[]{:S(2)}) copy-start(bf16[1024,2048]{1,0:T(8,128)(2,1)} %refs_2_.1) | copy-start | bytes 12582916
  1.3 8.0 %copy-start.3 = (bf16[8,2048]{1,0:T(8,128)(2,1)S(1)}, bf16[8,2048]{1,0:T(8,128)(2,1)}, u32[]{:S(2)}) copy-start(bf16[8,2048]{1,0:T(8,128)(2,1)} %refs_4_.1) | copy-start | bytes 98308
  1.3 8.0 %copy-start.5 = (s32[8,8]{1,0:T(8,128)S(1)}, s32[8,8]{1,0:T(8,128)}, u32[]{:S(2)}) copy-start(s32[8,8]{1,0:T(8,128)} %refs_5_.1) | copy-start | bytes 772
  1.3 8.0 %copy-start.6 = (s32[8,8]{1,0:T(8,128)S(1)}, s32[8,8]{1,0:T(8,128)}, u32[]{:S(2)}) copy-start(s32[8,8]{1,0:T(8,128)} %refs_6_.1) | copy-start | bytes 772
  1.3 22.0 %collective-permute-start.7 = (bf16[384,2048]{1,0:T(8,128)(2,1)}, bf16[384,2048]{1,0:T(8,128)(2,1)S(1)}, u32[]{:S(2)}, u32[]{:S(2)}) collective-permute-start(bf16[384,2048]{1,0:T(8,128)(2,1)} %bitcast.6), channel_id=1, source_target_pairs={{0,1},{1,0},{2,3},{3,2},{4,5},{5,4},{6,7},{7,6},{8,9},{9,8},{10,11... | collective-permute-start | bytes 4718600 | tf_op jit(solution)/shard_map/ppermute | solution.py:35
  4.3 4.9 %collective-permute-start = (bf16[1,8,2048]{2,1,0:T(8,128)(2,1)S(1)}, bf16[1,8,2048]{2,1,0:T(8,128)(2,1)S(1)}, u32[]{:S(2)}, u32[]{:S(2)}) collective-permute-start(bf16[1,8,2048]{2,1,0:T(8,128)(2,1)S(1)} %shard_map.123), channel_id=1, source_target_pairs={{0,3},{1,2},{2,1},{3,0},{4,7},{5,6},{6,5},{7,4},{8,11},{9,10},{10,... | collective-permute-start | bytes 98312 | tf_op jit(solution)/shard_map/ppermute | solution.py:42
  9.2 5.5 %copy-start.4 = (f32[2048]{0:T(1024)S(1)}, f32[2048]{0:T(1024)}, u32[]{:S(2)}) copy-start(f32[2048]{0:T(1024)} %param.17) | copy-start | bytes 24580
  9.2 18.1 %copy-start = (bf16[1,2048,768]{2,1,0:T(8,128)(2,1)S(1)}, bf16[1,2048,768]{2,1,0:T(8,128)(2,1)}, u32[]{:S(2)}) copy-start(bf16[1,2048,768]{2,1,0:T(8,128)(2,1)} %param.20) | copy-start | bytes 9437188
  9.2 18.1 %copy-start.1 = (bf16[1,384,2048]{2,1,0:T(8,128)(2,1)S(1)}, bf16[1,384,2048]{2,1,0:T(8,128)(2,1)}, u32[]{:S(2)}) copy-start(bf16[1,384,2048]{2,1,0:T(8,128)(2,1)} %param.21) | copy-start | bytes 4718596
  10.5 4.2 %collective-permute-start.2 = (bf16[16,2176]{1,0:T(8,128)(2,1)S(1)}, bf16[16,2176]{1,0:T(8,128)(2,1)S(1)}, u32[]{:S(2)}, u32[]{:S(2)}) collective-permute-start(bf16[16,2176]{1,0:T(8,128)(2,1)S(1)} %get-tuple-element.19), channel_id=1, source_target_pairs={{0,3},{1,2},{2,1},{3,0},{4,7},{5,6},{6,5},{7,4},{8,11},{9,10},{10,... | collective-permute-start | bytes 208904 | tf_op jit(solution)/shard_map/ppermute | solution.py:42
  14.8 5.1 %collective-permute-start.11 = (bf16[16,2176]{1,0:T(8,128)(2,1)S(1)}, bf16[16,2176]{1,0:T(8,128)(2,1)S(1)}, u32[]{:S(2)}, u32[]{:S(2)}) collective-permute-start(bf16[16,2176]{1,0:T(8,128)(2,1)S(1)} %get-tuple-element.21.refs_0_), channel_id=1, source_target_pairs={{0,17},{1,16},{2,19},{3,18},{4,21},{5,20},{6,23},{7,22},{8,25},{9,... | collective-permute-start | bytes 208904 | tf_op jit(solution)/shard_map/ppermute | solution.py:42
  17.5 5.6 %collective-permute-start.12 = (bf16[16,2176]{1,0:T(8,128)(2,1)S(1)}, bf16[16,2176]{1,0:T(8,128)(2,1)S(1)}, u32[]{:S(2)}, u32[]{:S(2)}) collective-permute-start(bf16[16,2176]{1,0:T(8,128)(2,1)S(1)} %get-tuple-element.21.refs_0_), channel_id=1, source_target_pairs={{0,9},{1,8},{2,11},{3,10},{4,13},{5,12},{6,15},{7,14},{8,1},{9,0},... | collective-permute-start | bytes 208904 | tf_op jit(solution)/shard_map/ppermute | solution.py:42
  19.0 6.0 %collective-permute-start.3 = (bf16[16,2176]{1,0:T(8,128)(2,1)S(1)}, bf16[16,2176]{1,0:T(8,128)(2,1)S(1)}, u32[]{:S(2)}, u32[]{:S(2)}) collective-permute-start(bf16[16,2176]{1,0:T(8,128)(2,1)S(1)} %get-tuple-element.21.refs_0_), channel_id=1, source_target_pairs={{0,25},{1,24},{2,27},{3,26},{4,29},{5,28},{6,31},{7,30},{8,17},{9,... | collective-permute-start | bytes 208904 | tf_op jit(solution)/shard_map/ppermute | solution.py:42
  19.9 6.4 %collective-permute-start.13 = (bf16[16,2176]{1,0:T(8,128)(2,1)S(1)}, bf16[16,2176]{1,0:T(8,128)(2,1)S(1)}, u32[]{:S(2)}, u32[]{:S(2)}) collective-permute-start(bf16[16,2176]{1,0:T(8,128)(2,1)S(1)} %collective-permute-done.11.refs_0_), channel_id=1, source_target_pairs={{0,5},{1,4},{2,7},{3,6},{4,1},{5,0},{6,3},{7,2},{8,13},{9,12},{10,... | collective-permute-start | bytes 208904 | tf_op jit(solution)/shard_map/ppermute | solution.py:42
  23.1 4.2 %collective-permute-start.14 = (bf16[16,2176]{1,0:T(8,128)(2,1)S(1)}, bf16[16,2176]{1,0:T(8,128)(2,1)S(1)}, u32[]{:S(2)}, u32[]{:S(2)}) collective-permute-start(bf16[16,2176]{1,0:T(8,128)(2,1)S(1)} %collective-permute-done.12.refs_1_), channel_id=1, source_target_pairs={{0,5},{1,4},{2,7},{3,6},{4,1},{5,0},{6,3},{7,2},{8,13},{9,12},{10,... | collective-permute-start | bytes 208904 | tf_op jit(solution)/shard_map/ppermute | solution.py:42
  23.3 8.0 %collective-permute-start.4 = (bf16[16,2176]{1,0:T(8,128)(2,1)S(1)}, bf16[16,2176]{1,0:T(8,128)(2,1)S(1)}, u32[]{:S(2)}, u32[]{:S(2)}) collective-permute-start(bf16[16,2176]{1,0:T(8,128)(2,1)S(1)} %get-tuple-element.21.refs_0_), channel_id=1, source_target_pairs={{0,5},{1,4},{2,7},{3,6},{4,1},{5,0},{6,3},{7,2},{8,13},{9,12},{10,... | collective-permute-start | bytes 208904 | tf_op jit(solution)/shard_map/ppermute | solution.py:42
  25.0 6.3 %collective-permute-start.5 = (bf16[16,2176]{1,0:T(8,128)(2,1)S(1)}, bf16[16,2176]{1,0:T(8,128)(2,1)S(1)}, u32[]{:S(2)}, u32[]{:S(2)}) collective-permute-start(bf16[16,2176]{1,0:T(8,128)(2,1)S(1)} %collective-permute-done.3.refs_1_), channel_id=1, source_target_pairs={{0,5},{1,4},{2,7},{3,6},{4,1},{5,0},{6,3},{7,2},{8,13},{9,12},{10,... | collective-permute-start | bytes 208904 | tf_op jit(solution)/shard_map/ppermute | solution.py:42
  29.2 4.8 %collective-permute-start.15 = (bf16[32,2048]{1,0:T(8,128)(2,1)S(1)}, bf16[32,2048]{1,0:T(8,128)(2,1)S(1)}, u32[]{:S(2)}, u32[]{:S(2)}) collective-permute-start(bf16[32,2048]{1,0:T(8,128)(2,1)S(1)} %get-tuple-element.29), channel_id=1, source_target_pairs={{0,5},{1,2},{2,1},{3,6},{4,7},{5,0},{6,3},{7,4},{8,13},{9,10},{10,... | collective-permute-start | bytes 393224 | tf_op jit(solution)/shard_map/ppermute | solution.py:60
  33.1 4.5 %collective-permute-start.8 = (bf16[32,2048]{1,0:T(8,128)(2,1)S(1)}, bf16[32,2048]{1,0:T(8,128)(2,1)S(1)}, u32[]{:S(2)}, u32[]{:S(2)}) collective-permute-start(bf16[32,2048]{1,0:T(8,128)(2,1)S(1)} %get-tuple-element.23), channel_id=1, source_target_pairs={{0,3},{1,4},{2,7},{3,0},{4,1},{5,6},{6,5},{7,2},{8,11},{9,12},{10,... | collective-permute-start | bytes 393224 | tf_op jit(solution)/shard_map/ppermute | solution.py:60
  34.0 4.3 %collective-permute-start.16 = (bf16[16,2048]{1,0:T(8,128)(2,1)S(1)}, bf16[16,2048]{1,0:T(8,128)(2,1)S(1)}, u32[]{:S(2)}, u32[]{:S(2)}) collective-permute-start(bf16[16,2048]{1,0:T(8,128)(2,1)S(1)} %get-tuple-element.31), channel_id=1, source_target_pairs={{0,3},{1,4},{2,7},{3,0},{4,1},{5,6},{6,5},{7,2},{8,11},{9,12},{10,... | collective-permute-start | bytes 196616 | tf_op jit(solution)/shard_map/ppermute | solution.py:60
  37.6 5.2 %collective-permute-start.9 = (bf16[16,2048]{1,0:T(8,128)(2,1)S(1)}, bf16[16,2048]{1,0:T(8,128)(2,1)S(1)}, u32[]{:S(2)}, u32[]{:S(2)}) collective-permute-start(bf16[16,2048]{1,0:T(8,128)(2,1)S(1)} %get-tuple-element.25), channel_id=1, source_target_pairs={{0,5},{1,2},{2,1},{3,6},{4,7},{5,0},{6,3},{7,4},{8,13},{9,10},{10,... | collective-permute-start | bytes 196616 | tf_op jit(solution)/shard_map/ppermute | solution.py:60
  38.3 7.9 %collective-permute-start.18 = (bf16[8,2048]{1,0:T(8,128)(2,1)S(1)}, bf16[8,2048]{1,0:T(8,128)(2,1)S(1)}, u32[]{:S(2)}, u32[]{:S(2)}) collective-permute-start(bf16[8,2048]{1,0:T(8,128)(2,1)S(1)} %get-tuple-element.33), channel_id=1, source_target_pairs={{0,9},{1,8},{2,11},{3,10},{4,13},{5,12},{6,15},{7,14},{8,1},{9,0},... | collective-permute-start | bytes 98312 | tf_op jit(solution)/shard_map/ppermute | solution.py:42
  39.3 7.0 %collective-permute-start.17 = (bf16[8,2048]{1,0:T(8,128)(2,1)S(1)}, bf16[8,2048]{1,0:T(8,128)(2,1)S(1)}, u32[]{:S(2)}, u32[]{:S(2)}) collective-permute-start(bf16[8,2048]{1,0:T(8,128)(2,1)S(1)} %get-tuple-element.32), channel_id=1, source_target_pairs={{0,17},{1,16},{2,19},{3,18},{4,21},{5,20},{6,23},{7,22},{8,25},{9,... | collective-permute-start | bytes 98312 | tf_op jit(solution)/shard_map/ppermute | solution.py:42
  42.8 5.2 %collective-permute-start.10 = (bf16[8,2048]{1,0:T(8,128)(2,1)S(1)}, bf16[8,2048]{1,0:T(8,128)(2,1)S(1)}, u32[]{:S(2)}, u32[]{:S(2)}) collective-permute-start(bf16[8,2048]{1,0:T(8,128)(2,1)S(1)} %get-tuple-element.27), channel_id=1, source_target_pairs={{0,25},{1,24},{2,27},{3,26},{4,29},{5,28},{6,31},{7,30},{8,17},{9,... | collective-permute-start | bytes 98312 | tf_op jit(solution)/shard_map/ppermute | solution.py:42

commit v6 on v5

--- a/solution.py
+++ b/solution.py
@@ -301,9 +301,9 @@
 
 
 def expert_kernel(rows, turn, *refs):
-    kept_ref, sent_ref, result = refs[-3:]
-    in_own, in_other, down_own, down_other = refs[-7:-3]
-    blocks = refs[:-7]
+    kept_ref, sent_ref = refs[-2:]
+    in_own, in_other, down_own, down_other = refs[-6:-2]
+    blocks = refs[:-6]
     width = kept_ref.shape[1]
     units = down_own.shape[0]
     chips = lax.axis_size("side") // 2
@@ -322,7 +322,7 @@
     total = jnp.dot(hidden[0], down_own[...], preferred_element_type=jnp.float32) + jnp.dot(
         hidden[1], down_other[...], preferred_element_type=jnp.float32
     )
-    result[...] = total * share
+    total = total * share
     kind = device_class(lax.axis_index("dev"), lax.axis_index("side")) ^ turn
     nearby = len(blocks) // 2
     slots = 2 * nearby * chips
@@ -331,8 +331,8 @@
         starts = []
         for chip, far in ((upper // 2, upper % 2), (upper % chips, upper // chips)):
             starts.append(((far * nearby + index) * chips + chip) * rows)
-        start = pl.multiple_of(jnp.where(kind == 0, starts[0], starts[1]), rows)
-        piece = result[pl.ds(start, rows), :]
+        first, second = (total[start : start + rows] for start in starts)
+        piece = jnp.where(kind == 0, first, second)
         to = slot % (slots // 2) * rows
         if slot < slots // 2:
             kept_ref[to : to + rows, :] = piece
@@ -347,7 +347,6 @@
         functools.partial(expert_kernel, rows, int(name == "experts_late")),
         (*blocks, *weights),
         (jax.ShapeDtypeStruct(shape, jnp.float32), jax.ShapeDtypeStruct(shape, jnp.bfloat16)),
-        scratch=[pltpu.VMEM((count, width), jnp.float32)],
         cost=pl.CostEstimate(flops=1 << 30, bytes_accessed=4 << 20, transcendentals=0),
     )
 

time: 48.8 us -> 48.8 us (level)
  no operation moved by 1% of the time
where the time goes in v6:
time: 48.8 us; the launch traced here: 48.7 us
  starting transfers between devices  27.4 us (56%)
  Pallas kernels  9.86 us (20%)
  waiting for transfers between devices  9.34 us (19%)
  between operations  0.78 us (2%)
  local copies, waits for them, and re-layouts  0.65 us (1%)
  other arithmetic  0.63 us (1%)
    ppermute x12, starting transfers between devices, across(): lax.ppermute(block, ('dev', 'side'), [(i, i ^ mask) for i in range(count)])  21.9 us
    pallas_call x10, Pallas kernels, kernel_call(): pl.pallas_call(body, out_shape=outs, in_specs=in_specs or [VMEM] * len(op...  9.86 us
    ppermute x12, waiting for transfers between devices, across(): lax.ppermute(block, ('dev', 'side'), [(i, i ^ mask) for i in range(count)])  6.54 us
    ppermute x4, starting transfers between devices, apart(): return lax.ppermute(block, ('dev', 'side'), route)  4.41 us
    ppermute x4, waiting for transfers between devices, apart(): return lax.ppermute(block, ('dev', 'side'), route)  2.79 us
    ppermute x3, starting transfers between devices, partner(): return lax.ppermute(block, axis, [(i, i ^ mask) for i in range(count)])  1.13 us
  transfers between devices with their start and end apart: 19, of which 8 were waited for; matrix products, arithmetic and copies ran while one was open for 1% of the time, Pallas kernels for 20%

profile of v6, /device:TPU:0, one launch (start us, length us, event | category | flops | bytes accessed | tf_op | source)
XLA Modules:
  0.0 48.7 jit_solution(9643754794512284584)
XLA Ops:
  0.6 0.6 %collective-permute-start.1 = (bf16[1024,2048]{1,0:T(8,128)(2,1)}, bf16[1024,2048]{1,0:T(8,128)(2,1)S(1)}, u32[]{:S(2)}, u32[]{:S(2)}) collective-permute-start(bf16[1024,2048]{1,0:T(8,128)(2,1)} %refs_2_.1), channel_id=1, source_target_pairs={{0,1},{1,0},{2,3},{3,2},{4,5},{5,4},{6,7},{7,6},{8,9},{9,8},{10,11... | collective-permute-start | bytes 12582920 | tf_op jit(solution)/shard_map/ppermute | solution.py:35
  1.2 0.1 collective-permute-start.6
  1.3 0.0 copy-start.2
  1.3 0.0 copy-start.3
  1.3 0.0 copy-start.5
  1.3 0.0 copy-start.6
  1.3 0.5 %collective-permute-start.7 = (bf16[384,2048]{1,0:T(8,128)(2,1)}, bf16[384,2048]{1,0:T(8,128)(2,1)S(1)}, u32[]{:S(2)}, u32[]{:S(2)}) collective-permute-start(bf16[384,2048]{1,0:T(8,128)(2,1)} %bitcast.6), channel_id=1, source_target_pairs={{0,1},{1,0},{2,3},{3,2},{4,5},{5,4},{6,7},{7,6},{8,9},{9,8},{10,11... | collective-permute-start | bytes 4718600 | tf_op jit(solution)/shard_map/ppermute | solution.py:35
  1.8 2.5 %shard_map.123 = bf16[1,8,2048]{2,1,0:T(8,128)(2,1)S(1)} custom-call(bf16[8,4096]{1,0:T(8,128)(2,1)} %q_hbm.3, bf16[8,192,1024]{2,1,0:T(8,128)(2,1)} %kv_hbm.3, bf16[8,1024]{1,0:T(8,128)(2,1)} %new_hbm.3, s32[8]{0:T(128)} %length_hbm.3), custom_call_target="tpu_custom_call" | custom-call | flops 8388608 | bytes 6291456 | tf_op jit(solution)/shard_map/pallas_call | solution.py:18
  4.3 2.7 %collective-permute-start = (bf16[1,8,2048]{2,1,0:T(8,128)(2,1)S(1)}, bf16[1,8,2048]{2,1,0:T(8,128)(2,1)S(1)}, u32[]{:S(2)}, u32[]{:S(2)}) collective-permute-start(bf16[1,8,2048]{2,1,0:T(8,128)(2,1)S(1)} %shard_map.123), channel_id=1, source_target_pairs={{0,3},{1,2},{2,1},{3,0},{4,7},{5,6},{6,5},{7,4},{8,11},{9,10},{10,... | collective-permute-start | bytes 98312 | tf_op jit(solution)/shard_map/ppermute | solution.py:42
  6.9 2.2 %shard_map.122.refs_0_ = bf16[1,8,2048]{2,1,0:T(8,128)(2,1)S(1)} custom-call(bf16[8,4096]{1,0:T(8,128)(2,1)} %q_hbm.3, bf16[8,192,1024]{2,1,0:T(8,128)(2,1)} %kv_hbm.3, bf16[8,1024]{1,0:T(8,128)(2,1)} %new_hbm.3, s32[8]{0:T(128)} %length_hbm.3), custom_call_target="tpu_custom_call" | custom-call | flops 8388608 | bytes 6291456 | tf_op jit(solution)/shard_map/pallas_call | solution.py:18
  9.2 0.0 copy-start.4
  9.2 0.0 copy-start
  9.2 0.0 copy-start.1
  9.2 0.0 collective-permute-done.refs_1_
  9.2 0.0 collective-permute-done.1.refs_3_
  9.2 0.0 copy-done.2
  9.3 0.0 copy-done.3
  9.3 0.0 copy-done.5
  9.3 0.0 copy-done.6
  9.3 1.2 %shard_map.124 = (f32[16,2176]{1,0:T(8,128)S(1)}, bf16[16,2176]{1,0:T(8,128)(2,1)S(1)}) custom-call(bf16[1,8,2048]{2,1,0:T(8,128)(2,1)S(1)} %shard_map.122.refs_0_, bf16[1,8,2048]{2,1,0:T(8,128)(2,1)S(1)} %collective-permute-done.refs_1_, bf16[1024,2048]{1,0:T(8,128)(2,1)S(1)} %copy-done.2, bf16[1024,2048]{1,0:T(8,128)(2,1)S(1)} %collective-permute-done.1.refs_3_, ...), custom_call_target="tpu_custom_call" | custom-call | tf_op jit(solution)/shard_map/pallas_call | solution.py:18
  10.5 1.5 %collective-permute-start.2 = (bf16[16,2176]{1,0:T(8,128)(2,1)S(1)}, bf16[16,2176]{1,0:T(8,128)(2,1)S(1)}, u32[]{:S(2)}, u32[]{:S(2)}) collective-permute-start(bf16[16,2176]{1,0:T(8,128)(2,1)S(1)} %get-tuple-element.19), channel_id=1, source_target_pairs={{0,3},{1,2},{2,1},{3,0},{4,7},{5,6},{6,5},{7,4},{8,11},{9,10},{10,... | collective-permute-start | bytes 208904 | tf_op jit(solution)/shard_map/ppermute | solution.py:42
  12.0 2.7 %collective-permute-done.2.more_ref = bf16[16,2176]{1,0:T(8,128)(2,1)S(1)} collective-permute-done((bf16[16,2176]{1,0:T(8,128)(2,1)S(1)}, bf16[16,2176]{1,0:T(8,128)(2,1)S(1)}, u32[]{:S(2)}, u32[]{:S(2)}) %collective-permute-start.2) | collective-permute-done | bytes 69664 | tf_op jit(solution)/shard_map/ppermute | solution.py:42
  14.7 0.0 copy-done.4
  14.7 0.1 shard_map.125
  14.8 2.7 %collective-permute-start.11 = (bf16[16,2176]{1,0:T(8,128)(2,1)S(1)}, bf16[16,2176]{1,0:T(8,128)(2,1)S(1)}, u32[]{:S(2)}, u32[]{:S(2)}) collective-permute-start(bf16[16,2176]{1,0:T(8,128)(2,1)S(1)} %get-tuple-element.21.refs_0_), channel_id=1, source_target_pairs={{0,17},{1,16},{2,19},{3,18},{4,21},{5,20},{6,23},{7,22},{8,25},{9,... | collective-permute-start | bytes 208904 | tf_op jit(solution)/shard_map/ppermute | solution.py:42
  17.5 1.6 %collective-permute-start.12 = (bf16[16,2176]{1,0:T(8,128)(2,1)S(1)}, bf16[16,2176]{1,0:T(8,128)(2,1)S(1)}, u32[]{:S(2)}, u32[]{:S(2)}) collective-permute-start(bf16[16,2176]{1,0:T(8,128)(2,1)S(1)} %get-tuple-element.21.refs_0_), channel_id=1, source_target_pairs={{0,9},{1,8},{2,11},{3,10},{4,13},{5,12},{6,15},{7,14},{8,1},{9,0},... | collective-permute-start | bytes 208904 | tf_op jit(solution)/shard_map/ppermute | solution.py:42
  19.0 0.0 collective-permute-start.3
  19.0 0.9 %collective-permute-done.11.refs_0_ = bf16[16,2176]{1,0:T(8,128)(2,1)S(1)} collective-permute-done((bf16[16,2176]{1,0:T(8,128)(2,1)S(1)}, bf16[16,2176]{1,0:T(8,128)(2,1)S(1)}, u32[]{:S(2)}, u32[]{:S(2)}) %collective-permute-start.11) | collective-permute-done | bytes 69664 | tf_op jit(solution)/shard_map/ppermute | solution.py:42
  19.9 3.2 %collective-permute-start.13 = (bf16[16,2176]{1,0:T(8,128)(2,1)S(1)}, bf16[16,2176]{1,0:T(8,128)(2,1)S(1)}, u32[]{:S(2)}, u32[]{:S(2)}) collective-permute-start(bf16[16,2176]{1,0:T(8,128)(2,1)S(1)} %collective-permute-done.11.refs_0_), channel_id=1, source_target_pairs={{0,5},{1,4},{2,7},{3,6},{4,1},{5,0},{6,3},{7,2},{8,13},{9,12},{10,... | collective-permute-start | bytes 208904 | tf_op jit(solution)/shard_map/ppermute | solution.py:42
  23.1 0.0 collective-permute-done.12.refs_1_
  23.1 0.2 collective-permute-start.14
  23.3 0.0 collective-permute-done.7.refs_7_
  23.3 1.5 %collective-permute-start.4 = (bf16[16,2176]{1,0:T(8,128)(2,1)S(1)}, bf16[16,2176]{1,0:T(8,128)(2,1)S(1)}, u32[]{:S(2)}, u32[]{:S(2)}) collective-permute-start(bf16[16,2176]{1,0:T(8,128)(2,1)S(1)} %get-tuple-element.21.refs_0_), channel_id=1, source_target_pairs={{0,5},{1,4},{2,7},{3,6},{4,1},{5,0},{6,3},{7,2},{8,13},{9,12},{10,... | collective-permute-start | bytes 208904 | tf_op jit(solution)/shard_map/ppermute | solution.py:42
  24.8 0.2 collective-permute-done.3.refs_1_
  25.0 1.3 %collective-permute-start.5 = (bf16[16,2176]{1,0:T(8,128)(2,1)S(1)}, bf16[16,2176]{1,0:T(8,128)(2,1)S(1)}, u32[]{:S(2)}, u32[]{:S(2)}) collective-permute-start(bf16[16,2176]{1,0:T(8,128)(2,1)S(1)} %collective-permute-done.3.refs_1_), channel_id=1, source_target_pairs={{0,5},{1,4},{2,7},{3,6},{4,1},{5,0},{6,3},{7,2},{8,13},{9,12},{10,... | collective-permute-start | bytes 208904 | tf_op jit(solution)/shard_map/ppermute | solution.py:42
  26.2 0.0 collective-permute-done.6.refs_5_
  26.2 0.0 collective-permute-done.13.refs_2_
  26.3 1.0 %collective-permute-done.14.refs_3_ = bf16[16,2176]{1,0:T(8,128)(2,1)S(1)} collective-permute-done((bf16[16,2176]{1,0:T(8,128)(2,1)S(1)}, bf16[16,2176]{1,0:T(8,128)(2,1)S(1)}, u32[]{:S(2)}, u32[]{:S(2)}) %collective-permute-start.14) | collective-permute-done | bytes 69664 | tf_op jit(solution)/shard_map/ppermute | solution.py:42
  27.3 0.0 copy-done
  27.3 0.0 copy-done.1
  27.3 1.9 %shard_map.129 = (f32[32,2048]{1,0:T(8,128)S(1)}, bf16[32,2048]{1,0:T(8,128)(2,1)S(1)}) custom-call(bf16[16,2176]{1,0:T(8,128)(2,1)S(1)} %collective-permute-done.11.refs_0_, bf16[16,2176]{1,0:T(8,128)(2,1)S(1)} %collective-permute-done.12.refs_1_, bf16[16,2176]{1,0:T(8,128)(2,1)S(1)} %collective-permute-done.13.refs_2_, ...), custom_call_target="tpu_custom_call" | custom-call | flops 1073741824 | bytes 4194304 | tf_op jit(solution)/shard_map/pallas_call | solution.py:18
  29.2 2.1 %collective-permute-start.15 = (bf16[32,2048]{1,0:T(8,128)(2,1)S(1)}, bf16[32,2048]{1,0:T(8,128)(2,1)S(1)}, u32[]{:S(2)}, u32[]{:S(2)}) collective-permute-start(bf16[32,2048]{1,0:T(8,128)(2,1)S(1)} %get-tuple-element.29), channel_id=1, source_target_pairs={{0,5},{1,2},{2,1},{3,6},{4,7},{5,0},{6,3},{7,4},{8,13},{9,10},{10,... | collective-permute-start | bytes 393224 | tf_op jit(solution)/shard_map/ppermute | solution.py:60
  31.3 0.0 collective-permute-done.4.refs_2_
  31.3 0.0 collective-permute-done.5.refs_3_
  31.3 1.8 %shard_map.126 = (f32[32,2048]{1,0:T(8,128)S(1)}, bf16[32,2048]{1,0:T(8,128)(2,1)S(1)}) custom-call(bf16[16,2176]{1,0:T(8,128)(2,1)S(1)} %get-tuple-element.21.refs_0_, bf16[16,2176]{1,0:T(8,128)(2,1)S(1)} %collective-permute-done.3.refs_1_, bf16[16,2176]{1,0:T(8,128)(2,1)S(1)} %collective-permute-done.4.refs_2_, ...), custom_call_target="tpu_custom_call" | custom-call | flops 1073741824 | bytes 4194304 | tf_op jit(solution)/shard_map/pallas_call | solution.py:18
  33.1 0.3 collective-permute-start.8
  33.4 0.5 collective-permute-done.15.more_ref
  34.0 1.5 %collective-permute-start.16 = (bf16[16,2048]{1,0:T(8,128)(2,1)S(1)}, bf16[16,2048]{1,0:T(8,128)(2,1)S(1)}, u32[]{:S(2)}, u32[]{:S(2)}) collective-permute-start(bf16[16,2048]{1,0:T(8,128)(2,1)S(1)} %get-tuple-element.31), channel_id=1, source_target_pairs={{0,3},{1,4},{2,7},{3,0},{4,1},{5,6},{6,5},{7,2},{8,11},{9,12},{10,... | collective-permute-start | bytes 196616 | tf_op jit(solution)/shard_map/ppermute | solution.py:60
  35.4 2.1 %collective-permute-done.8.more_ref = bf16[32,2048]{1,0:T(8,128)(2,1)S(1)} collective-permute-done((bf16[32,2048]{1,0:T(8,128)(2,1)S(1)}, bf16[32,2048]{1,0:T(8,128)(2,1)S(1)}, u32[]{:S(2)}, u32[]{:S(2)}) %collective-permute-start.8) | collective-permute-done | bytes 131104 | tf_op jit(solution)/shard_map/ppermute | solution.py:60
  37.6 0.5 %collective-permute-start.9 = (bf16[16,2048]{1,0:T(8,128)(2,1)S(1)}, bf16[16,2048]{1,0:T(8,128)(2,1)S(1)}, u32[]{:S(2)}, u32[]{:S(2)}) collective-permute-start(bf16[16,2048]{1,0:T(8,128)(2,1)S(1)} %get-tuple-element.25), channel_id=1, source_target_pairs={{0,5},{1,2},{2,1},{3,6},{4,7},{5,0},{6,3},{7,4},{8,13},{9,10},{10,... | collective-permute-start | bytes 196616 | tf_op jit(solution)/shard_map/ppermute | solution.py:60
  38.1 0.2 collective-permute-done.16.more_ref
  38.3 0.9 %collective-permute-start.18 = (bf16[8,2048]{1,0:T(8,128)(2,1)S(1)}, bf16[8,2048]{1,0:T(8,128)(2,1)S(1)}, u32[]{:S(2)}, u32[]{:S(2)}) collective-permute-start(bf16[8,2048]{1,0:T(8,128)(2,1)S(1)} %get-tuple-element.33), channel_id=1, source_target_pairs={{0,9},{1,8},{2,11},{3,10},{4,13},{5,12},{6,15},{7,14},{8,1},{9,0},... | collective-permute-start | bytes 98312 | tf_op jit(solution)/shard_map/ppermute | solution.py:42
  39.3 3.5 %collective-permute-start.17 = (bf16[8,2048]{1,0:T(8,128)(2,1)S(1)}, bf16[8,2048]{1,0:T(8,128)(2,1)S(1)}, u32[]{:S(2)}, u32[]{:S(2)}) collective-permute-start(bf16[8,2048]{1,0:T(8,128)(2,1)S(1)} %get-tuple-element.32), channel_id=1, source_target_pairs={{0,17},{1,16},{2,19},{3,18},{4,21},{5,20},{6,23},{7,22},{8,25},{9,... | collective-permute-start | bytes 98312 | tf_op jit(solution)/shard_map/ppermute | solution.py:42
  42.8 0.0 collective-permute-done.9.more_ref
  42.8 2.8 %collective-permute-start.10 = (bf16[8,2048]{1,0:T(8,128)(2,1)S(1)}, bf16[8,2048]{1,0:T(8,128)(2,1)S(1)}, u32[]{:S(2)}, u32[]{:S(2)}) collective-permute-start(bf16[8,2048]{1,0:T(8,128)(2,1)S(1)} %get-tuple-element.27), channel_id=1, source_target_pairs={{0,25},{1,24},{2,27},{3,26},{4,29},{5,28},{6,31},{7,30},{8,17},{9,... | collective-permute-start | bytes 98312 | tf_op jit(solution)/shard_map/ppermute | solution.py:42
  45.6 0.6 %copy.13 = bf16[8,2048]{1,0:T(8,128)(2,1)} copy(bf16[8,2048]{1,0:T(8,128)(2,1)S(1)} %get-tuple-element.34) | data formatting | bytes 65536
  46.2 0.0 collective-permute-done.18
  46.2 0.0 collective-permute-done.17
  46.2 1.8 %collective-permute-done.10 = bf16[8,2048]{1,0:T(8,128)(2,1)S(1)} collective-permute-done((bf16[8,2048]{1,0:T(8,128)(2,1)S(1)}, bf16[8,2048]{1,0:T(8,128)(2,1)S(1)}, u32[]{:S(2)}, u32[]{:S(2)}) %collective-permute-start.10) | collective-permute-done | bytes 32800 | tf_op jit(solution)/shard_map/ppermute | solution.py:42
  48.0 0.6 %add_convert_fusion = bf16[8,2048]{1,0:T(8,128)(2,1)} fusion(bf16[8,2048]{1,0:T(8,128)(2,1)S(1)} %collective-permute-done.18, bf16[8,2048]{1,0:T(8,128)(2,1)S(1)} %collective-permute-done.17, f32[8,2048]{1,0:T(8,128)S(1)} %get-tuple-element.26, bf16[8,2048]{1,0:T(8,128)(2,1)S(1)} %collective-permute-done.10), kind=kLoop, calls=%fused_computation | loop fusion | flops 114688 | bytes 196608 | tf_op jit(solution)/shard_map/convert_element_type | solution.py:442
  (4 shorter events, 0.1 us)
Async XLA Ops:
  0.6 8.6 %collective-permute-start.1 = (bf16[1024,2048]{1,0:T(8,128)(2,1)}, bf16[1024,2048]{1,0:T(8,128)(2,1)S(1)}, u32[]{:S(2)}, u32[]{:S(2)}) collective-permute-start(bf16[1024,2048]{1,0:T(8,128)(2,1)} %refs_2_.1), channel_id=1, source_target_pairs={{0,1},{1,0},{2,3},{3,2},{4,5},{5,4},{6,7},{7,6},{8,9},{9,8},{10,11... | collective-permute-start | bytes 12582920 | tf_op jit(solution)/shard_map/ppermute | solution.py:35
  1.2 25.1 %collective-permute-start.6 = (bf16[2048,768]{1,0:T(8,128)(2,1)}, bf16[2048,768]{1,0:T(8,128)(2,1)S(1)}, u32[]{:S(2)}, u32[]{:S(2)}) collective-permute-start(bf16[2048,768]{1,0:T(8,128)(2,1)} %bitcast.3), channel_id=1, source_target_pairs={{0,1},{1,0},{2,3},{3,2},{4,5},{5,4},{6,7},{7,6},{8,9},{9,8},{10,11... | collective-permute-start | bytes 9437192 | tf_op jit(solution)/shard_map/ppermute | solution.py:35
  1.3 8.0 %copy-start.2 = (bf16[1024,2048]{1,0:T(8,128)(2,1)S(1)}, bf16[1024,2048]{1,0:T(8,128)(2,1)}, u32[]{:S(2)}) copy-start(bf16[1024,2048]{1,0:T(8,128)(2,1)} %refs_2_.1) | copy-start | bytes 12582916
  1.3 8.0 %copy-start.3 = (bf16[8,2048]{1,0:T(8,128)(2,1)S(1)}, bf16[8,2048]{1,0:T(8,128)(2,1)}, u32[]{:S(2)}) copy-start(bf16[8,2048]{1,0:T(8,128)(2,1)} %refs_4_.1) | copy-start | bytes 98308
  1.3 8.0 %copy-start.5 = (s32[8,8]{1,0:T(8,128)S(1)}, s32[8,8]{1,0:T(8,128)}, u32[]{:S(2)}) copy-start(s32[8,8]{1,0:T(8,128)} %refs_5_.1) | copy-start | bytes 772
  1.3 8.0 %copy-start.6 = (s32[8,8]{1,0:T(8,128)S(1)}, s32[8,8]{1,0:T(8,128)}, u32[]{:S(2)}) copy-start(s32[8,8]{1,0:T(8,128)} %refs_6_.1) | copy-start | bytes 772
  1.3 22.0 %collective-permute-start.7 = (bf16[384,2048]{1,0:T(8,128)(2,1)}, bf16[384,2048]{1,0:T(8,128)(2,1)S(1)}, u32[]{:S(2)}, u32[]{:S(2)}) collective-permute-start(bf16[384,2048]{1,0:T(8,128)(2,1)} %bitcast.6), channel_id=1, source_target_pairs={{0,1},{1,0},{2,3},{3,2},{4,5},{5,4},{6,7},{7,6},{8,9},{9,8},{10,11... | collective-permute-start | bytes 4718600 | tf_op jit(solution)/shard_map/ppermute | solution.py:35
  4.3 4.9 %collective-permute-start = (bf16[1,8,2048]{2,1,0:T(8,128)(2,1)S(1)}, bf16[1,8,2048]{2,1,0:T(8,128)(2,1)S(1)}, u32[]{:S(2)}, u32[]{:S(2)}) collective-permute-start(bf16[1,8,2048]{2,1,0:T(8,128)(2,1)S(1)} %shard_map.123), channel_id=1, source_target_pairs={{0,3},{1,2},{2,1},{3,0},{4,7},{5,6},{6,5},{7,4},{8,11},{9,10},{10,... | collective-permute-start | bytes 98312 | tf_op jit(solution)/shard_map/ppermute | solution.py:42
  9.2 5.5 %copy-start.4 = (f32[2048]{0:T(1024)S(1)}, f32[2048]{0:T(1024)}, u32[]{:S(2)}) copy-start(f32[2048]{0:T(1024)} %param.17) | copy-start | bytes 24580
  9.2 18.1 %copy-start = (bf16[1,2048,768]{2,1,0:T(8,128)(2,1)S(1)}, bf16[1,2048,768]{2,1,0:T(8,128)(2,1)}, u32[]{:S(2)}) copy-start(bf16[1,2048,768]{2,1,0:T(8,128)(2,1)} %param.20) | copy-start | bytes 9437188
  9.2 18.1 %copy-start.1 = (bf16[1,384,2048]{2,1,0:T(8,128)(2,1)S(1)}, bf16[1,384,2048]{2,1,0:T(8,128)(2,1)}, u32[]{:S(2)}) copy-start(bf16[1,384,2048]{2,1,0:T(8,128)(2,1)} %param.21) | copy-start | bytes 4718596
  10.5 4.2 %collective-permute-start.2 = (bf16[16,2176]{1,0:T(8,128)(2,1)S(1)}, bf16[16,2176]{1,0:T(8,128)(2,1)S(1)}, u32[]{:S(2)}, u32[]{:S(2)}) collective-permute-start(bf16[16,2176]{1,0:T(8,128)(2,1)S(1)} %get-tuple-element.19), channel_id=1, source_target_pairs={{0,3},{1,2},{2,1},{3,0},{4,7},{5,6},{6,5},{7,4},{8,11},{9,10},{10,... | collective-permute-start | bytes 208904 | tf_op jit(solution)/shard_map/ppermute | solution.py:42
  14.8 5.1 %collective-permute-start.11 = (bf16[16,2176]{1,0:T(8,128)(2,1)S(1)}, bf16[16,2176]{1,0:T(8,128)(2,1)S(1)}, u32[]{:S(2)}, u32[]{:S(2)}) collective-permute-start(bf16[16,2176]{1,0:T(8,128)(2,1)S(1)} %get-tuple-element.21.refs_0_), channel_id=1, source_target_pairs={{0,17},{1,16},{2,19},{3,18},{4,21},{5,20},{6,23},{7,22},{8,25},{9,... | collective-permute-start | bytes 208904 | tf_op jit(solution)/shard_map/ppermute | solution.py:42
  17.5 5.6 %collective-permute-start.12 = (bf16[16,2176]{1,0:T(8,128)(2,1)S(1)}, bf16[16,2176]{1,0:T(8,128)(2,1)S(1)}, u32[]{:S(2)}, u32[]{:S(2)}) collective-permute-start(bf16[16,2176]{1,0:T(8,128)(2,1)S(1)} %get-tuple-element.21.refs_0_), channel_id=1, source_target_pairs={{0,9},{1,8},{2,11},{3,10},{4,13},{5,12},{6,15},{7,14},{8,1},{9,0},... | collective-permute-start | bytes 208904 | tf_op jit(solution)/shard_map/ppermute | solution.py:42
  19.0 6.0 %collective-permute-start.3 = (bf16[16,2176]{1,0:T(8,128)(2,1)S(1)}, bf16[16,2176]{1,0:T(8,128)(2,1)S(1)}, u32[]{:S(2)}, u32[]{:S(2)}) collective-permute-start(bf16[16,2176]{1,0:T(8,128)(2,1)S(1)} %get-tuple-element.21.refs_0_), channel_id=1, source_target_pairs={{0,25},{1,24},{2,27},{3,26},{4,29},{5,28},{6,31},{7,30},{8,17},{9,... | collective-permute-start | bytes 208904 | tf_op jit(solution)/shard_map/ppermute | solution.py:42
  19.9 6.4 %collective-permute-start.13 = (bf16[16,2176]{1,0:T(8,128)(2,1)S(1)}, bf16[16,2176]{1,0:T(8,128)(2,1)S(1)}, u32[]{:S(2)}, u32[]{:S(2)}) collective-permute-start(bf16[16,2176]{1,0:T(8,128)(2,1)S(1)} %collective-permute-done.11.refs_0_), channel_id=1, source_target_pairs={{0,5},{1,4},{2,7},{3,6},{4,1},{5,0},{6,3},{7,2},{8,13},{9,12},{10,... | collective-permute-start | bytes 208904 | tf_op jit(solution)/shard_map/ppermute | solution.py:42
  23.1 4.2 %collective-permute-start.14 = (bf16[16,2176]{1,0:T(8,128)(2,1)S(1)}, bf16[16,2176]{1,0:T(8,128)(2,1)S(1)}, u32[]{:S(2)}, u32[]{:S(2)}) collective-permute-start(bf16[16,2176]{1,0:T(8,128)(2,1)S(1)} %collective-permute-done.12.refs_1_), channel_id=1, source_target_pairs={{0,5},{1,4},{2,7},{3,6},{4,1},{5,0},{6,3},{7,2},{8,13},{9,12},{10,... | collective-permute-start | bytes 208904 | tf_op jit(solution)/shard_map/ppermute | solution.py:42
  23.3 8.0 %collective-permute-start.4 = (bf16[16,2176]{1,0:T(8,128)(2,1)S(1)}, bf16[16,2176]{1,0:T(8,128)(2,1)S(1)}, u32[]{:S(2)}, u32[]{:S(2)}) collective-permute-start(bf16[16,2176]{1,0:T(8,128)(2,1)S(1)} %get-tuple-element.21.refs_0_), channel_id=1, source_target_pairs={{0,5},{1,4},{2,7},{3,6},{4,1},{5,0},{6,3},{7,2},{8,13},{9,12},{10,... | collective-permute-start | bytes 208904 | tf_op jit(solution)/shard_map/ppermute | solution.py:42
  25.0 6.3 %collective-permute-start.5 = (bf16[16,2176]{1,0:T(8,128)(2,1)S(1)}, bf16[16,2176]{1,0:T(8,128)(2,1)S(1)}, u32[]{:S(2)}, u32[]{:S(2)}) collective-permute-start(bf16[16,2176]{1,0:T(8,128)(2,1)S(1)} %collective-permute-done.3.refs_1_), channel_id=1, source_target_pairs={{0,5},{1,4},{2,7},{3,6},{4,1},{5,0},{6,3},{7,2},{8,13},{9,12},{10,... | collective-permute-start | bytes 208904 | tf_op jit(solution)/shard_map/ppermute | solution.py:42
  29.2 4.8 %collective-permute-start.15 = (bf16[32,2048]{1,0:T(8,128)(2,1)S(1)}, bf16[32,2048]{1,0:T(8,128)(2,1)S(1)}, u32[]{:S(2)}, u32[]{:S(2)}) collective-permute-start(bf16[32,2048]{1,0:T(8,128)(2,1)S(1)} %get-tuple-element.29), channel_id=1, source_target_pairs={{0,5},{1,2},{2,1},{3,6},{4,7},{5,0},{6,3},{7,4},{8,13},{9,10},{10,... | collective-permute-start | bytes 393224 | tf_op jit(solution)/shard_map/ppermute | solution.py:60
  33.1 4.5 %collective-permute-start.8 = (bf16[32,2048]{1,0:T(8,128)(2,1)S(1)}, bf16[32,2048]{1,0:T(8,128)(2,1)S(1)}, u32[]{:S(2)}, u32[]{:S(2)}) collective-permute-start(bf16[32,2048]{1,0:T(8,128)(2,1)S(1)} %get-tuple-element.23), channel_id=1, source_target_pairs={{0,3},{1,4},{2,7},{3,0},{4,1},{5,6},{6,5},{7,2},{8,11},{9,12},{10,... | collective-permute-start | bytes 393224 | tf_op jit(solution)/shard_map/ppermute | solution.py:60
  34.0 4.3 %collective-permute-start.16 = (bf16[16,2048]{1,0:T(8,128)(2,1)S(1)}, bf16[16,2048]{1,0:T(8,128)(2,1)S(1)}, u32[]{:S(2)}, u32[]{:S(2)}) collective-permute-start(bf16[16,2048]{1,0:T(8,128)(2,1)S(1)} %get-tuple-element.31), channel_id=1, source_target_pairs={{0,3},{1,4},{2,7},{3,0},{4,1},{5,6},{6,5},{7,2},{8,11},{9,12},{10,... | collective-permute-start | bytes 196616 | tf_op jit(solution)/shard_map/ppermute | solution.py:60
  37.6 5.2 %collective-permute-start.9 = (bf16[16,2048]{1,0:T(8,128)(2,1)S(1)}, bf16[16,2048]{1,0:T(8,128)(2,1)S(1)}, u32[]{:S(2)}, u32[]{:S(2)}) collective-permute-start(bf16[16,2048]{1,0:T(8,128)(2,1)S(1)} %get-tuple-element.25), channel_id=1, source_target_pairs={{0,5},{1,2},{2,1},{3,6},{4,7},{5,0},{6,3},{7,4},{8,13},{9,10},{10,... | collective-permute-start | bytes 196616 | tf_op jit(solution)/shard_map/ppermute | solution.py:60
  38.3 7.9 %collective-permute-start.18 = (bf16[8,2048]{1,0:T(8,128)(2,1)S(1)}, bf16[8,2048]{1,0:T(8,128)(2,1)S(1)}, u32[]{:S(2)}, u32[]{:S(2)}) collective-permute-start(bf16[8,2048]{1,0:T(8,128)(2,1)S(1)} %get-tuple-element.33), channel_id=1, source_target_pairs={{0,9},{1,8},{2,11},{3,10},{4,13},{5,12},{6,15},{7,14},{8,1},{9,0},... | collective-permute-start | bytes 98312 | tf_op jit(solution)/shard_map/ppermute | solution.py:42
  39.3 7.0 %collective-permute-start.17 = (bf16[8,2048]{1,0:T(8,128)(2,1)S(1)}, bf16[8,2048]{1,0:T(8,128)(2,1)S(1)}, u32[]{:S(2)}, u32[]{:S(2)}) collective-permute-start(bf16[8,2048]{1,0:T(8,128)(2,1)S(1)} %get-tuple-element.32), channel_id=1, source_target_pairs={{0,17},{1,16},{2,19},{3,18},{4,21},{5,20},{6,23},{7,22},{8,25},{9,... | collective-permute-start | bytes 98312 | tf_op jit(solution)/shard_map/ppermute | solution.py:42
  42.8 5.2 %collective-permute-start.10 = (bf16[8,2048]{1,0:T(8,128)(2,1)S(1)}, bf16[8,2048]{1,0:T(8,128)(2,1)S(1)}, u32[]{:S(2)}, u32[]{:S(2)}) collective-permute-start(bf16[8,2048]{1,0:T(8,128)(2,1)S(1)} %get-tuple-element.27), channel_id=1, source_target_pairs={{0,25},{1,24},{2,27},{3,26},{4,29},{5,28},{6,31},{7,30},{8,17},{9,... | collective-permute-start | bytes 98312 | tf_op jit(solution)/shard_map/ppermute | solution.py:42
